TPU v7x, 32 devices: a whole 2x2x4 slice. The times are simulated.
32 devices in a mesh: req: 8 (over z, x), mp: 4 (over y, core).
Axes of the slice: x: 2, y: 2, z: 4, core: 2. Of those that a mesh axis runs over, the one named last changes fastest.
Arguments:
- hidden: bfloat16 [2048, 4096], P(('req', 'mp')), may hold values from -4 to 4
- queries: bfloat16 [2048, 2048], P('req', 'mp'), may hold values from -130 to 130
- rotated_rollout_keys: bfloat16 [2048, 2, 128], P('req'), may hold values from -4 to 4
- rollout_value_matrix: bfloat16 [2048, 2, 128], P('req'), may hold values from -4 to 4
- cached_key_slabs: bfloat16 [16384, 2, 128], P('req'), may hold values from -4 to 4
- cached_value_slabs: bfloat16 [16384, 2, 128], P('req'), may hold values from -4 to 4
- out_weight: bfloat16 [2048, 4096], P('mp'), may hold values from -0.5 to 0.5
- final_gain: float32 [4096], replicated, may hold values from 0.1 to 1.9
- head_weight: bfloat16 [4096, 32000], P(None, 'req'), may hold values from -1 to 1
- token_ids: int32 [2048], P(('req', 'mp')), may hold values from 0 to 31999
- rollout_len: int32 [8], P('req'), may hold values from 64 to 256
- piece_offset: int32 [8], P('req'), may hold values from 0 to 3
- piece_len: int32 [8], P('req'), may hold values from 256 to 2048
Outputs:
- logprob: float32 [2048], P(('req', 'mp'))
- entropy: float32 [2048], P(('req', 'mp'))
All inputs are finite; a program needn't handle non-finite values.
Results may differ from a plain program's by a relative error of at most 0.0045.
Values may be sent and summed in bfloat16 or wider, within the bound.
No kernel may reach another device: no remote copies, remote signals or barrier semaphores. Data moves between devices by JAX's collectives and lax.ppermute only.
A program may use at most 128 MiB of HBM per device.

v0:
```python
import math

import jax
import jax.numpy as jnp
from jax import lax
from jax.sharding import PartitionSpec as P

REACH = 4


NEGATIVE = -1e30


def shifted(block, axis, distance):
    devices = range(lax.axis_size(axis))
    route = [((i - distance) % len(devices), i) for i in devices]
    return lax.ppermute(block, axis, route)


def combined_all(shard, axis, combine):
    everything = jax.tree.map(lambda part: lax.all_gather(part, axis), shard)
    leading = jax.tree.map(lambda part: part[0], everything)

    def hop(k, so_far):
        return combine(so_far, jax.tree.map(lambda part: part[k], everything))

    return lax.fori_loop(1, lax.axis_size(axis), hop, leading)


def partial_softmax(query, keys, values, mask, factor):
    scores = jnp.einsum("thd,cd->thc", query, keys, preferred_element_type=jnp.float32) * factor
    scores = jnp.where(mask[:, None, :], scores, NEGATIVE)
    top = jnp.max(scores, axis=-1)
    weights = jnp.exp(scores - top[..., None])
    total = jnp.sum(weights, axis=-1)
    summed = jnp.einsum(
        "thc,cd->thd", weights.astype(jnp.bfloat16), values, preferred_element_type=jnp.float32
    )
    return (top, total, summed)


def join_parts(parts):
    tops = jnp.concatenate([item[0] for item in parts], axis=0)
    totals = jnp.concatenate([item[1] for item in parts], axis=0)
    sums = jnp.concatenate([item[2] for item in parts], axis=0)
    highest = jnp.max(tops, axis=0)
    scales = jnp.exp(tops - highest[None])
    total = jnp.sum(totals * scales, axis=0)
    summed = jnp.einsum("nth,nthd->thd", scales, sums)
    return summed / total[..., None]


def merge_summary(leading_slab, second):
    highest = jnp.maximum(leading_slab[0], second[0])
    left = jnp.exp(leading_slab[0] - highest)
    right = jnp.exp(second[0] - highest)
    return (
        highest,
        leading_slab[1] * left + second[1] * right,
        leading_slab[2] * left + second[2] * right,
        leading_slab[3] + second[3],
    )


def body(
    hidden,
    queries,
    rotated_rollout_keys,
    rollout_value_matrix,
    cached_key_slabs,
    cached_value_slabs,
    out_weight,
    final_gain,
    head_weight,
    token_ids,
    rollout_len,
    piece_offset,
    piece_len,
):
    groups = lax.axis_size("req")
    request = lax.axis_index("req")
    shard = lax.axis_index("mp")
    rollout = queries.shape[0]
    head_size = rotated_rollout_keys.shape[2]
    heads_here = queries.shape[1] // head_size
    group_size = heads_here * lax.axis_size("mp") // rotated_rollout_keys.shape[1]
    value_head = shard * heads_here // group_size
    factor = 1.0 / math.sqrt(head_size)
    offset = piece_offset[0]
    current_slab_keys = lax.dynamic_index_in_dim(cached_key_slabs, value_head, 1, keepdims=False)
    current_slab_values = lax.dynamic_index_in_dim(
        cached_value_slabs, value_head, 1, keepdims=False
    )
    slab_valid = jnp.arange(cached_key_slabs.shape[0]) < piece_len[0]
    rollout_key_rows = lax.dynamic_index_in_dim(rotated_rollout_keys, value_head, 1, keepdims=False)
    rollout_value_rows = lax.dynamic_index_in_dim(
        rollout_value_matrix, value_head, 1, keepdims=False
    )
    rows = jnp.arange(rollout)
    causal = rows[None, :] <= rows[:, None]
    own_query = queries.reshape(rollout, heads_here, head_size)
    local = partial_softmax(own_query, rollout_key_rows, rollout_value_rows, causal, factor)
    parts = [tuple((item[None] for item in local))]
    slab_mask = jnp.broadcast_to(slab_valid, (rollout, cached_key_slabs.shape[0]))
    visitor = queries
    for step in range(1, REACH):
        moved = shifted(queries, "req", step)
        visitor = jnp.where(offset == step, moved, visitor)
    top, total, summed = partial_softmax(
        visitor.reshape(rollout, heads_here, head_size),
        current_slab_keys,
        current_slab_values,
        slab_mask,
        factor,
    )
    keep = offset == 0
    parts.append(
        (
            jnp.where(keep, top, NEGATIVE)[None],
            jnp.where(keep, total, 0.0)[None],
            jnp.where(keep, summed, 0.0)[None],
        )
    )
    for step in range(1, REACH):
        mine = offset == step
        back_sum, back_top, back_total = shifted(
            (
                jnp.where(mine, summed, 0.0),
                jnp.where(mine, top, NEGATIVE),
                jnp.where(mine, total, 0.0),
            ),
            "req",
            -step,
        )
        parts.append((back_top[None], back_total[None], back_sum[None]))
    mixed = join_parts(parts).astype(jnp.bfloat16).reshape(rollout, heads_here * head_size)
    rows_here = hidden.shape[0]
    block = mixed
    added = lax.psum_scatter(
        jnp.dot(block, out_weight, preferred_element_type=jnp.float32),
        "mp",
        scatter_dimension=0,
        tiled=True,
    )
    stream = hidden.astype(jnp.float32) + added
    normed = (
        stream * lax.rsqrt(jnp.mean(stream * stream, axis=-1, keepdims=True) + 1e-06) * final_gain
    ).astype(jnp.bfloat16)
    vocabulary_here = head_weight.shape[1]
    first_word = request * vocabulary_here
    columns = jnp.arange(vocabulary_here)
    block = lax.all_gather(normed, "req", axis=0, tiled=True)
    words = lax.all_gather(token_ids, "req", axis=0, tiled=True)
    logits = jnp.dot(block, head_weight, preferred_element_type=jnp.float32)
    highest = jnp.max(logits, axis=-1)
    spread = jnp.exp(logits - highest[:, None])
    total = jnp.sum(spread, axis=-1)
    weighted = jnp.sum(spread * logits, axis=-1)
    picked = jnp.sum(
        jnp.where(columns[None, :] == (words - first_word)[:, None], logits, 0.0), axis=-1
    )
    fresh = (highest, total, weighted, picked)
    summary = tuple((fresh[index] for index in range(4)))
    table = tuple((item.reshape(groups, rows_here) for item in summary))
    pooled = combined_all(table, "req", merge_summary)
    highest, total, weighted, picked = (
        lax.dynamic_index_in_dim(item, request, 0, keepdims=False) for item in pooled
    )
    log_total = highest + jnp.log(total)
    positions = shard * rows_here + jnp.arange(rows_here)
    valid = positions < rollout_len[0]
    logprob = jnp.where(valid, picked - log_total, 0.0)
    entropy = jnp.where(valid, log_total - weighted / total, 0.0)
    return (logprob, entropy)


def solution(mesh):
    placed = (
        P(("req", "mp"), None),
        P("req", "mp"),
        P("req", None, None),
        P("req", None, None),
        P("req", None, None),
        P("req", None, None),
        P("mp", None),
        P(),
        P(None, "req"),
        P(("req", "mp")),
        P("req"),
        P("req"),
        P("req"),
    )
    return jax.shard_map(
        body,
        mesh=mesh,
        in_specs=placed,
        out_specs=(P(("req", "mp")), P(("req", "mp"))),
        check_vma=False,
    )
```

profile of v0, /device:TPU:0, one launch (start us, length us, event | category | flops | bytes accessed | tf_op | source)
XLA Modules:
  0.0 363.0 jit_solution(10148285551743144967)
XLA Ops:
  7.2 4.0 %collective-permute-start = (bf16[256,512]{1,0:T(8,128)(2,1)}, bf16[256,512]{1,0:T(8,128)(2,1)S(1)}, u32[]{:S(2)}, u32[]{:S(2)}) collective-permute-start(bf16[256,512]{1,0:T(8,128)(2,1)} %param.16), channel_id=1, source_target_pairs={{20,0},{24,4},{28,8},{0,12},{4,16},{8,20},{12,24},{16,28},{21,1},{... | collective-permute-start | bytes 786440 | tf_op jit(solution)/shard_map/ppermute | solution.py:17
  11.2 1.6 collective-permute-start.1
  12.8 1.5 collective-permute-start.2
  15.7 1.1 constant_dynamic-slice_fusion.6
  17.9 1.3 fusion.34
  20.5 2.2 constant_dynamic-slice_fusion.4
  23.0 12.6 %collective-permute-done = bf16[256,512]{1,0:T(8,128)(2,1)S(1)} collective-permute-done((bf16[256,512]{1,0:T(8,128)(2,1)}, bf16[256,512]{1,0:T(8,128)(2,1)S(1)}, u32[]{:S(2)}, u32[]{:S(2)}) %collective-permute-start) | collective-permute-done | bytes 262176 | tf_op jit(solution)/shard_map/ppermute | solution.py:17
  35.6 1.6 fusion.4
  37.2 1.9 fusion.5
  39.2 1.1 collective-permute-start.10
  40.3 3.0 collective-permute-start.11
  43.3 1.5 collective-permute-start.3
  45.1 2.0 bitcast_dynamic-update-slice_fusion.3
  47.3 3.2 collective-permute-start.5
  50.5 1.9 collective-permute-start.6
  52.4 2.7 collective-permute-start.7
  56.7 2.4 collective-permute-done.6
  59.2 5.6 %collective-permute-done.7 = bf16[256,4,128]{2,0,1:T(8,128)(2,1)S(1)} collective-permute-done((bf16[256,4,128]{2,0,1:T(8,128)(2,1)S(1)}, bf16[256,4,128]{2,0,1:T(8,128)(2,1)S(1)}, u32[]{:S(2)}, u32[]{:S(2)}) %collective-permute-start.7) | collective-permute-done | bytes 262176 | tf_op jit(solution)/shard_map/ppermute | solution.py:17
  64.8 3.2 collective-permute-done.8
  68.1 1.3 fusion.7
  69.8 5.4 %fusion.20 = f32[256,4096]{1,0:T(8,128)} fusion(bf16[512,4096]{1,0:T(8,128)(2,1)} %param.21, bf16[32,8,4,128]{3,2,1,0:T(4,128)(2,1)S(1)} %bitcast.137), kind=kOutput, calls=%fused_computation.43 | convolution fusion | flops 1073741824 | bytes 8650752 | tf_op jit(solution)/shard_map/dot_general | solution.py:140
  75.5 51.9 %reduce-scatter.2.cloned.1.call-done = f32[64,4096]{1,0:T(8,128)} async-done(((f32[256,4096]{1,0:T(8,128)}), f32[64,4096]{1,0:T(8,128)}) %reduce-scatter.2.cloned.1.call-update) | async-done | bytes 1048592 | tf_op jit(solution)/shard_map/reduce_scatter | solution.py:139
  127.4 1.5 multiply_reduce_fusion.1
  128.9 2.2 multiply_convert_fusion
  133.3 11.8 %all-reduce = s32[512]{0:T(512)S(1)} all-reduce(s32[512]{0:T(512)S(1)} %dynamic-update-slice), channel_id=1, replica_groups=mesh['req'=8,'mp'=4] {'req'}, use_global_device_ids=true, to_apply=%add | all-reduce | flops 512 | bytes 4096
  145.1 59.6 %all-gather.2.cloned.1.call-done = bf16[512,4096]{1,0:T(8,128)(2,1)} async-done(((bf16[64,4096]{1,0:T(8,128)(2,1)}), bf16[512,4096]{1,0:T(8,128)(2,1)}) %all-gather.2.cloned.1.call-update) | async-done | bytes 4194320 | tf_op jit(solution)/shard_map/all_gather | solution.py:152
  204.7 23.6 %fusion.35 = (f32[512]{0:T(512)S(1)}, f32[512,4000]{0,1:T(8,128)}) fusion(bf16[512,4096]{1,0:T(8,128)(2,1)} %all-gather.2.cloned.1.call-done, bf16[4096,4000]{0,1:T(8,128)(2,1)} %param.23), kind=kOutput, calls=%fused_computation.102 | convolution fusion | flops 16779264000 | bytes 45156352 | tf_op jit(solution)/shard_map/dot_general | solution.py:154
  228.4 4.8 %multiply_reduce_fusion = (f32[512]{0:T(512)S(1)}, f32[512]{0:T(512)S(1)}, f32[512]{0:T(512)S(1)}) fusion(f32[512,4000]{0,1:T(8,128)} %get-tuple-element.271, f32[512]{0:T(512)S(1)} %get-tuple-element.270, s32[512]{0:T(512)S(1)} %broadcast_subtract_fusion), kind=kLoop, calls=%fused_computation.13 | loop fusion | flops 14334464 | bytes 8202240 | tf_op jit(solution)/shard_map/reduce_sum | solution.py:158
  233.3 30.4 %all_gather.23 = f32[8,8,64]{2,1,0:T(8,128)S(1)} all-gather(f32[1,8,64]{2,1,0:T(8,128)S(1)} %all_gather_reshape.15), channel_id=1, replica_groups=mesh['req'=8,'mp'=4] {'req'}, dimensions={0}, use_global_device_ids=true | all-gather | bytes 18432 | tf_op jit(solution)/shard_map/all_gather | solution.py:21
  263.8 30.4 %all_gather.21 = f32[8,8,64]{2,1,0:T(8,128)S(1)} all-gather(f32[1,8,64]{2,1,0:T(8,128)S(1)} %all_gather_reshape.14), channel_id=1, replica_groups=mesh['req'=8,'mp'=4] {'req'}, dimensions={0}, use_global_device_ids=true | all-gather | bytes 18432 | tf_op jit(solution)/shard_map/all_gather | solution.py:21
  294.3 30.4 %all_gather.20 = f32[8,8,64]{2,1,0:T(8,128)S(1)} all-gather(f32[1,8,64]{2,1,0:T(8,128)S(1)} %all_gather_reshape.13), channel_id=1, replica_groups=mesh['req'=8,'mp'=4] {'req'}, dimensions={0}, use_global_device_ids=true | all-gather | bytes 18432 | tf_op jit(solution)/shard_map/all_gather | solution.py:21
  324.7 30.4 %all_gather.19 = f32[8,8,64]{2,1,0:T(8,128)S(1)} all-gather(f32[1,8,64]{2,1,0:T(8,128)S(1)} %all_gather_reshape.12), channel_id=1, replica_groups=mesh['req'=8,'mp'=4] {'req'}, dimensions={0}, use_global_device_ids=true | all-gather | bytes 18432 | tf_op jit(solution)/shard_map/all_gather | solution.py:21
  (93 shorter events, 8.2 us)
Async XLA Ops:
  7.2 8.6 %copy-start = (bf16[2048,2,128]{2,1,0:T(2,128)(2,1)S(1)}, bf16[2048,2,128]{2,1,0:T(2,128)(2,1)}, u32[]{:S(2)}) copy-start(bf16[2048,2,128]{2,1,0:T(2,128)(2,1)} %param.19) | copy-start | bytes 3145732
  7.2 28.5 %copy-start.3 = (bf16[256,512]{1,0:T(8,128)(2,1)S(1)}, bf16[256,512]{1,0:T(8,128)(2,1)}, u32[]{:S(2)}) copy-start(bf16[256,512]{1,0:T(8,128)(2,1)} %param.16) | copy-start | bytes 786436
  7.2 120.2 %reduce-scatter.2.cloned.1.call-start = ((), (), s32[]{:S(2)}) async-start(), calls=%async_computation.1 | async-start | bytes 5242880 | tf_op jit(solution)/shard_map/reduce_scatter | solution.py:139
  7.2 28.4 %collective-permute-start = (bf16[256,512]{1,0:T(8,128)(2,1)}, bf16[256,512]{1,0:T(8,128)(2,1)S(1)}, u32[]{:S(2)}, u32[]{:S(2)}) collective-permute-start(bf16[256,512]{1,0:T(8,128)(2,1)} %param.16), channel_id=1, source_target_pairs={{20,0},{24,4},{28,8},{0,12},{4,16},{8,20},{12,24},{16,28},{21,1},{... | collective-permute-start | bytes 786440 | tf_op jit(solution)/shard_map/ppermute | solution.py:17
  11.2 24.4 %collective-permute-start.1 = (bf16[256,512]{1,0:T(8,128)(2,1)}, bf16[256,512]{1,0:T(8,128)(2,1)S(1)}, u32[]{:S(2)}, u32[]{:S(2)}) collective-permute-start(bf16[256,512]{1,0:T(8,128)(2,1)} %param.16), channel_id=1, source_target_pairs={{24,0},{28,4},{0,8},{4,12},{8,16},{12,20},{16,24},{20,28},{25,1},{... | collective-permute-start | bytes 786440 | tf_op jit(solution)/shard_map/ppermute | solution.py:17
  12.8 22.8 %collective-permute-start.2 = (bf16[256,512]{1,0:T(8,128)(2,1)}, bf16[256,512]{1,0:T(8,128)(2,1)S(1)}, u32[]{:S(2)}, u32[]{:S(2)}) collective-permute-start(bf16[256,512]{1,0:T(8,128)(2,1)} %param.16), channel_id=1, source_target_pairs={{28,0},{0,4},{4,8},{8,12},{12,16},{16,20},{20,24},{24,28},{29,1},{... | collective-permute-start | bytes 786440 | tf_op jit(solution)/shard_map/ppermute | solution.py:17
  39.1 16.0 %collective-permute-start.9 = (f32[256,4]{0,1:T(4,128)S(1)}, f32[256,4]{0,1:T(4,128)S(1)}, u32[]{:S(2)}, u32[]{:S(2)}) collective-permute-start(f32[256,4]{0,1:T(4,128)S(1)} %get-tuple-element.260), channel_id=1, source_target_pairs={{4,0},{8,4},{12,8},{16,12},{20,16},{24,20},{28,24},{0,28},{5,1},{9... | collective-permute-start | bytes 12296 | tf_op jit(solution)/shard_map/ppermute | solution.py:17
  39.2 16.9 %collective-permute-start.10 = (f32[256,4]{0,1:T(4,128)S(1)}, f32[256,4]{0,1:T(4,128)S(1)}, u32[]{:S(2)}, u32[]{:S(2)}) collective-permute-start(f32[256,4]{0,1:T(4,128)S(1)} %get-tuple-element.259), channel_id=1, source_target_pairs={{8,0},{12,4},{16,8},{20,12},{24,16},{28,20},{0,24},{4,28},{9,1},{1... | collective-permute-start | bytes 12296 | tf_op jit(solution)/shard_map/ppermute | solution.py:17
  40.3 15.8 %collective-permute-start.11 = (f32[256,4]{0,1:T(4,128)S(1)}, f32[256,4]{0,1:T(4,128)S(1)}, u32[]{:S(2)}, u32[]{:S(2)}) collective-permute-start(f32[256,4]{0,1:T(4,128)S(1)} %get-tuple-element.258), channel_id=1, source_target_pairs={{12,0},{16,4},{20,8},{24,12},{28,16},{0,20},{4,24},{8,28},{13,1},{... | collective-permute-start | bytes 12296 | tf_op jit(solution)/shard_map/ppermute | solution.py:17
  43.3 4.0 %collective-permute-start.3 = (f32[256,4]{0,1:T(4,128)S(1)}, f32[256,4]{0,1:T(4,128)S(1)}, u32[]{:S(2)}, u32[]{:S(2)}) collective-permute-start(f32[256,4]{0,1:T(4,128)S(1)} %get-tuple-element.263), channel_id=1, source_target_pairs={{4,0},{8,4},{12,8},{16,12},{20,16},{24,20},{28,24},{0,28},{5,1},{9... | collective-permute-start | bytes 12296 | tf_op jit(solution)/shard_map/ppermute | solution.py:17
  44.8 5.7 %collective-permute-start.4 = (f32[256,4]{0,1:T(4,128)S(1)}, f32[256,4]{0,1:T(4,128)S(1)}, u32[]{:S(2)}, u32[]{:S(2)}) collective-permute-start(f32[256,4]{0,1:T(4,128)S(1)} %get-tuple-element.262), channel_id=1, source_target_pairs={{8,0},{12,4},{16,8},{20,12},{24,16},{28,20},{0,24},{4,28},{9,1},{1... | collective-permute-start | bytes 12296 | tf_op jit(solution)/shard_map/ppermute | solution.py:17
  47.3 5.1 %collective-permute-start.5 = (f32[256,4]{0,1:T(4,128)S(1)}, f32[256,4]{0,1:T(4,128)S(1)}, u32[]{:S(2)}, u32[]{:S(2)}) collective-permute-start(f32[256,4]{0,1:T(4,128)S(1)} %get-tuple-element.261), channel_id=1, source_target_pairs={{12,0},{16,4},{20,8},{24,12},{28,16},{0,20},{4,24},{8,28},{13,1},{... | collective-permute-start | bytes 12296 | tf_op jit(solution)/shard_map/ppermute | solution.py:17
  50.5 8.7 %collective-permute-start.6 = (bf16[256,4,128]{2,0,1:T(8,128)(2,1)S(1)}, bf16[256,4,128]{2,0,1:T(8,128)(2,1)S(1)}, u32[]{:S(2)}, u32[]{:S(2)}) collective-permute-start(bf16[256,4,128]{2,0,1:T(8,128)(2,1)S(1)} %get-tuple-element.255), channel_id=1, source_target_pairs={{4,0},{8,4},{12,8},{16,12},{20,16},{24,20},{28,24},{0,28},{5,1},{9... | collective-permute-start | bytes 786440 | tf_op jit(solution)/shard_map/ppermute | solution.py:17
  52.4 12.4 %collective-permute-start.7 = (bf16[256,4,128]{2,0,1:T(8,128)(2,1)S(1)}, bf16[256,4,128]{2,0,1:T(8,128)(2,1)S(1)}, u32[]{:S(2)}, u32[]{:S(2)}) collective-permute-start(bf16[256,4,128]{2,0,1:T(8,128)(2,1)S(1)} %get-tuple-element.254), channel_id=1, source_target_pairs={{8,0},{12,4},{16,8},{20,12},{24,16},{28,20},{0,24},{4,28},{9,1},{1... | collective-permute-start | bytes 786440 | tf_op jit(solution)/shard_map/ppermute | solution.py:17
  55.1 12.9 %collective-permute-start.8 = (bf16[256,4,128]{2,0,1:T(8,128)(2,1)S(1)}, bf16[256,4,128]{2,0,1:T(8,128)(2,1)S(1)}, u32[]{:S(2)}, u32[]{:S(2)}) collective-permute-start(bf16[256,4,128]{2,0,1:T(8,128)(2,1)S(1)} %get-tuple-element.253), channel_id=1, source_target_pairs={{12,0},{16,4},{20,8},{24,12},{28,16},{0,20},{4,24},{8,28},{13,1},{... | collective-permute-start | bytes 786440 | tf_op jit(solution)/shard_map/ppermute | solution.py:17
  69.4 58.0 %copy-start.2 = (bf16[64,4096]{1,0:T(8,128)(2,1)S(1)}, bf16[64,4096]{1,0:T(8,128)(2,1)}, u32[]{:S(2)}) copy-start(bf16[64,4096]{1,0:T(8,128)(2,1)} %param.15) | copy-start | bytes 1572868
  69.8 59.1 %copy-start.4 = (f32[4096]{0:T(1024)S(1)}, f32[4096]{0:T(1024)}, u32[]{:S(2)}) copy-start(f32[4096]{0:T(1024)} %param.22) | copy-start | bytes 49156
  69.8 62.0 %copy-start.6 = (u32[32]{0:T(128)S(1)}, u32[32]{0:T(128)}, u32[]{:S(2)}) copy-start(u32[32]{0:T(128)} %constant.121) | copy-start | bytes 388
  69.8 63.2 %copy-start.5 = (s32[64]{0:T(128)S(1)}, s32[64]{0:T(128)}, u32[]{:S(2)}) copy-start(s32[64]{0:T(128)} %param.24) | copy-start | bytes 772
  75.2 129.4 %all-gather.2.cloned.1.call-start = ((), (), s32[]{:S(2)}) async-start(), calls=%async_computation.2 | async-start | bytes 4718592 | tf_op jit(solution)/shard_map/all_gather | solution.py:152
  204.7 151.5 %copy-start.1 = (bf16[2048,2,128]{2,1,0:T(2,128)(2,1)S(1)}, bf16[2048,2,128]{2,1,0:T(2,128)(2,1)}, u32[]{:S(2)}) copy-start(bf16[2048,2,128]{2,1,0:T(2,128)(2,1)} %param.19) | copy-start | bytes 3145732
Sparse Core Ops, SparseCore 0:
  75.4 51.9 reduce-scatter.1
  131.2 73.3 all-gather.1
where the time goes:
time: 363 us
  waiting for transfers between devices  135 us (37%)
  blocking collectives  133 us (37%)
  matrix products  35.6 us (10%)
  starting transfers between devices  22.1 us (6%)
  between operations  17 us (5%)
  other arithmetic  12 us (3%)
  local copies, waits for them, and re-layouts  7.34 us (2%)
    all_gather x4, blocking collectives, combined_all(): everything = jax.tree.map(lambda part: lax.all_gather(part, axis), shard)  122 us
    all_gather x1, waiting for transfers between devices, body(): block = lax.all_gather(normed, 'req', axis=0, tiled=True)  59.6 us
    reduce_scatter x1, waiting for transfers between devices, body(): lax.psum_scatter(jnp.dot(block, out_weight, preferred_element_type=jnp.fl...  51.9 us
    ppermute x12, waiting for transfers between devices, shifted(): return lax.ppermute(block, axis, route)  23.8 us
    dot_general x1, matrix products, body(): logits = jnp.dot(block, head_weight, preferred_element_type=jnp.float32)  23.6 us
    ppermute x12, starting transfers between devices, shifted(): return lax.ppermute(block, axis, route)  21.8 us
    unnamed x1, blocking collectives  11.8 us
  transfers between devices with their start and end apart: 14, of which 6 were waited for; matrix products, arithmetic and copies ran while one was open for 3% of the time, Pallas kernels for 0%

commit v1 on v0

v1 whole, which is shorter than its diff:
```python
import functools
import math

import jax
import jax.numpy as jnp
from jax import lax
from jax.experimental import pallas as pl
from jax.experimental.pallas import tpu as pltpu
from jax.sharding import PartitionSpec as P

NEGATIVE = -1e30
BLOCK = 256
META = 16
STATE = 8
MIB = 1 << 20


def ring_order(groups):
    wide = 1 << (int(math.log2(groups)) // 2)
    tall = groups // wide
    order = [z * wide for z in range(tall)]
    for step, z in enumerate(reversed(range(tall))):
        across = range(1, wide) if step % 2 == 0 else reversed(range(1, wide))
        order += [z * wide + x for x in across]
    return order


def nt(a, b):
    return lax.dot_general(a, b, (((1,), (1,)), ((), ())), preferred_element_type=jnp.float32)


def tn(a, b):
    return lax.dot_general(a, b, (((0,), (0,)), ((), ())), preferred_element_type=jnp.float32)


def put_state(state, head, size, top, total):
    rows = lax.broadcasted_iota(jnp.int32, (STATE, top.shape[1]), 0)
    state[head, size : size + STATE, :] = jnp.where(rows == 0, top, total)


def attend_slab(core, want, kv, query, state, size, scale):
    half = (kv.shape[0] - META) // 2
    heads = query.shape[1] // size
    meta = kv[2 * half : 2 * half + META, :].astype(jnp.float32)
    offset = jnp.max(meta[0:1, :]).astype(jnp.int32)
    length = jnp.max(meta[1:2, :] * 256.0 + meta[2:3, :]).astype(jnp.int32)
    blocks = jnp.clip((length - core * BLOCK + 2 * BLOCK - 1) // (2 * BLOCK), 0, half // BLOCK)
    blocks = jnp.where(offset == want, blocks, 0)

    def step(j, carry):
        start = pl.multiple_of(j * BLOCK, BLOCK)
        keys = kv[pl.ds(start, BLOCK), :]
        values = kv[pl.ds(half + start, BLOCK), :]
        place = lax.broadcasted_iota(jnp.int32, (BLOCK, 1), 0) + (2 * j + core) * BLOCK
        valid = place < length
        for h in range(heads):
            scores = nt(keys, query[:, h * size : (h + 1) * size]) * scale
            scores = jnp.where(valid, scores, NEGATIVE)
            before = state[h, size : size + 1, :]
            top = jnp.maximum(before, jnp.max(scores, axis=0, keepdims=True))
            old = jnp.exp2(before - top)
            weights = jnp.exp2(scores - top)
            total = state[h, size + 1 : size + 2, :] * old + jnp.sum(weights, axis=0, keepdims=True)
            state[h, :size, :] = state[h, :size, :] * old + tn(values, weights.astype(jnp.bfloat16))
            put_state(state, h, size, top, total)
        return carry

    lax.fori_loop(0, blocks, step, 0)


def first_kernel(sc, times, query, keys, values, kv, state, *, size, scale):
    core = sc[0]
    here = keys.shape[0]
    place = lax.broadcasted_iota(jnp.int32, (here, 1), 0) + core * here
    valid = place <= times[...]
    for h in range(query.shape[1] // size):
        scores = nt(keys[...], query[:, h * size : (h + 1) * size]) * scale
        scores = jnp.where(valid, scores, NEGATIVE)
        top = jnp.max(scores, axis=0, keepdims=True)
        weights = jnp.exp2(scores - top)
        state[h, :size, :] = tn(values[...], weights.astype(jnp.bfloat16))
        put_state(state, h, size, top, jnp.sum(weights, axis=0, keepdims=True))
    attend_slab(core, sc[1], kv, query, state, size, scale)


def more_kernel(sc, query, *refs, size, scale, slots, split):
    kvs, given, outs = refs[:slots], refs[slots], refs[slots + 1 :]
    if split:
        state = outs[2]
    else:
        state = outs[0]
    state[...] = given[...]
    for i, kv in enumerate(kvs):
        attend_slab(sc[0], sc[1 + i], kv, query, state, size, scale)
    if split:
        middle = state.shape[2] // 2
        outs[0][...] = state[:, :, :middle]
        outs[1][...] = state[:, :, middle:]


def merge_kernel(kept, came, mine, mate, own, send, mixed, *, size, rows):
    heads = kept.shape[0]

    @pl.when(pl.program_id(0) == 0)
    def _():
        for h in range(heads):
            other = (h + heads // 2) % heads
            first, second = kept[h, size : size + 1, :], came[other, size : size + 1, :]
            top = jnp.maximum(first, second)
            left, right = jnp.exp2(first - top), jnp.exp2(second - top)
            total = kept[h, size + 1 : size + 2, :] * left + came[other, size + 1 : size + 2, :] * right
            value = (kept[h, :size, :] * left + came[other, :size, :] * right) / total
            mixed[:, h * size : (h + 1) * size] = value.T.astype(jnp.bfloat16)

    width = mine.shape[0]
    out = jnp.dot(mixed[:, :width], mine[...], preferred_element_type=jnp.float32)
    out += jnp.dot(mixed[:, width:], mate[...], preferred_element_type=jnp.float32)
    own[...] = out[:rows, :]
    send[...] = out[rows:, :].astype(jnp.bfloat16)


def norm_kernel(own, hidden, gain, words, *refs):
    came, out = refs[:-1], refs[-1]
    stream = own[...] + hidden[...].astype(jnp.float32)
    for part in came:
        stream += part[...].astype(jnp.float32)
    width = stream.shape[1]
    square = jnp.sum(stream * stream, axis=1, keepdims=True) * (1.0 / width)
    out[:, :width] = (stream * lax.rsqrt(square + 1e-06) * gain[...]).astype(jnp.bfloat16)
    lane = lax.broadcasted_iota(jnp.int32, (stream.shape[0], out.shape[1] - width), 1)
    code = jnp.where(lane == 0, words[...] >> 8, words[...] & 255)
    out[:, width:] = code.astype(jnp.float32).astype(jnp.bfloat16)


def logits_kernel(sc, *refs, block):
    parts, weight, out, rows, codes = refs[:-4], refs[-4], refs[-3], refs[-2], refs[-1]
    width = weight.shape[1]
    at = 0
    for part in parts:
        rows[at : at + part.shape[0], :] = part[:, :width]
        codes[at : at + part.shape[0], :] = part[:, width:].astype(jnp.float32)
        at += part.shape[0]
    turned = codes[...].T
    words = (turned[0:1, :] * 256.0 + turned[1:2, :]).astype(jnp.int32) - sc[0]
    count = at
    place = lax.broadcasted_iota(jnp.int32, (block, 1), 0)

    def step(i, carry):
        top, total, weighted, picked = carry
        start = pl.multiple_of(i * block, 8)
        logits = nt(weight[pl.ds(start, block), :], rows[...])
        now = jnp.maximum(top, jnp.max(logits, axis=0, keepdims=True))
        old = jnp.exp(top - now)
        spread = jnp.exp(logits - now)
        total = total * old + jnp.sum(spread, axis=0, keepdims=True)
        weighted = weighted * old + jnp.sum(spread * logits, axis=0, keepdims=True)
        hit = place == words - start
        picked = picked + jnp.sum(jnp.where(hit, logits, 0.0), axis=0, keepdims=True)
        return now, total, weighted, picked

    zero = jnp.zeros((1, count), jnp.float32)
    carry = (jnp.full((1, count), NEGATIVE, jnp.float32), zero, zero, zero)
    top, total, weighted, picked = lax.fori_loop(0, weight.shape[0] // block, step, carry)
    line = lax.broadcasted_iota(jnp.int32, (STATE, count), 0)
    result = jnp.where(line == 0, top, jnp.where(line == 1, total, weighted))
    out[...] = jnp.where(line == 3, picked, result)


def smem():
    return pl.BlockSpec(memory_space=pltpu.SMEM)


def vmem():
    return pl.BlockSpec(memory_space=pltpu.VMEM)


def call(kernel, shapes, specs, limit, flops=0, read=0, **extra):
    return pl.pallas_call(
        kernel,
        out_shape=shapes,
        in_specs=specs,
        compiler_params=pltpu.CompilerParams(vmem_limit_bytes=limit * MIB),
        cost_estimate=pl.CostEstimate(flops=flops, bytes_accessed=read, transcendentals=0),
        **extra,
    )


def shape(dims, kind=jnp.float32):
    return jax.ShapeDtypeStruct(dims, kind)


def body(
    hidden,
    queries,
    rotated_rollout_keys,
    rollout_value_matrix,
    cached_key_slabs,
    cached_value_slabs,
    out_weight,
    final_gain,
    head_weight,
    token_ids,
    rollout_len,
    piece_offset,
    piece_len,
):
    groups, members = lax.axis_size("req"), lax.axis_size("mp")
    request, member = lax.axis_index("req"), lax.axis_index("mp")
    core = member % 2
    rollout, rows_here = queries.shape[0], hidden.shape[0]
    width = hidden.shape[1]
    size = rotated_rollout_keys.shape[2]
    heads_here = queries.shape[1] // size
    group_size = heads_here * members // rotated_rollout_keys.shape[1]
    value_head = member * heads_here // group_size
    scale = math.log2(math.e) / math.sqrt(size)
    heads = 2 * heads_here

    def over(block, axis, route):
        count = lax.axis_size(axis)
        pairs = [(i, route(i)) for i in range(count) if route(i) is not None]
        return lax.ppermute(block, axis, pairs)

    positions = cached_key_slabs.shape[0]
    half = positions // 2

    def half_of(slab):
        cut = slab.reshape(half // BLOCK, 2, BLOCK, slab.shape[1], size)
        cut = lax.dynamic_index_in_dim(cut, core, 1, keepdims=False)
        return lax.dynamic_index_in_dim(cut, value_head, 2, keepdims=False).reshape(half, size)

    line = lax.broadcasted_iota(jnp.int32, (META, size), 0)
    numbers = jnp.where(
        line == 0, piece_offset[0], jnp.where(line == 1, piece_len[0] // 256, piece_len[0] % 256)
    )
    kv = jnp.concatenate(
        [half_of(cached_key_slabs), half_of(cached_value_slabs), numbers.astype(jnp.bfloat16)]
    )
    two = over(kv, "req", lambda i: (i - 2) % groups)
    one = over(kv, "req", lambda i: i - 1 if i % 2 else None)
    mate_queries = over(queries, "mp", lambda i: i ^ 1)
    mate_weight = over(out_weight, "mp", lambda i: i ^ 1)
    swap = over(two, "req", lambda i: i ^ 1)
    three = over(swap, "req", lambda i: (i - 2) % groups if i % 2 else None)

    order = list(range(0, members, 2)) + list(range(1, members, 2))

    def arrange(block):
        return [lax.dynamic_slice_in_dim(block, (member ^ k) * rows_here, rows_here) for k in order]

    query = jnp.concatenate(
        [jnp.concatenate(arrange(part)) for part in (queries, mate_queries)], axis=1
    )
    times = jnp.concatenate(
        [(member ^ k) * rows_here + jnp.arange(rows_here, dtype=jnp.int32) for k in order]
    )[None]

    def own_half(block):
        cut = lax.dynamic_index_in_dim(block, value_head, 1, keepdims=False)
        return lax.dynamic_slice_in_dim(cut, core * (rollout // 2), rollout // 2)

    full = shape((heads, size + STATE, rollout))
    part = shape((heads, size + STATE, rollout // 2))
    numbers = functools.partial(jnp.stack)
    work = 4 * heads * rollout * half * size
    state = call(
        functools.partial(first_kernel, size=size, scale=scale),
        full,
        [smem()] + [vmem()] * 5,
        16,
        work,
        2 * half * size * 4,
    )(
        jnp.stack([core, jnp.zeros_like(core)]),
        times,
        query,
        own_half(rotated_rollout_keys),
        own_half(rollout_value_matrix),
        kv,
    )
    even = request % 2 == 0
    first_tags = jnp.stack([core, jnp.full_like(core, 1), jnp.full_like(core, 2)])
    swap_tags = jnp.stack([core, jnp.where(even, 3, 1)])
    last_tags = jnp.stack([core, jnp.full_like(core, 3)])
    state = call(
        functools.partial(more_kernel, size=size, scale=scale, slots=2, split=False),
        full,
        [smem()] + [vmem()] * 4,
        16,
        2 * work,
        4 * half * size * 4,
    )(first_tags, query, one, two, state)
    state = call(
        functools.partial(more_kernel, size=size, scale=scale, slots=1, split=False),
        full,
        [smem()] + [vmem()] * 3,
        16,
        work,
        2 * half * size * 4,
    )(swap_tags, query, swap, state)
    kept, sent = call(
        functools.partial(more_kernel, size=size, scale=scale, slots=1, split=True),
        (part, part),
        [smem()] + [vmem()] * 3,
        16,
        work,
        2 * half * size * 4,
        scratch_shapes=[pltpu.VMEM(full.shape, jnp.float32)],
    )(last_tags, query, three, state)
    came = over(sent, "mp", lambda i: i ^ 1)

    tile = 1024
    rows_core = rollout // 2
    away = rows_core - rows_here
    own, send = pl.pallas_call(
        functools.partial(merge_kernel, size=size, rows=rows_here),
        out_shape=(shape((rows_here, width)), shape((away, width), jnp.bfloat16)),
        grid=(width // tile,),
        in_specs=[
            pl.BlockSpec(part.shape, lambda i: (0, 0, 0)),
            pl.BlockSpec(part.shape, lambda i: (0, 0, 0)),
            pl.BlockSpec((out_weight.shape[0], tile), lambda i: (0, i)),
            pl.BlockSpec((out_weight.shape[0], tile), lambda i: (0, i)),
        ],
        out_specs=(
            pl.BlockSpec((rows_here, tile), lambda i: (0, i)),
            pl.BlockSpec((away, tile), lambda i: (0, i)),
        ),
        scratch_shapes=[pltpu.VMEM((rows_core, heads * size), jnp.bfloat16)],
        compiler_params=pltpu.CompilerParams(vmem_limit_bytes=16 * MIB),
        cost_estimate=pl.CostEstimate(
            flops=2 * rows_core * heads * size * width,
            bytes_accessed=4 * out_weight.shape[0] * width,
            transcendentals=0,
        ),
    )(kept, came, out_weight, mate_weight)
    parts = []
    for k in range(1, members // 2):
        block = send[(k - 1) * rows_here : k * rows_here]
        parts.append(over(block, "mp", lambda i, k=k: i ^ (2 * k)))
    rows = call(
        norm_kernel,
        shape((rows_here, width + size), jnp.bfloat16),
        [vmem()] * (4 + len(parts)),
        16,
        0,
        rows_here * width * 8,
    )(own, hidden, final_gain[None], token_ids[:, None], *parts)

    ring = ring_order(groups)
    place = {group: at for at, group in enumerate(ring)}

    def ahead(block):
        return over(block, "req", lambda i: ring[(place[i] + 1) % groups])

    def behind(block):
        return over(block, "req", lambda i: ring[(place[i] - 1) % groups])

    vocabulary_here = head_weight.shape[1]
    weight = head_weight.T
    block = 400 if vocabulary_here % 400 == 0 else vocabulary_here
    first_word = (request * vocabulary_here)[None].astype(jnp.int32)

    def statistics(blocks):
        count = sum(part.shape[0] for part in blocks)
        return call(
            functools.partial(logits_kernel, block=block),
            shape((STATE, count)),
            [smem()] + [vmem()] * (len(blocks) + 1),
            10,
            2 * count * width * vocabulary_here,
            2 * width * vocabulary_here,
            scratch_shapes=[
                pltpu.VMEM((count, width), jnp.bfloat16),
                pltpu.VMEM((count, size), jnp.float32),
            ],
        )(first_word, *blocks, weight)

    passed, returned = [rows], [rows]
    for _ in range(groups // 2 - 1):
        passed.append(ahead(passed[-1]))
        returned.append(behind(returned[-1]))
    middle = rows_here // 2
    final = [ahead(passed[-1][:middle]), behind(returned[-1][middle:])]
    arrived = [[rows]] + [[passed[s], returned[s]] for s in range(1, groups // 2)] + [final]
    names = [[0]] + [[-s, s] for s in range(1, groups // 2)] + [[groups // 2]]
    found = {}
    batches = [[0, 1]] + [[s] for s in range(2, groups // 2 - 1)]
    batches += [[groups // 2 - 1, groups // 2]]
    for batch in batches:
        blocks = [part for s in batch for part in arrived[s]]
        table = statistics(blocks)
        at = 0
        for name in [name for s in batch for name in names[s]]:
            found[name % groups] = table[:, at : at + rows_here]
            at += rows_here
    stacked = jnp.stack([found[d] for d in range(groups)])
    where = jnp.array([place[group] for group in range(groups)], jnp.int32)
    stacked = jnp.take(stacked, (where - where[request]) % groups, axis=0)
    pooled = lax.all_to_all(stacked, "req", 0, 0)
    tops = pooled[:, 0]
    highest = jnp.max(tops, axis=0)
    scales = jnp.exp(tops - highest)
    total = jnp.sum(pooled[:, 1] * scales, axis=0)
    weighted = jnp.sum(pooled[:, 2] * scales, axis=0)
    picked = jnp.sum(pooled[:, 3], axis=0)
    log_total = highest + jnp.log(total)
    valid = member * rows_here + jnp.arange(rows_here) < rollout_len[0]
    logprob = jnp.where(valid, picked - log_total, 0.0)
    entropy = jnp.where(valid, log_total - weighted / total, 0.0)
    return (logprob, entropy)


def solution(mesh):
    placed = (
        P(("req", "mp"), None),
        P("req", "mp"),
        P("req", None, None),
        P("req", None, None),
        P("req", None, None),
        P("req", None, None),
        P("mp", None),
        P(),
        P(None, "req"),
        P(("req", "mp")),
        P("req"),
        P("req"),
        P("req"),
    )
    return jax.shard_map(
        body,
        mesh=mesh,
        in_specs=placed,
        out_specs=(P(("req", "mp")), P(("req", "mp"))),
        check_vma=False,
    )
```

time: 363 us -> 190 us (0.52)
  blocking collectives: 133 us -> 0 us
  waiting for transfers between devices: 135 us -> 65 us
  Pallas kernels: 0 us -> 51.2 us
  matrix products: 35.6 us -> 0 us
  local copies, waits for them, and re-layouts: 7.34 us -> 36.4 us
  between operations: 17 us -> 3.07 us
  other arithmetic: 12 us -> 2.59 us
  starting transfers between devices: 22.1 us -> 30.1 us
    all_gather x4 -> x0, blocking collectives: 122 us -> none  [combined_all(): everything = jax.tree.map(lambda part: lax.all_gather(part, axis), shard)]
    all_gather x1 -> x0, waiting for transfers between devices: 59.6 us -> none  [body(): block = lax.all_gather(normed, 'req', axis=0, tiled=True)]
    reduce_scatter x1 -> x0, waiting for transfers between devices: 51.9 us -> none  [body(): lax.psum_scatter(jnp.dot(block, out_weight, preferred_element_type=jnp.fl...]
    pallas_call x0 -> x9, Pallas kernels: none -> 51.2 us  [the longest x3 35.5 us: statistics(): call(functools.partial(logits_kernel, block=block), shape((STATE, count))...]
    dot_general x7 -> x0, matrix products: 35.6 us -> none  [the longest x1 23.6 us: body(): logits = jnp.dot(block, head_weight, preferred_element_type=jnp.float32)]
    ppermute x12 -> x16, waiting for transfers between devices: 23.8 us -> 59.2 us  [over(): return lax.ppermute(block, axis, pairs)]
    unnamed x25 -> x35, local copies, waits for them, and re-layouts: 0.98 us -> 32 us
    unnamed x1 -> x0, blocking collectives: 11.8 us -> none
  transfers between devices with their start and end apart: 14 -> 17, of which waited for: 6 -> 7; matrix products, arithmetic and copies ran while one was open for 3% -> 2% of each run, Pallas kernels for 0% -> 18%
where the time goes in v1:
time: 190 us; the launch traced here: 188 us
  waiting for transfers between devices  65 us (34%)
  Pallas kernels  51.2 us (27%)
  local copies, waits for them, and re-layouts  36.4 us (19%)
  starting transfers between devices  30.1 us (16%)
  between operations  3.07 us (2%)
  other arithmetic  2.59 us (1%)
    ppermute x16, waiting for transfers between devices, over(): return lax.ppermute(block, axis, pairs)  59.2 us
    pallas_call x3, Pallas kernels, statistics(): call(functools.partial(logits_kernel, block=block), shape((STATE, count))...  35.5 us
    unnamed x35, local copies, waits for them, and re-layouts  32 us
    ppermute x16, starting transfers between devices, over(): return lax.ppermute(block, axis, pairs)  26.8 us
    pallas_call x1, Pallas kernels, body(): call(functools.partial(more_kernel, size=size, scale=scale, slots=2, spli...  7.93 us
    all_to_all x1, waiting for transfers between devices, body(): pooled = lax.all_to_all(stacked, 'req', 0, 0)  5.87 us
    pallas_call x1, Pallas kernels, body(): pl.pallas_call(functools.partial(merge_kernel, size=size, rows=rows_here)...  4.45 us
  transfers between devices with their start and end apart: 17, of which 7 were waited for; matrix products, arithmetic and copies ran while one was open for 2% of the time, Pallas kernels for 18%

profile of v1, /device:TPU:0, one launch (start us, length us, event | category | flops | bytes accessed | tf_op | source)
XLA Modules:
  0.0 188.5 jit_solution(4524960647158172461)
XLA Ops:
  1.8 2.4 %constant_dynamic-slice_fusion.2 = (bf16[4,1,256,1,128]{4,3,2,1,0:T(2,128)(2,1)S(1)}, bf16[4,1,256,1,128]{4,3,2,1,0:T(2,128)(2,1)S(1)}) fusion(bf16[4,2,256,2,128]{4,3,2,1,0:T(2,128)(2,1)} %bitcast.71, s32[]{:T(128)S(6)} %select_n.108, s32[]{:T(128)S(6)} %select_n.111, bf16[4,2,256,2,128]{4,3,2,1,0:T(2,128)(2,1)} %bitcast.72), kind=kLoop, calls=%fused_computation.28 | loop fusion | bytes 1048584 | tf_op jit(solution)/shard_map/jit(dynamic_index_in_dim)/dynamic_slice | solution.py:230
  5.2 4.7 %collective-permute-start.1 = (bf16[2064,128]{1,0:T(8,128)(2,1)S(1)}, bf16[2064,128]{1,0:T(8,128)(2,1)S(1)}, u32[]{:S(2)}, u32[]{:S(2)}) collective-permute-start(bf16[2064,128]{1,0:T(8,128)(2,1)S(1)} %pad_maximum_fusion.kv), channel_id=1, source_target_pairs={{0,24},{4,28},{8,0},{12,4},{16,8},{20,12},{24,16},{28,20},{1,25},{... | collective-permute-start | bytes 1585160 | tf_op jit(solution)/shard_map/ppermute | solution.py:222
  9.9 1.3 collective-permute-start.4
  11.8 10.0 %collective-permute-done.1.refs_1_ = bf16[2064,128]{1,0:T(8,128)(2,1)S(1)} collective-permute-done((bf16[2064,128]{1,0:T(8,128)(2,1)S(1)}, bf16[2064,128]{1,0:T(8,128)(2,1)S(1)}, u32[]{:S(2)}, u32[]{:S(2)}) %collective-permute-start.1) | collective-permute-done | bytes 528416 | tf_op jit(solution)/shard_map/ppermute | solution.py:222
  21.8 1.5 collective-permute-start.2
  23.7 13.6 %collective-permute-done.2.refs_0_ = bf16[2064,128]{1,0:T(8,128)(2,1)S(1)} collective-permute-done((bf16[2064,128]{1,0:T(8,128)(2,1)S(1)}, bf16[2064,128]{1,0:T(8,128)(2,1)S(1)}, u32[]{:S(2)}, u32[]{:S(2)}) %collective-permute-start.2) | collective-permute-done | bytes 528416 | tf_op jit(solution)/shard_map/ppermute | solution.py:222
  37.3 0.7 collective-permute-start.3
  38.0 1.4 shard_map.149.refs_2_
  39.4 7.9 %shard_map.150.refs_1_ = f32[8,136,256]{2,1,0:T(8,128)S(1)} custom-call(s32[3]{0:T(128)S(1)} %pad_add_fusion.3.sc, bf16[256,1024]{1,0:T(8,128)(2,1)S(1)} %maximum_maximum_fusion.query, bf16[2064,128]{1,0:T(8,128)(2,1)S(1)} %collective-permute-done.4.refs_0_, bf16[2064,128]{1,0:T(8,128)(2,1)S(1)} %collective-permute-done.1.refs_1_, ...), custom_call_target="tpu_custom_call" | custom-call | flops 2147483648 | bytes 2097152 | tf_op jit(solution)/shard_map/pallas_call | solution.py:285
  47.3 0.7 shard_map.151.refs_1_
  48.0 0.9 shard_map.152
  49.0 1.9 %collective-permute-done.5.came = f32[8,136,128]{2,1,0:T(8,128)S(1)} collective-permute-done((f32[8,136,128]{2,1,0:T(8,128)S(1)}, f32[8,136,128]{2,1,0:T(8,128)S(1)}, u32[]{:S(2)}, u32[]{:S(2)}) %collective-permute-start.5) | collective-permute-done | bytes 557088 | tf_op jit(solution)/shard_map/ppermute | solution.py:222
  51.0 4.5 %shard_map.153 = (f32[64,4096]{1,0:T(8,128)S(1)}, bf16[64,4096]{1,0:T(8,128)(2,1)S(1)}) custom-call(f32[8,136,128]{2,1,0:T(8,128)S(1)} %get-tuple-element.6.kept, f32[8,136,128]{2,1,0:T(8,128)S(1)} %collective-permute-done.5.came, bf16[512,4096]{1,0:T(8,128)(2,1)S(1)} %copy-done.3, bf16[512,4096]{1,0:T(8,128)(2,1)} %collective-permute-done.6.mate), custom_call_target="tpu_custom_call" | custom-call | flops 1073741824 | bytes 8388608 | tf_op jit(solution)/shard_map/pallas_call | solution.py:315
  55.5 1.6 collective-permute-start.7
  57.2 12.3 %collective-permute-done.7.refs_0_ = bf16[64,4096]{1,0:T(8,128)(2,1)S(1)} collective-permute-done((bf16[64,4096]{1,0:T(8,128)(2,1)S(1)}, bf16[64,4096]{1,0:T(8,128)(2,1)S(1)}, u32[]{:S(2)}, u32[]{:S(2)}) %collective-permute-start.7) | collective-permute-done | bytes 524320 | tf_op jit(solution)/shard_map/ppermute | solution.py:222
  70.0 10.0 %collective-permute-start.9 = (bf16[64,4224]{1,0:T(8,128)(2,1)S(1)}, bf16[64,4224]{1,0:T(8,128)(2,1)S(1)}, u32[]{:S(2)}, u32[]{:S(2)}) collective-permute-start(bf16[64,4224]{1,0:T(8,128)(2,1)S(1)} %shard_map.154.refs_0_), channel_id=1, source_target_pairs={{0,4},{4,12},{8,0},{12,20},{16,8},{20,28},{24,16},{28,24},{1,5},{5... | collective-permute-start | bytes 1622024 | tf_op jit(solution)/shard_map/ppermute | solution.py:222
  79.9 11.7 %collective-permute-done.8.refs_1_ = bf16[64,4224]{1,0:T(8,128)(2,1)S(1)} collective-permute-done((bf16[64,4224]{1,0:T(8,128)(2,1)S(1)}, bf16[64,4224]{1,0:T(8,128)(2,1)S(1)}, u32[]{:S(2)}, u32[]{:S(2)}) %collective-permute-start.8) | collective-permute-done | bytes 540704 | tf_op jit(solution)/shard_map/ppermute | solution.py:222
  91.6 2.0 %collective-permute-start.11 = (bf16[64,4224]{1,0:T(8,128)(2,1)S(1)}, bf16[64,4224]{1,0:T(8,128)(2,1)S(1)}, u32[]{:S(2)}, u32[]{:S(2)}) collective-permute-start(bf16[64,4224]{1,0:T(8,128)(2,1)S(1)} %collective-permute-done.9.refs_2_), channel_id=1, source_target_pairs={{0,4},{4,12},{8,0},{12,20},{16,8},{20,28},{24,16},{28,24},{1,5},{5... | collective-permute-start | bytes 1622024 | tf_op jit(solution)/shard_map/ppermute | solution.py:222
  94.2 0.7 compare_and_fusion
  94.9 9.6 %collective-permute-done.10.refs_0_ = bf16[64,4224]{1,0:T(8,128)(2,1)S(1)} collective-permute-done((bf16[64,4224]{1,0:T(8,128)(2,1)S(1)}, bf16[64,4224]{1,0:T(8,128)(2,1)S(1)}, u32[]{:S(2)}, u32[]{:S(2)}) %collective-permute-start.10) | collective-permute-done | bytes 540704 | tf_op jit(solution)/shard_map/ppermute | solution.py:222
  104.8 1.7 collective-permute-start.13
  106.5 10.3 %copy-done = bf16[4096,4000]{0,1:T(8,128)(2,1)S(1)} copy-done((bf16[4096,4000]{0,1:T(8,128)(2,1)S(1)}, bf16[4096,4000]{0,1:T(8,128)(2,1)}, u32[]{:S(2)}) %copy-start) | copy-done | bytes 32768024
  116.8 12.2 %shard_map.155 = f32[8,192]{1,0:T(8,128)S(1)} custom-call(s32[1]{0:T(128)} %bitcast.2.sc, bf16[64,4224]{1,0:T(8,128)(2,1)S(1)} %shard_map.154.refs_0_, bf16[64,4224]{1,0:T(8,128)(2,1)S(1)} %collective-permute-done.8.refs_1_, bf16[64,4224]{1,0:T(8,128)(2,1)S(1)} %collective-permute-done.9.refs_2_, bf16[4000,4096]{1,0:T(8,128)(2,1)S(1)} %bitcast.62), custom_call_target="tpu_custom_call" | custom-call | flops 6291456000 | bytes 32768000 | tf_op jit(solution)/shard_map/pallas_call | solution.py:366
  129.4 1.8 collective-permute-start.15
  131.2 10.3 %copy-done.1 = bf16[4096,4000]{0,1:T(8,128)(2,1)S(1)} copy-done((bf16[4096,4000]{0,1:T(8,128)(2,1)S(1)}, bf16[4096,4000]{0,1:T(8,128)(2,1)}, u32[]{:S(2)}) %copy-start.1) | copy-done | bytes 32768024
  141.5 11.2 %shard_map.156 = f32[8,128]{1,0:T(8,128)S(1)} custom-call(s32[1]{0:T(128)} %bitcast.2.sc, bf16[64,4224]{1,0:T(8,128)(2,1)S(1)} %collective-permute-done.10.refs_0_, bf16[64,4224]{1,0:T(8,128)(2,1)S(1)} %collective-permute-done.11.refs_1_, bf16[4000,4096]{1,0:T(8,128)(2,1)S(1)} %bitcast.63), custom_call_target="tpu_custom_call" | custom-call | flops 4194304000 | bytes 32768000 | tf_op jit(solution)/shard_map/pallas_call | solution.py:366
  152.8 10.3 %copy-done.2 = bf16[4096,4000]{0,1:T(8,128)(2,1)S(1)} copy-done((bf16[4096,4000]{0,1:T(8,128)(2,1)S(1)}, bf16[4096,4000]{0,1:T(8,128)(2,1)}, u32[]{:S(2)}) %copy-start.2) | copy-done | bytes 32768024
  163.1 12.2 %shard_map.157 = f32[8,192]{1,0:T(8,128)S(1)} custom-call(s32[1]{0:T(128)} %bitcast.2.sc, bf16[64,4224]{1,0:T(8,128)(2,1)S(1)} %collective-permute-done.12.refs_0_, bf16[64,4224]{1,0:T(8,128)(2,1)S(1)} %collective-permute-done.13.refs_1_, bf16[32,4224]{1,0:T(8,128)(2,1)S(1)} %collective-permute-done.14.refs_2_, ...), custom_call_target="tpu_custom_call" | custom-call | flops 6291456000 | bytes 32768000 | tf_op jit(solution)/shard_map/pallas_call | solution.py:366
  176.1 0.7 reshape.43
  176.8 3.3 %all-to-all-start = ((f32[8,1,512]{2,1,0:T(1,128)}), f32[8,1,512]{2,1,0:T(1,128)S(1)}, u32[]{:S(2)}, u32[]{:S(2)}) async-start(f32[8,1,512]{2,1,0:T(1,128)} %reshape.43), calls=%async_computation | async-start | bytes 32768 | tf_op jit(solution)/shard_map/all_to_all | solution.py:400
  180.7 5.9 %all-to-all-done = f32[8,1,512]{2,1,0:T(1,128)S(1)} async-done(((f32[8,1,512]{2,1,0:T(1,128)}), f32[8,1,512]{2,1,0:T(1,128)S(1)}, u32[]{:S(2)}, u32[]{:S(2)}) %all-to-all-start) | async-done | bytes 16416 | tf_op jit(solution)/shard_map/all_to_all | solution.py:400
  187.1 0.7 reduce.2
  (77 shorter events, 5.6 us)
Async XLA Ops:
  0.6 50.4 %collective-permute-start.6 = (bf16[512,4096]{1,0:T(8,128)(2,1)}, bf16[512,4096]{1,0:T(8,128)(2,1)}, u32[]{:S(2)}, u32[]{:S(2)}) collective-permute-start(bf16[512,4096]{1,0:T(8,128)(2,1)} %mine.1), channel_id=1, source_target_pairs={{0,1},{1,0},{2,3},{3,2},{4,5},{5,4},{6,7},{7,6},{8,9},{9,8},{10,11... | collective-permute-start | bytes 12582920 | tf_op jit(solution)/shard_map/ppermute | solution.py:222
  4.3 7.0 %copy-start.6 = (bf16[256,512]{1,0:T(8,128)(2,1)S(1)}, bf16[256,512]{1,0:T(8,128)(2,1)}, u32[]{:S(2)}) copy-start(bf16[256,512]{1,0:T(8,128)(2,1)} %param.15) | copy-start | bytes 786436
  4.3 7.4 %copy-start.7 = (bf16[256,2,128]{2,1,0:T(2,128)(2,1)S(1)}, bf16[256,2,128]{2,1,0:T(2,128)(2,1)}, u32[]{:S(2)}) copy-start(bf16[256,2,128]{2,1,0:T(2,128)(2,1)} %param.17) | copy-start | bytes 393220
  4.3 7.4 %copy-start.8 = (bf16[256,2,128]{2,1,0:T(2,128)(2,1)S(1)}, bf16[256,2,128]{2,1,0:T(2,128)(2,1)}, u32[]{:S(2)}) copy-start(bf16[256,2,128]{2,1,0:T(2,128)(2,1)} %param.16) | copy-start | bytes 393220
  5.2 16.6 %collective-permute-start.1 = (bf16[2064,128]{1,0:T(8,128)(2,1)S(1)}, bf16[2064,128]{1,0:T(8,128)(2,1)S(1)}, u32[]{:S(2)}, u32[]{:S(2)}) collective-permute-start(bf16[2064,128]{1,0:T(8,128)(2,1)S(1)} %pad_maximum_fusion.kv), channel_id=1, source_target_pairs={{0,24},{4,28},{8,0},{12,4},{16,8},{20,12},{24,16},{28,20},{1,25},{... | collective-permute-start | bytes 1585160 | tf_op jit(solution)/shard_map/ppermute | solution.py:222
  9.9 29.4 %collective-permute-start.4 = (bf16[2064,128]{1,0:T(8,128)(2,1)S(1)}, bf16[2064,128]{1,0:T(8,128)(2,1)S(1)}, u32[]{:S(2)}, u32[]{:S(2)}) collective-permute-start(bf16[2064,128]{1,0:T(8,128)(2,1)S(1)} %pad_maximum_fusion.kv), channel_id=1, source_target_pairs={{4,0},{12,8},{20,16},{28,24},{5,1},{13,9},{21,17},{29,25},{6,2},{1... | collective-permute-start | bytes 1585160 | tf_op jit(solution)/shard_map/ppermute | solution.py:222
  11.2 12.4 %collective-permute-start = (bf16[256,512]{1,0:T(8,128)(2,1)S(1)}, bf16[256,512]{1,0:T(8,128)(2,1)S(1)}, u32[]{:S(2)}, u32[]{:S(2)}) collective-permute-start(bf16[256,512]{1,0:T(8,128)(2,1)S(1)} %copy-done.6), channel_id=1, source_target_pairs={{0,1},{1,0},{2,3},{3,2},{4,5},{5,4},{6,7},{7,6},{8,9},{9,8},{10,11... | collective-permute-start | bytes 786440 | tf_op jit(solution)/shard_map/ppermute | solution.py:222
  21.8 15.4 %collective-permute-start.2 = (bf16[2064,128]{1,0:T(8,128)(2,1)S(1)}, bf16[2064,128]{1,0:T(8,128)(2,1)S(1)}, u32[]{:S(2)}, u32[]{:S(2)}) collective-permute-start(bf16[2064,128]{1,0:T(8,128)(2,1)S(1)} %collective-permute-done.1.refs_1_), channel_id=1, source_target_pairs={{0,4},{4,0},{8,12},{12,8},{16,20},{20,16},{24,28},{28,24},{1,5},{5... | collective-permute-start | bytes 1585160 | tf_op jit(solution)/shard_map/ppermute | solution.py:222
  37.3 10.8 %collective-permute-start.3 = (bf16[2064,128]{1,0:T(8,128)(2,1)S(1)}, bf16[2064,128]{1,0:T(8,128)(2,1)S(1)}, u32[]{:S(2)}, u32[]{:S(2)}) collective-permute-start(bf16[2064,128]{1,0:T(8,128)(2,1)S(1)} %collective-permute-done.2.refs_0_), channel_id=1, source_target_pairs={{4,28},{12,4},{20,12},{28,20},{5,29},{13,5},{21,13},{29,21},{6,30}... | collective-permute-start | bytes 1585160 | tf_op jit(solution)/shard_map/ppermute | solution.py:222
  47.3 3.7 %copy-start.3 = (bf16[512,4096]{1,0:T(8,128)(2,1)S(1)}, bf16[512,4096]{1,0:T(8,128)(2,1)}, u32[]{:S(2)}) copy-start(bf16[512,4096]{1,0:T(8,128)(2,1)} %mine.1) | copy-start | bytes 12582916
  49.0 2.0 %collective-permute-start.5 = (f32[8,136,128]{2,1,0:T(8,128)S(1)}, f32[8,136,128]{2,1,0:T(8,128)S(1)}, u32[]{:S(2)}, u32[]{:S(2)}) collective-permute-start(f32[8,136,128]{2,1,0:T(8,128)S(1)} %get-tuple-element.7), channel_id=1, source_target_pairs={{0,1},{1,0},{2,3},{3,2},{4,5},{5,4},{6,7},{7,6},{8,9},{9,8},{10,11... | collective-permute-start | bytes 1671176 | tf_op jit(solution)/shard_map/ppermute | solution.py:222
  51.0 6.1 %copy-start.9 = (s32[64]{0:T(128)S(1)}, s32[64]{0:T(128)}, u32[]{:S(2)}) copy-start(s32[64]{0:T(128)} %param.23) | copy-start | bytes 772
  51.0 18.5 %copy-start.4 = (bf16[64,4096]{1,0:T(8,128)(2,1)S(1)}, bf16[64,4096]{1,0:T(8,128)(2,1)}, u32[]{:S(2)}) copy-start(bf16[64,4096]{1,0:T(8,128)(2,1)} %hidden.1) | copy-start | bytes 1572868
  51.0 18.5 %copy-start.5 = (f32[4096]{0:T(1024)S(1)}, f32[4096]{0:T(1024)}, u32[]{:S(2)}) copy-start(f32[4096]{0:T(1024)} %param.21) | copy-start | bytes 49156
  55.5 14.0 %collective-permute-start.7 = (bf16[64,4096]{1,0:T(8,128)(2,1)S(1)}, bf16[64,4096]{1,0:T(8,128)(2,1)S(1)}, u32[]{:S(2)}, u32[]{:S(2)}) collective-permute-start(bf16[64,4096]{1,0:T(8,128)(2,1)S(1)} %get-tuple-element.9), channel_id=1, source_target_pairs={{0,2},{1,3},{2,0},{3,1},{4,6},{5,7},{6,4},{7,5},{8,10},{9,11},{10,... | collective-permute-start | bytes 1572872 | tf_op jit(solution)/shard_map/ppermute | solution.py:222
  69.5 24.2 %copy-start.10 = (s32[8]{0:T(128)S(1)}, s32[8]{0:T(128)}, u32[]{:S(2)}) copy-start(s32[8]{0:T(128)} %constant.208.clone) | copy-start | bytes 100
  69.9 21.7 %collective-permute-start.8 = (bf16[64,4224]{1,0:T(8,128)(2,1)S(1)}, bf16[64,4224]{1,0:T(8,128)(2,1)S(1)}, u32[]{:S(2)}, u32[]{:S(2)}) collective-permute-start(bf16[64,4224]{1,0:T(8,128)(2,1)S(1)} %shard_map.154.refs_0_), channel_id=1, source_target_pairs={{0,8},{4,0},{8,16},{12,4},{16,24},{20,12},{24,28},{28,20},{1,9},{5... | collective-permute-start | bytes 1622024 | tf_op jit(solution)/shard_map/ppermute | solution.py:222
  70.0 21.7 %collective-permute-start.9 = (bf16[64,4224]{1,0:T(8,128)(2,1)S(1)}, bf16[64,4224]{1,0:T(8,128)(2,1)S(1)}, u32[]{:S(2)}, u32[]{:S(2)}) collective-permute-start(bf16[64,4224]{1,0:T(8,128)(2,1)S(1)} %shard_map.154.refs_0_), channel_id=1, source_target_pairs={{0,4},{4,12},{8,0},{12,20},{16,8},{20,28},{24,16},{28,24},{1,5},{5... | collective-permute-start | bytes 1622024 | tf_op jit(solution)/shard_map/ppermute | solution.py:222
  91.6 12.9 %collective-permute-start.10 = (bf16[64,4224]{1,0:T(8,128)(2,1)S(1)}, bf16[64,4224]{1,0:T(8,128)(2,1)S(1)}, u32[]{:S(2)}, u32[]{:S(2)}) collective-permute-start(bf16[64,4224]{1,0:T(8,128)(2,1)S(1)} %collective-permute-done.8.refs_1_), channel_id=1, source_target_pairs={{0,8},{4,0},{8,16},{12,4},{16,24},{20,12},{24,28},{28,20},{1,9},{5... | collective-permute-start | bytes 1622024 | tf_op jit(solution)/shard_map/ppermute | solution.py:222
  91.6 13.1 %collective-permute-start.11 = (bf16[64,4224]{1,0:T(8,128)(2,1)S(1)}, bf16[64,4224]{1,0:T(8,128)(2,1)S(1)}, u32[]{:S(2)}, u32[]{:S(2)}) collective-permute-start(bf16[64,4224]{1,0:T(8,128)(2,1)S(1)} %collective-permute-done.9.refs_2_), channel_id=1, source_target_pairs={{0,4},{4,12},{8,0},{12,20},{16,8},{20,28},{24,16},{28,24},{1,5},{5... | collective-permute-start | bytes 1622024 | tf_op jit(solution)/shard_map/ppermute | solution.py:222
  104.5 24.5 %collective-permute-start.12 = (bf16[64,4224]{1,0:T(8,128)(2,1)S(1)}, bf16[64,4224]{1,0:T(8,128)(2,1)S(1)}, u32[]{:S(2)}, u32[]{:S(2)}) collective-permute-start(bf16[64,4224]{1,0:T(8,128)(2,1)S(1)} %collective-permute-done.10.refs_0_), channel_id=1, source_target_pairs={{0,8},{4,0},{8,16},{12,4},{16,24},{20,12},{24,28},{28,20},{1,9},{5... | collective-permute-start | bytes 1622024 | tf_op jit(solution)/shard_map/ppermute | solution.py:222
  104.8 24.6 %collective-permute-start.13 = (bf16[64,4224]{1,0:T(8,128)(2,1)S(1)}, bf16[64,4224]{1,0:T(8,128)(2,1)S(1)}, u32[]{:S(2)}, u32[]{:S(2)}) collective-permute-start(bf16[64,4224]{1,0:T(8,128)(2,1)S(1)} %collective-permute-done.11.refs_1_), channel_id=1, source_target_pairs={{0,4},{4,12},{8,0},{12,20},{16,8},{20,28},{24,16},{28,24},{1,5},{5... | collective-permute-start | bytes 1622024 | tf_op jit(solution)/shard_map/ppermute | solution.py:222
  106.5 10.3 %copy-start = (bf16[4096,4000]{0,1:T(8,128)(2,1)S(1)}, bf16[4096,4000]{0,1:T(8,128)(2,1)}, u32[]{:S(2)}) copy-start(bf16[4096,4000]{0,1:T(8,128)(2,1)} %param.22) | copy-start | bytes 98304000
  129.1 23.7 %collective-permute-start.14 = (bf16[32,4224]{1,0:T(8,128)(2,1)S(1)}, bf16[32,4224]{1,0:T(8,128)(2,1)S(1)}, u32[]{:S(2)}, u32[]{:S(2)}) collective-permute-start(bf16[32,4224]{1,0:T(8,128)(2,1)S(1)} %slice.60), channel_id=1, source_target_pairs={{0,8},{4,0},{8,16},{12,4},{16,24},{20,12},{24,28},{28,20},{1,9},{5... | collective-permute-start | bytes 811016 | tf_op jit(solution)/shard_map/ppermute | solution.py:222
  129.4 23.4 %collective-permute-start.15 = (bf16[32,4224]{1,0:T(8,128)(2,1)S(1)}, bf16[32,4224]{1,0:T(8,128)(2,1)S(1)}, u32[]{:S(2)}, u32[]{:S(2)}) collective-permute-start(bf16[32,4224]{1,0:T(8,128)(2,1)S(1)} %slice.61), channel_id=1, source_target_pairs={{0,4},{4,12},{8,0},{12,20},{16,8},{20,28},{24,16},{28,24},{1,5},{5... | collective-permute-start | bytes 811016 | tf_op jit(solution)/shard_map/ppermute | solution.py:222
  131.2 10.3 %copy-start.1 = (bf16[4096,4000]{0,1:T(8,128)(2,1)S(1)}, bf16[4096,4000]{0,1:T(8,128)(2,1)}, u32[]{:S(2)}) copy-start(bf16[4096,4000]{0,1:T(8,128)(2,1)} %param.22) | copy-start | bytes 98304000
  152.8 10.3 %copy-start.2 = (bf16[4096,4000]{0,1:T(8,128)(2,1)S(1)}, bf16[4096,4000]{0,1:T(8,128)(2,1)}, u32[]{:S(2)}) copy-start(bf16[4096,4000]{0,1:T(8,128)(2,1)} %param.22) | copy-start | bytes 98304000
  176.8 9.8 %all-to-all-start = ((f32[8,1,512]{2,1,0:T(1,128)}), f32[8,1,512]{2,1,0:T(1,128)S(1)}, u32[]{:S(2)}, u32[]{:S(2)}) async-start(f32[8,1,512]{2,1,0:T(1,128)} %reshape.43), calls=%async_computation | async-start | bytes 32768 | tf_op jit(solution)/shard_map/all_to_all | solution.py:400

commit v2 on v1

--- a/solution.py
+++ b/solution.py
@@ -12,6 +12,7 @@
 BLOCK = 256
 META = 16
 STATE = 8
+FACTS = 5
 MIB = 1 << 20
 
 
@@ -80,10 +81,11 @@
         weights = jnp.exp2(scores - top)
         state[h, :size, :] = tn(values[...], weights.astype(jnp.bfloat16))
         put_state(state, h, size, top, jnp.sum(weights, axis=0, keepdims=True))
-    attend_slab(core, sc[1], kv, query, state, size, scale)
-
-
-def more_kernel(sc, query, *refs, size, scale, slots, split):
+    attend_slab(core, 0, kv, query, state, size, scale)
+
+
+def more_kernel(sc, query, *refs, size, scale, wants, split):
+    slots = len(wants)
     kvs, given, outs = refs[:slots], refs[slots], refs[slots + 1 :]
     if split:
         state = outs[2]
@@ -91,14 +93,15 @@
         state = outs[0]
     state[...] = given[...]
     for i, kv in enumerate(kvs):
-        attend_slab(sc[0], sc[1 + i], kv, query, state, size, scale)
+        attend_slab(sc[0], sc[1] if wants[i] is None else wants[i], kv, query, state, size, scale)
     if split:
         middle = state.shape[2] // 2
         outs[0][...] = state[:, :, :middle]
         outs[1][...] = state[:, :, middle:]
 
 
-def merge_kernel(kept, came, mine, mate, own, send, mixed, *, size, rows):
+def merge_kernel(kept, came, mine, mate, own, *refs, size, rows):
+    sends, mixed = refs[:-1], refs[-1]
     heads = kept.shape[0]
 
     @pl.when(pl.program_id(0) == 0)
@@ -116,7 +119,10 @@
     out = jnp.dot(mixed[:, :width], mine[...], preferred_element_type=jnp.float32)
     out += jnp.dot(mixed[:, width:], mate[...], preferred_element_type=jnp.float32)
     own[...] = out[:rows, :]
-    send[...] = out[rows:, :].astype(jnp.bfloat16)
+    at = rows
+    for send in sends:
+        send[...] = out[at : at + send.shape[0], :].astype(jnp.bfloat16)
+        at += send.shape[0]
 
 
 def norm_kernel(own, hidden, gain, words, *refs):
@@ -132,38 +138,75 @@
     out[:, width:] = code.astype(jnp.float32).astype(jnp.bfloat16)
 
 
-def logits_kernel(sc, *refs, block):
-    parts, weight, out, rows, codes = refs[:-4], refs[-4], refs[-3], refs[-2], refs[-1]
+def head_kernel(sc, *refs, block, homes, given):
+    parts, weight = refs[: len(homes)], refs[len(homes)]
+    table, rows, codes, slots, sems = refs[-5:]
     width = weight.shape[1]
-    at = 0
-    for part in parts:
-        rows[at : at + part.shape[0], :] = part[:, :width]
-        codes[at : at + part.shape[0], :] = part[:, width:].astype(jnp.float32)
-        at += part.shape[0]
+    deep = parts[0].shape[0]
+    count = deep * len(homes)
+    depth = slots.shape[0]
+    steps = weight.shape[0] // block
+
+    def fetch(i):
+        start, slot = pl.multiple_of(i * block, 8), lax.rem(i, depth)
+        source = weight.at[pl.ds(start, block), :]
+        return pltpu.make_async_copy(source, slots.at[slot], sems.at[slot])
+
+    for i in range(min(depth - 1, steps)):
+        fetch(i).start()
+    for i, part in enumerate(parts):
+        rows[i * deep : (i + 1) * deep, :] = part[:, :width]
+        codes[i * deep : (i + 1) * deep, :] = part[:, width:].astype(jnp.float32)
     turned = codes[...].T
-    words = (turned[0:1, :] * 256.0 + turned[1:2, :]).astype(jnp.int32) - sc[0]
-    count = at
+    words = (turned[0:1, :] * 256.0 + turned[1:2, :]).astype(jnp.int32) - sc[2]
     place = lax.broadcasted_iota(jnp.int32, (block, 1), 0)
 
     def step(i, carry):
         top, total, weighted, picked = carry
-        start = pl.multiple_of(i * block, 8)
-        logits = nt(weight[pl.ds(start, block), :], rows[...])
+        fetch(i).wait()
+
+        @pl.when(i + depth - 1 < steps)
+        def _():
+            fetch(i + depth - 1).start()
+
+        logits = nt(slots[lax.rem(i, depth)], rows[...])
         now = jnp.maximum(top, jnp.max(logits, axis=0, keepdims=True))
         old = jnp.exp(top - now)
         spread = jnp.exp(logits - now)
         total = total * old + jnp.sum(spread, axis=0, keepdims=True)
         weighted = weighted * old + jnp.sum(spread * logits, axis=0, keepdims=True)
-        hit = place == words - start
+        hit = place == words - i * block
         picked = picked + jnp.sum(jnp.where(hit, logits, 0.0), axis=0, keepdims=True)
         return now, total, weighted, picked
 
     zero = jnp.zeros((1, count), jnp.float32)
     carry = (jnp.full((1, count), NEGATIVE, jnp.float32), zero, zero, zero)
-    top, total, weighted, picked = lax.fori_loop(0, weight.shape[0] // block, step, carry)
+    top, total, weighted, picked = lax.fori_loop(0, steps, step, carry)
     line = lax.broadcasted_iota(jnp.int32, (STATE, count), 0)
-    result = jnp.where(line == 0, top, jnp.where(line == 1, total, weighted))
-    out[...] = jnp.where(line == 3, picked, result)
+    value = jnp.where(line == 0, top, jnp.where(line == 1, total, weighted))
+    value = jnp.where(line == 3, picked, value)
+    if given:
+        table[...] = refs[len(homes) + 1][...]
+    else:
+        table[...] = jnp.zeros_like(table)
+    for i, (name, side) in enumerate(homes):
+        piece = value[:, i * deep : (i + 1) * deep]
+        table[sc[FACTS + name], :, side * deep : (side + 1) * deep] = piece
+
+
+def final_kernel(sc, pooled, out):
+    tops = pooled[:, 0:1, :]
+    highest = jnp.max(tops, axis=0)
+    scales = jnp.exp(tops - highest[None])
+    total = jnp.sum(pooled[:, 1:2, :] * scales, axis=0)
+    weighted = jnp.sum(pooled[:, 2:3, :] * scales, axis=0)
+    picked = jnp.sum(pooled[:, 3:4, :], axis=0)
+    log_total = highest + jnp.log(total)
+    place = lax.broadcasted_iota(jnp.int32, (1, pooled.shape[2]), 1) + sc[3]
+    valid = place < sc[4]
+    line = lax.broadcasted_iota(jnp.int32, (STATE, pooled.shape[2]), 0)
+    value = jnp.where(line == 0, picked - log_total, log_total - weighted / total)
+    out[...] = jnp.where(valid, value, 0.0)
 
 
 def smem():
@@ -240,8 +283,15 @@
     one = over(kv, "req", lambda i: i - 1 if i % 2 else None)
     mate_queries = over(queries, "mp", lambda i: i ^ 1)
     mate_weight = over(out_weight, "mp", lambda i: i ^ 1)
-    swap = over(two, "req", lambda i: i ^ 1)
-    three = over(swap, "req", lambda i: (i - 2) % groups if i % 2 else None)
+
+    vocabulary_here = head_weight.shape[1]
+    tour = jnp.array(ring_order(groups), jnp.int32)
+    at = jnp.sum(jnp.where(tour == request, jnp.arange(groups, dtype=jnp.int32), 0))
+    spots = (at + jnp.arange(groups, dtype=jnp.int32)) % groups
+    match = spots[:, None] == jnp.arange(groups, dtype=jnp.int32)[None]
+    homes = jnp.sum(jnp.where(match, tour[None], 0), axis=1)
+    facts = [core, 3 - 2 * (request % 2), request * vocabulary_here, member * rows_here, rollout_len[0]]
+    plan = jnp.concatenate([jnp.stack(facts).astype(jnp.int32), homes])
 
     order = list(range(0, members, 2)) + list(range(1, members, 2))
 
@@ -261,7 +311,6 @@
 
     full = shape((heads, size + STATE, rollout))
     part = shape((heads, size + STATE, rollout // 2))
-    numbers = functools.partial(jnp.stack)
     work = 4 * heads * rollout * half * size
     state = call(
         functools.partial(first_kernel, size=size, scale=scale),
@@ -271,50 +320,51 @@
         work,
         2 * half * size * 4,
     )(
-        jnp.stack([core, jnp.zeros_like(core)]),
+        plan,
         times,
         query,
         own_half(rotated_rollout_keys),
         own_half(rollout_value_matrix),
         kv,
     )
-    even = request % 2 == 0
-    first_tags = jnp.stack([core, jnp.full_like(core, 1), jnp.full_like(core, 2)])
-    swap_tags = jnp.stack([core, jnp.where(even, 3, 1)])
-    last_tags = jnp.stack([core, jnp.full_like(core, 3)])
+    two, state = lax.optimization_barrier((two, state))
+    swap = over(two, "req", lambda i: i ^ 1)
     state = call(
-        functools.partial(more_kernel, size=size, scale=scale, slots=2, split=False),
+        functools.partial(more_kernel, size=size, scale=scale, wants=(1, 2), split=False),
         full,
         [smem()] + [vmem()] * 4,
         16,
         2 * work,
         4 * half * size * 4,
-    )(first_tags, query, one, two, state)
+    )(plan, query, one, two, state)
+    swap, state = lax.optimization_barrier((swap, state))
+    three = over(swap, "req", lambda i: (i - 2) % groups if i % 2 else None)
     state = call(
-        functools.partial(more_kernel, size=size, scale=scale, slots=1, split=False),
+        functools.partial(more_kernel, size=size, scale=scale, wants=(None,), split=False),
         full,
         [smem()] + [vmem()] * 3,
         16,
         work,
         2 * half * size * 4,
-    )(swap_tags, query, swap, state)
+    )(plan, query, swap, state)
     kept, sent = call(
-        functools.partial(more_kernel, size=size, scale=scale, slots=1, split=True),
+        functools.partial(more_kernel, size=size, scale=scale, wants=(3,), split=True),
         (part, part),
         [smem()] + [vmem()] * 3,
         16,
         work,
         2 * half * size * 4,
         scratch_shapes=[pltpu.VMEM(full.shape, jnp.float32)],
-    )(last_tags, query, three, state)
+    )(plan, query, three, state)
     came = over(sent, "mp", lambda i: i ^ 1)
 
     tile = 1024
     rows_core = rollout // 2
-    away = rows_core - rows_here
-    own, send = pl.pallas_call(
+    deep = rows_here // 2
+    pieces = [(k, side) for k in range(1, members // 2) for side in (0, 1)]
+    own, *sends = pl.pallas_call(
         functools.partial(merge_kernel, size=size, rows=rows_here),
-        out_shape=(shape((rows_here, width)), shape((away, width), jnp.bfloat16)),
+        out_shape=(shape((rows_here, width)), *[shape((deep, width), jnp.bfloat16)] * len(pieces)),
         grid=(width // tile,),
         in_specs=[
             pl.BlockSpec(part.shape, lambda i: (0, 0, 0)),
@@ -324,7 +374,7 @@
         ],
         out_specs=(
             pl.BlockSpec((rows_here, tile), lambda i: (0, i)),
-            pl.BlockSpec((away, tile), lambda i: (0, i)),
+            *[pl.BlockSpec((deep, tile), lambda i: (0, i))] * len(pieces),
         ),
         scratch_shapes=[pltpu.VMEM((rows_core, heads * size), jnp.bfloat16)],
         compiler_params=pltpu.CompilerParams(vmem_limit_bytes=16 * MIB),
@@ -334,18 +384,6 @@
             transcendentals=0,
         ),
     )(kept, came, out_weight, mate_weight)
-    parts = []
-    for k in range(1, members // 2):
-        block = send[(k - 1) * rows_here : k * rows_here]
-        parts.append(over(block, "mp", lambda i, k=k: i ^ (2 * k)))
-    rows = call(
-        norm_kernel,
-        shape((rows_here, width + size), jnp.bfloat16),
-        [vmem()] * (4 + len(parts)),
-        16,
-        0,
-        rows_here * width * 8,
-    )(own, hidden, final_gain[None], token_ids[:, None], *parts)
 
     ring = ring_order(groups)
     place = {group: at for at, group in enumerate(ring)}
@@ -356,59 +394,76 @@
     def behind(block):
         return over(block, "req", lambda i: ring[(place[i] - 1) % groups])
 
-    vocabulary_here = head_weight.shape[1]
+    def normed(side):
+        came = [
+            over(block, "mp", lambda i, k=k: i ^ (2 * k))
+            for (k, half_side), block in zip(pieces, sends)
+            if half_side == side
+        ]
+
+        def cut(columns):
+            return pl.BlockSpec((deep, columns), lambda i: (side, 0))
+
+        return pl.pallas_call(
+            norm_kernel,
+            out_shape=shape((deep, width + size), jnp.bfloat16),
+            grid=(1,),
+            in_specs=[cut(width), cut(width), pl.BlockSpec((1, width), lambda i: (0, 0)), cut(1)]
+            + [pl.BlockSpec((deep, width), lambda i: (0, 0))] * len(came),
+            out_specs=pl.BlockSpec((deep, width + size), lambda i: (0, 0)),
+            compiler_params=pltpu.CompilerParams(vmem_limit_bytes=8 * MIB),
+            cost_estimate=pl.CostEstimate(
+                flops=0, bytes_accessed=deep * width * 8, transcendentals=0
+            ),
+        )(own, hidden, final_gain[None], token_ids[:, None], *came)
+
     weight = head_weight.T
     block = 400 if vocabulary_here % 400 == 0 else vocabulary_here
-    first_word = (request * vocabulary_here)[None].astype(jnp.int32)
-
-    def statistics(blocks):
-        count = sum(part.shape[0] for part in blocks)
-        return call(
-            functools.partial(logits_kernel, block=block),
-            shape((STATE, count)),
-            [smem()] + [vmem()] * (len(blocks) + 1),
-            10,
+    forth, back = [None, None], [None, None]
+    ready = [[], []]
+    for side in (0, 1):
+        forth[side] = back[side] = normed(side)
+        ready[side].append((0, side, forth[side]))
+    for step in range(1, groups // 2):
+        for side in (0, 1):
+            forth[side], back[side] = ahead(forth[side]), behind(back[side])
+            ready[side] += [(-step % groups, side, forth[side]), (step, side, back[side])]
+    final = [(groups // 2, 0, ahead(forth[0])), (groups // 2, 1, behind(back[1]))]
+    own_rows, *_ = lax.optimization_barrier((ready[0][0][2], forth[1], back[1]))
+    ready[0][0] = (0, 0, own_rows)
+    arrived = ready[0] + ready[1] + final
+    batch = max(1, 256 // deep)
+    depth = 4
+    table = None
+    for at in range(0, len(arrived), batch):
+        now = arrived[at : at + batch]
+        count = deep * len(now)
+        given = [] if table is None else [table]
+        table = call(
+            functools.partial(
+                head_kernel,
+                block=block,
+                homes=[(name, side) for name, side, _ in now],
+                given=len(given),
+            ),
+            shape((groups, STATE, 128)),
+            [smem()]
+            + [vmem()] * len(now)
+            + [pl.BlockSpec(memory_space=pl.ANY)]
+            + [vmem()] * len(given),
+            44,
             2 * count * width * vocabulary_here,
             2 * width * vocabulary_here,
             scratch_shapes=[
                 pltpu.VMEM((count, width), jnp.bfloat16),
                 pltpu.VMEM((count, size), jnp.float32),
+                pltpu.VMEM((depth, block, width), jnp.bfloat16),
+                pltpu.SemaphoreType.DMA((depth,)),
             ],
-        )(first_word, *blocks, weight)
-
-    passed, returned = [rows], [rows]
-    for _ in range(groups // 2 - 1):
-        passed.append(ahead(passed[-1]))
-        returned.append(behind(returned[-1]))
-    middle = rows_here // 2
-    final = [ahead(passed[-1][:middle]), behind(returned[-1][middle:])]
-    arrived = [[rows]] + [[passed[s], returned[s]] for s in range(1, groups // 2)] + [final]
-    names = [[0]] + [[-s, s] for s in range(1, groups // 2)] + [[groups // 2]]
-    found = {}
-    batches = [[0, 1]] + [[s] for s in range(2, groups // 2 - 1)]
-    batches += [[groups // 2 - 1, groups // 2]]
-    for batch in batches:
-        blocks = [part for s in batch for part in arrived[s]]
-        table = statistics(blocks)
-        at = 0
-        for name in [name for s in batch for name in names[s]]:
-            found[name % groups] = table[:, at : at + rows_here]
-            at += rows_here
-    stacked = jnp.stack([found[d] for d in range(groups)])
-    where = jnp.array([place[group] for group in range(groups)], jnp.int32)
-    stacked = jnp.take(stacked, (where - where[request]) % groups, axis=0)
-    pooled = lax.all_to_all(stacked, "req", 0, 0)
-    tops = pooled[:, 0]
-    highest = jnp.max(tops, axis=0)
-    scales = jnp.exp(tops - highest)
-    total = jnp.sum(pooled[:, 1] * scales, axis=0)
-    weighted = jnp.sum(pooled[:, 2] * scales, axis=0)
-    picked = jnp.sum(pooled[:, 3], axis=0)
-    log_total = highest + jnp.log(total)
-    valid = member * rows_here + jnp.arange(rows_here) < rollout_len[0]
-    logprob = jnp.where(valid, picked - log_total, 0.0)
-    entropy = jnp.where(valid, log_total - weighted / total, 0.0)
-    return (logprob, entropy)
+        )(plan, *[rows for _, _, rows in now], weight, *given)
+    pooled = lax.all_to_all(table, "req", 0, 0)
+    out = call(final_kernel, shape((STATE, 128)), [smem(), vmem()], 4)(plan, pooled)
+    return (out[0, :rows_here], out[1, :rows_here])
 
 
 def solution(mesh):

time: 190 us -> 157 us (0.83)
  local copies, waits for them, and re-layouts: 36.4 us -> 3.41 us
  starting transfers between devices: 30.1 us -> 51.1 us
  waiting for transfers between devices: 65 us -> 44.4 us
  blocking collectives: 0 us -> 11.6 us
  Pallas kernels: 51.2 us -> 40.3 us
    unnamed x35 -> x20, local copies, waits for them, and re-layouts: 32 us -> 0.14 us
    ppermute x16 -> x23, starting transfers between devices: 26.8 us -> 51.1 us  [over(): return lax.ppermute(block, axis, pairs)]
    ppermute x16 -> x23, waiting for transfers between devices: 59.2 us -> 44.4 us  [over(): return lax.ppermute(block, axis, pairs)]
    all_to_all x0 -> x1, blocking collectives: none -> 11.6 us  [body(): pooled = lax.all_to_all(table, 'req', 0, 0)]
    pallas_call x7 -> x8, Pallas kernels: 45.4 us -> 34.5 us  [the longest x2 28.7 us: body(): call(functools.partial(head_kernel, block=block, homes=[(name, side) for...]
    all_to_all x1 -> x0, waiting for transfers between devices: 5.87 us -> none  [body(): pooled = lax.all_to_all(stacked, 'req', 0, 0)]
    all_to_all x1 -> x0, starting transfers between devices: 3.32 us -> none  [body(): pooled = lax.all_to_all(stacked, 'req', 0, 0)]
  transfers between devices with their start and end apart: 17 -> 23, of which waited for: 7 -> 11; matrix products, arithmetic and copies ran while one was open for 2% -> 3% of each run, Pallas kernels for 18% -> 13%
where the time goes in v2:
time: 157 us; the launch traced here: 156 us
  starting transfers between devices  51.1 us (33%)
  waiting for transfers between devices  44.4 us (28%)
  Pallas kernels  40.3 us (26%)
  blocking collectives  11.6 us (7%)
  local copies, waits for them, and re-layouts  3.41 us (2%)
  between operations  3.15 us (2%)
  other arithmetic  1.73 us (1%)
    ppermute x23, starting transfers between devices, over(): return lax.ppermute(block, axis, pairs)  51.1 us
    ppermute x23, waiting for transfers between devices, over(): return lax.ppermute(block, axis, pairs)  44.4 us
    pallas_call x2, Pallas kernels, body(): call(functools.partial(head_kernel, block=block, homes=[(name, side) for...  28.7 us
    all_to_all x1, blocking collectives, body(): pooled = lax.all_to_all(table, 'req', 0, 0)  11.6 us
    pallas_call x1, Pallas kernels, body(): pl.pallas_call(functools.partial(merge_kernel, size=size, rows=rows_here)...  4.45 us
    pallas_call x1, Pallas kernels, body(): call(functools.partial(more_kernel, size=size, scale=scale, wants=(1, 2),...  3.18 us
  transfers between devices with their start and end apart: 23, of which 11 were waited for; matrix products, arithmetic and copies ran while one was open for 3% of the time, Pallas kernels for 13%

profile of v2, /device:TPU:0, one launch (start us, length us, event | category | flops | bytes accessed | tf_op | source)
XLA Modules:
  0.0 155.7 jit_solution(6328955234464942662)
XLA Ops:
  1.8 2.4 %constant_dynamic-slice_fusion.2 = (bf16[4,1,256,1,128]{4,3,2,1,0:T(2,128)(2,1)S(1)}, bf16[4,1,256,1,128]{4,3,2,1,0:T(2,128)(2,1)S(1)}) fusion(bf16[4,2,256,2,128]{4,3,2,1,0:T(2,128)(2,1)} %bitcast.38, s32[]{:T(128)S(6)} %select_n.98, s32[]{:T(128)S(6)} %select_n.101, bf16[4,2,256,2,128]{4,3,2,1,0:T(2,128)(2,1)} %bitcast.39), kind=kLoop, calls=%fused_computation.9 | loop fusion | bytes 1048584 | tf_op jit(solution)/shard_map/jit(dynamic_index_in_dim)/dynamic_slice | solution.py:273
  5.3 4.7 %collective-permute-start.1 = (bf16[2064,128]{1,0:T(8,128)(2,1)S(1)}, bf16[2064,128]{1,0:T(8,128)(2,1)S(1)}, u32[]{:S(2)}, u32[]{:S(2)}) collective-permute-start(bf16[2064,128]{1,0:T(8,128)(2,1)S(1)} %pad_maximum_fusion.kv), channel_id=1, source_target_pairs={{0,24},{4,28},{8,0},{12,4},{16,8},{20,12},{24,16},{28,20},{1,25},{... | collective-permute-start | bytes 1585160 | tf_op jit(solution)/shard_map/ppermute | solution.py:265
  10.0 1.3 collective-permute-start.3
  12.2 0.7 and_select_fusion
  14.2 1.4 shard_map.149.refs_2_
  15.6 6.3 %collective-permute-done.1.refs_1_ = bf16[2064,128]{1,0:T(8,128)(2,1)S(1)} collective-permute-done((bf16[2064,128]{1,0:T(8,128)(2,1)S(1)}, bf16[2064,128]{1,0:T(8,128)(2,1)S(1)}, u32[]{:S(2)}, u32[]{:S(2)}) %collective-permute-start.1) | collective-permute-done | bytes 528416 | tf_op jit(solution)/shard_map/ppermute | solution.py:265
  21.9 5.8 %collective-permute-start.2 = (bf16[2064,128]{1,0:T(8,128)(2,1)S(1)}, bf16[2064,128]{1,0:T(8,128)(2,1)S(1)}, u32[]{:S(2)}, u32[]{:S(2)}) collective-permute-start(bf16[2064,128]{1,0:T(8,128)(2,1)S(1)} %collective-permute-done.1.refs_1_), channel_id=1, source_target_pairs={{0,4},{4,0},{8,12},{12,8},{16,20},{20,16},{24,28},{28,24},{1,5},{5... | collective-permute-start | bytes 1585160 | tf_op jit(solution)/shard_map/ppermute | solution.py:265
  27.7 3.2 %shard_map.150.refs_1_ = f32[8,136,256]{2,1,0:T(8,128)S(1)} custom-call(s32[13]{0:T(128)S(1)} %concatenate.18.sc, bf16[256,1024]{1,0:T(8,128)(2,1)S(1)} %maximum_maximum_fusion.query, bf16[2064,128]{1,0:T(8,128)(2,1)S(1)} %collective-permute-done.3.refs_0_, bf16[2064,128]{1,0:T(8,128)(2,1)S(1)} %collective-permute-done.1.refs_1_, ...), custom_call_target="tpu_custom_call" | custom-call | flops 2147483648 | bytes 2097152 | tf_op jit(solution)/shard_map/pallas_call | solution.py:332
  30.9 9.4 %collective-permute-done.2.refs_0_ = bf16[2064,128]{1,0:T(8,128)(2,1)S(1)} collective-permute-done((bf16[2064,128]{1,0:T(8,128)(2,1)S(1)}, bf16[2064,128]{1,0:T(8,128)(2,1)S(1)}, u32[]{:S(2)}, u32[]{:S(2)}) %collective-permute-start.2) | collective-permute-done | bytes 528416 | tf_op jit(solution)/shard_map/ppermute | solution.py:265
  40.4 0.7 collective-permute-start.4
  41.1 0.7 shard_map.151.refs_1_
  41.7 0.9 shard_map.152
  42.8 1.9 %collective-permute-done.5.came = f32[8,136,128]{2,1,0:T(8,128)S(1)} collective-permute-done((f32[8,136,128]{2,1,0:T(8,128)S(1)}, f32[8,136,128]{2,1,0:T(8,128)S(1)}, u32[]{:S(2)}, u32[]{:S(2)}) %collective-permute-start.5) | collective-permute-done | bytes 557088 | tf_op jit(solution)/shard_map/ppermute | solution.py:265
  44.7 4.4 %shard_map.153 = (f32[64,4096]{1,0:T(8,128)S(1)}, bf16[32,4096]{1,0:T(8,128)(2,1)S(1)}, bf16[32,4096]{1,0:T(8,128)(2,1)S(1)}) custom-call(f32[8,136,128]{2,1,0:T(8,128)S(1)} %get-tuple-element.16.kept, f32[8,136,128]{2,1,0:T(8,128)S(1)} %collective-permute-done.5.came, bf16[512,4096]{1,0:T(8,128)(2,1)S(1)} %copy-done, ...), custom_call_target="tpu_custom_call" | custom-call | flops 1073741824 | bytes 8388608 | tf_op jit(solution)/shard_map/pallas_call | solution.py:365
  49.2 1.6 %collective-permute-start.7 = (bf16[32,4096]{1,0:T(8,128)(2,1)S(1)}, bf16[32,4096]{1,0:T(8,128)(2,1)S(1)}, u32[]{:S(2)}, u32[]{:S(2)}) collective-permute-start(bf16[32,4096]{1,0:T(8,128)(2,1)S(1)} %get-tuple-element.19), channel_id=1, source_target_pairs={{0,2},{1,3},{2,0},{3,1},{4,6},{5,7},{6,4},{7,5},{8,10},{9,11},{10,... | collective-permute-start | bytes 786440 | tf_op jit(solution)/shard_map/ppermute | solution.py:265
  51.4 7.0 %collective-permute-done.7.refs_0_ = bf16[32,4096]{1,0:T(8,128)(2,1)S(1)} collective-permute-done((bf16[32,4096]{1,0:T(8,128)(2,1)S(1)}, bf16[32,4096]{1,0:T(8,128)(2,1)S(1)}, u32[]{:S(2)}, u32[]{:S(2)}) %collective-permute-start.7) | collective-permute-done | bytes 262176 | tf_op jit(solution)/shard_map/ppermute | solution.py:265
  58.7 20.6 %collective-permute-start.9 = (bf16[32,4224]{1,0:T(8,128)(2,1)S(1)}, bf16[32,4224]{1,0:T(8,128)(2,1)S(1)}, u32[]{:S(2)}, u32[]{:S(2)}) collective-permute-start(bf16[32,4224]{1,0:T(8,128)(2,1)S(1)} %shard_map.154.refs_7_), channel_id=1, source_target_pairs={{0,4},{4,12},{8,0},{12,20},{16,8},{20,28},{24,16},{28,24},{1,5},{5... | collective-permute-start | bytes 811016 | tf_op jit(solution)/shard_map/ppermute | solution.py:265
  79.6 4.5 %collective-permute-start.20 = (bf16[32,4224]{1,0:T(8,128)(2,1)S(1)}, bf16[32,4224]{1,0:T(8,128)(2,1)S(1)}, u32[]{:S(2)}, u32[]{:S(2)}) collective-permute-start(bf16[32,4224]{1,0:T(8,128)(2,1)S(1)} %shard_map.155.refs_0_), channel_id=1, source_target_pairs={{0,4},{4,12},{8,0},{12,20},{16,8},{20,28},{24,16},{28,24},{1,5},{5... | collective-permute-start | bytes 811016 | tf_op jit(solution)/shard_map/ppermute | solution.py:265
  84.5 2.0 %collective-permute-start.11 = (bf16[32,4224]{1,0:T(8,128)(2,1)S(1)}, bf16[32,4224]{1,0:T(8,128)(2,1)S(1)}, u32[]{:S(2)}, u32[]{:S(2)}) collective-permute-start(bf16[32,4224]{1,0:T(8,128)(2,1)S(1)} %collective-permute-done.9.refs_1_), channel_id=1, source_target_pairs={{0,4},{4,12},{8,0},{12,20},{16,8},{20,28},{24,16},{28,24},{1,5},{5... | collective-permute-start | bytes 811016 | tf_op jit(solution)/shard_map/ppermute | solution.py:265
  86.5 4.9 %collective-permute-done.15.refs_1_ = bf16[32,4224]{1,0:T(8,128)(2,1)S(1)} collective-permute-done((bf16[32,4224]{1,0:T(8,128)(2,1)S(1)}, bf16[32,4224]{1,0:T(8,128)(2,1)S(1)}, u32[]{:S(2)}, u32[]{:S(2)}) %collective-permute-start.15) | collective-permute-done | bytes 270368 | tf_op jit(solution)/shard_map/ppermute | solution.py:265
  91.4 2.1 %collective-permute-start.21 = (bf16[32,4224]{1,0:T(8,128)(2,1)S(1)}, bf16[32,4224]{1,0:T(8,128)(2,1)S(1)}, u32[]{:S(2)}, u32[]{:S(2)}) collective-permute-start(bf16[32,4224]{1,0:T(8,128)(2,1)S(1)} %collective-permute-done.20.refs_2_), channel_id=1, source_target_pairs={{0,4},{4,12},{8,0},{12,20},{16,8},{20,28},{24,16},{28,24},{1,5},{5... | collective-permute-start | bytes 811016 | tf_op jit(solution)/shard_map/ppermute | solution.py:265
  93.5 3.7 %collective-permute-done.10.refs_2_ = bf16[32,4224]{1,0:T(8,128)(2,1)S(1)} collective-permute-done((bf16[32,4224]{1,0:T(8,128)(2,1)S(1)}, bf16[32,4224]{1,0:T(8,128)(2,1)S(1)}, u32[]{:S(2)}, u32[]{:S(2)}) %collective-permute-start.10) | collective-permute-done | bytes 270368 | tf_op jit(solution)/shard_map/ppermute | solution.py:265
  97.2 2.1 %collective-permute-start.13 = (bf16[32,4224]{1,0:T(8,128)(2,1)S(1)}, bf16[32,4224]{1,0:T(8,128)(2,1)S(1)}, u32[]{:S(2)}, u32[]{:S(2)}) collective-permute-start(bf16[32,4224]{1,0:T(8,128)(2,1)S(1)} %collective-permute-done.11.refs_3_), channel_id=1, source_target_pairs={{0,4},{4,12},{8,0},{12,20},{16,8},{20,28},{24,16},{28,24},{1,5},{5... | collective-permute-start | bytes 811016 | tf_op jit(solution)/shard_map/ppermute | solution.py:265
  99.3 3.7 %collective-permute-done.16.refs_3_ = bf16[32,4224]{1,0:T(8,128)(2,1)S(1)} collective-permute-done((bf16[32,4224]{1,0:T(8,128)(2,1)S(1)}, bf16[32,4224]{1,0:T(8,128)(2,1)S(1)}, u32[]{:S(2)}, u32[]{:S(2)}) %collective-permute-start.16) | collective-permute-done | bytes 270368 | tf_op jit(solution)/shard_map/ppermute | solution.py:265
  103.0 2.1 %collective-permute-start.22 = (bf16[32,4224]{1,0:T(8,128)(2,1)S(1)}, bf16[32,4224]{1,0:T(8,128)(2,1)S(1)}, u32[]{:S(2)}, u32[]{:S(2)}) collective-permute-start(bf16[32,4224]{1,0:T(8,128)(2,1)S(1)} %collective-permute-done.21.refs_4_), channel_id=1, source_target_pairs={{0,4},{4,12},{8,0},{12,20},{16,8},{20,28},{24,16},{28,24},{1,5},{5... | collective-permute-start | bytes 811016 | tf_op jit(solution)/shard_map/ppermute | solution.py:265
  105.1 3.7 %collective-permute-done.12.refs_4_ = bf16[32,4224]{1,0:T(8,128)(2,1)S(1)} collective-permute-done((bf16[32,4224]{1,0:T(8,128)(2,1)S(1)}, bf16[32,4224]{1,0:T(8,128)(2,1)S(1)}, u32[]{:S(2)}, u32[]{:S(2)}) %collective-permute-start.12) | collective-permute-done | bytes 270368 | tf_op jit(solution)/shard_map/ppermute | solution.py:265
  108.8 2.1 %collective-permute-start.19 = (bf16[32,4224]{1,0:T(8,128)(2,1)S(1)}, bf16[32,4224]{1,0:T(8,128)(2,1)S(1)}, u32[]{:S(2)}, u32[]{:S(2)}) collective-permute-start(bf16[32,4224]{1,0:T(8,128)(2,1)S(1)} %collective-permute-done.13.refs_5_), channel_id=1, source_target_pairs={{0,4},{4,12},{8,0},{12,20},{16,8},{20,28},{24,16},{28,24},{1,5},{5... | collective-permute-start | bytes 811016 | tf_op jit(solution)/shard_map/ppermute | solution.py:265
  110.9 2.4 %collective-permute-done.17.refs_5_ = bf16[32,4224]{1,0:T(8,128)(2,1)S(1)} collective-permute-done((bf16[32,4224]{1,0:T(8,128)(2,1)S(1)}, bf16[32,4224]{1,0:T(8,128)(2,1)S(1)}, u32[]{:S(2)}, u32[]{:S(2)}) %collective-permute-start.17) | collective-permute-done | bytes 270368 | tf_op jit(solution)/shard_map/ppermute | solution.py:265
  113.4 0.9 collective-permute-done.22.refs_6_
  114.2 14.4 %shard_map.156.refs_9_ = f32[8,8,128]{2,1,0:T(8,128)S(1)} custom-call(s32[13]{0:T(128)S(1)} %concatenate.18.sc, bf16[32,4224]{1,0:T(8,128)(2,1)S(1)} %shard_map.155.refs_0_, bf16[32,4224]{1,0:T(8,128)(2,1)S(1)} %collective-permute-done.15.refs_1_, bf16[32,4224]{1,0:T(8,128)(2,1)S(1)} %collective-permute-done.20.refs_2_, ...), custom_call_target="tpu_custom_call" | custom-call | flops 8388608000 | bytes 32768000 | tf_op jit(solution)/shard_map/pallas_call | solution.py:442
  128.6 14.4 %shard_map.157 = f32[8,8,128]{2,1,0:T(8,128)S(1)} custom-call(s32[13]{0:T(128)S(1)} %concatenate.18.sc, bf16[32,4224]{1,0:T(8,128)(2,1)S(1)} %collective-permute-done.8.refs_0_, bf16[32,4224]{1,0:T(8,128)(2,1)S(1)} %collective-permute-done.9.refs_1_, bf16[32,4224]{1,0:T(8,128)(2,1)S(1)} %collective-permute-done.10.refs_2_, ...), custom_call_target="tpu_custom_call" | custom-call | flops 8388608000 | bytes 32768000 | tf_op jit(solution)/shard_map/pallas_call | solution.py:442
  143.0 11.6 %all_to_all.5.pooled = f32[8,8,128]{2,1,0:T(8,128)S(1)} all-to-all(f32[8,8,128]{2,1,0:T(8,128)S(1)} %shard_map.157), channel_id=1, replica_groups=mesh['req'=8,'mp'=4] {'req'}, dimensions={0} | all-to-all | bytes 65536 | tf_op jit(solution)/shard_map/all_to_all | solution.py:464
  (63 shorter events, 5.0 us)
Async XLA Ops:
  0.6 44.1 %collective-permute-start.6 = (bf16[512,4096]{1,0:T(8,128)(2,1)}, bf16[512,4096]{1,0:T(8,128)(2,1)}, u32[]{:S(2)}, u32[]{:S(2)}) collective-permute-start(bf16[512,4096]{1,0:T(8,128)(2,1)} %mine.1), channel_id=1, source_target_pairs={{0,1},{1,0},{2,3},{3,2},{4,5},{5,4},{6,7},{7,6},{8,9},{9,8},{10,11... | collective-permute-start | bytes 12582920 | tf_op jit(solution)/shard_map/ppermute | solution.py:265
  4.3 7.0 %copy-start.3 = (bf16[256,512]{1,0:T(8,128)(2,1)S(1)}, bf16[256,512]{1,0:T(8,128)(2,1)}, u32[]{:S(2)}) copy-start(bf16[256,512]{1,0:T(8,128)(2,1)} %param.15) | copy-start | bytes 786436
  4.3 7.3 %copy-start.7 = (s32[8]{0:T(128)S(1)}, s32[8]{0:T(128)}, u32[]{:S(2)}) copy-start(s32[8]{0:T(128)} %constant.183.clone) | copy-start | bytes 100
  4.3 8.7 %copy-start.4 = (bf16[256,2,128]{2,1,0:T(2,128)(2,1)S(1)}, bf16[256,2,128]{2,1,0:T(2,128)(2,1)}, u32[]{:S(2)}) copy-start(bf16[256,2,128]{2,1,0:T(2,128)(2,1)} %param.17) | copy-start | bytes 393220
  4.3 8.7 %copy-start.5 = (bf16[256,2,128]{2,1,0:T(2,128)(2,1)S(1)}, bf16[256,2,128]{2,1,0:T(2,128)(2,1)}, u32[]{:S(2)}) copy-start(bf16[256,2,128]{2,1,0:T(2,128)(2,1)} %param.16) | copy-start | bytes 393220
  5.3 16.6 %collective-permute-start.1 = (bf16[2064,128]{1,0:T(8,128)(2,1)S(1)}, bf16[2064,128]{1,0:T(8,128)(2,1)S(1)}, u32[]{:S(2)}, u32[]{:S(2)}) collective-permute-start(bf16[2064,128]{1,0:T(8,128)(2,1)S(1)} %pad_maximum_fusion.kv), channel_id=1, source_target_pairs={{0,24},{4,28},{8,0},{12,4},{16,8},{20,12},{24,16},{28,20},{1,25},{... | collective-permute-start | bytes 1585160 | tf_op jit(solution)/shard_map/ppermute | solution.py:265
  10.0 17.8 %collective-permute-start.3 = (bf16[2064,128]{1,0:T(8,128)(2,1)S(1)}, bf16[2064,128]{1,0:T(8,128)(2,1)S(1)}, u32[]{:S(2)}, u32[]{:S(2)}) collective-permute-start(bf16[2064,128]{1,0:T(8,128)(2,1)S(1)} %pad_maximum_fusion.kv), channel_id=1, source_target_pairs={{4,0},{12,8},{20,16},{28,24},{5,1},{13,9},{21,17},{29,25},{6,2},{1... | collective-permute-start | bytes 1585160 | tf_op jit(solution)/shard_map/ppermute | solution.py:265
  11.3 2.8 %collective-permute-start = (bf16[256,512]{1,0:T(8,128)(2,1)S(1)}, bf16[256,512]{1,0:T(8,128)(2,1)S(1)}, u32[]{:S(2)}, u32[]{:S(2)}) collective-permute-start(bf16[256,512]{1,0:T(8,128)(2,1)S(1)} %copy-done.3), channel_id=1, source_target_pairs={{0,1},{1,0},{2,3},{3,2},{4,5},{5,4},{6,7},{7,6},{8,9},{9,8},{10,11... | collective-permute-start | bytes 786440 | tf_op jit(solution)/shard_map/ppermute | solution.py:265
  21.9 18.5 %collective-permute-start.2 = (bf16[2064,128]{1,0:T(8,128)(2,1)S(1)}, bf16[2064,128]{1,0:T(8,128)(2,1)S(1)}, u32[]{:S(2)}, u32[]{:S(2)}) collective-permute-start(bf16[2064,128]{1,0:T(8,128)(2,1)S(1)} %collective-permute-done.1.refs_1_), channel_id=1, source_target_pairs={{0,4},{4,0},{8,12},{12,8},{16,20},{20,16},{24,28},{28,24},{1,5},{5... | collective-permute-start | bytes 1585160 | tf_op jit(solution)/shard_map/ppermute | solution.py:265
  40.4 1.4 collective-permute-start.4
  41.0 3.7 %copy-start = (bf16[512,4096]{1,0:T(8,128)(2,1)S(1)}, bf16[512,4096]{1,0:T(8,128)(2,1)}, u32[]{:S(2)}) copy-start(bf16[512,4096]{1,0:T(8,128)(2,1)} %mine.1) | copy-start | bytes 12582916
  42.7 2.0 %collective-permute-start.5 = (f32[8,136,128]{2,1,0:T(8,128)S(1)}, f32[8,136,128]{2,1,0:T(8,128)S(1)}, u32[]{:S(2)}, u32[]{:S(2)}) collective-permute-start(f32[8,136,128]{2,1,0:T(8,128)S(1)} %get-tuple-element.17), channel_id=1, source_target_pairs={{0,1},{1,0},{2,3},{3,2},{4,5},{5,4},{6,7},{7,6},{8,9},{9,8},{10,11... | collective-permute-start | bytes 1671176 | tf_op jit(solution)/shard_map/ppermute | solution.py:265
  44.7 6.6 %copy-start.6 = (s32[64]{0:T(128)S(1)}, s32[64]{0:T(128)}, u32[]{:S(2)}) copy-start(s32[64]{0:T(128)} %param.23) | copy-start | bytes 772
  44.7 13.7 %copy-start.1 = (bf16[64,4096]{1,0:T(8,128)(2,1)S(1)}, bf16[64,4096]{1,0:T(8,128)(2,1)}, u32[]{:S(2)}) copy-start(bf16[64,4096]{1,0:T(8,128)(2,1)} %hidden.3) | copy-start | bytes 1572868
  44.7 13.7 %copy-start.2 = (f32[4096]{0:T(1024)S(1)}, f32[4096]{0:T(1024)}, u32[]{:S(2)}) copy-start(f32[4096]{0:T(1024)} %param.21) | copy-start | bytes 49156
  49.2 9.2 %collective-permute-start.7 = (bf16[32,4096]{1,0:T(8,128)(2,1)S(1)}, bf16[32,4096]{1,0:T(8,128)(2,1)S(1)}, u32[]{:S(2)}, u32[]{:S(2)}) collective-permute-start(bf16[32,4096]{1,0:T(8,128)(2,1)S(1)} %get-tuple-element.19), channel_id=1, source_target_pairs={{0,2},{1,3},{2,0},{3,1},{4,6},{5,7},{6,4},{7,5},{8,10},{9,11},{10,... | collective-permute-start | bytes 786440 | tf_op jit(solution)/shard_map/ppermute | solution.py:265
  50.8 28.5 %collective-permute-start.14 = (bf16[32,4096]{1,0:T(8,128)(2,1)S(1)}, bf16[32,4096]{1,0:T(8,128)(2,1)S(1)}, u32[]{:S(2)}, u32[]{:S(2)}) collective-permute-start(bf16[32,4096]{1,0:T(8,128)(2,1)S(1)} %get-tuple-element.20), channel_id=1, source_target_pairs={{0,2},{1,3},{2,0},{3,1},{4,6},{5,7},{6,4},{7,5},{8,10},{9,11},{10,... | collective-permute-start | bytes 786440 | tf_op jit(solution)/shard_map/ppermute | solution.py:265
  58.6 25.9 %collective-permute-start.8 = (bf16[32,4224]{1,0:T(8,128)(2,1)S(1)}, bf16[32,4224]{1,0:T(8,128)(2,1)S(1)}, u32[]{:S(2)}, u32[]{:S(2)}) collective-permute-start(bf16[32,4224]{1,0:T(8,128)(2,1)S(1)} %shard_map.154.refs_7_), channel_id=1, source_target_pairs={{0,8},{4,0},{8,16},{12,4},{16,24},{20,12},{24,28},{28,20},{1,9},{5... | collective-permute-start | bytes 811016 | tf_op jit(solution)/shard_map/ppermute | solution.py:265
  58.7 25.8 %collective-permute-start.9 = (bf16[32,4224]{1,0:T(8,128)(2,1)S(1)}, bf16[32,4224]{1,0:T(8,128)(2,1)S(1)}, u32[]{:S(2)}, u32[]{:S(2)}) collective-permute-start(bf16[32,4224]{1,0:T(8,128)(2,1)S(1)} %shard_map.154.refs_7_), channel_id=1, source_target_pairs={{0,4},{4,12},{8,0},{12,20},{16,8},{20,28},{24,16},{28,24},{1,5},{5... | collective-permute-start | bytes 811016 | tf_op jit(solution)/shard_map/ppermute | solution.py:265
  79.5 11.9 %collective-permute-start.15 = (bf16[32,4224]{1,0:T(8,128)(2,1)S(1)}, bf16[32,4224]{1,0:T(8,128)(2,1)S(1)}, u32[]{:S(2)}, u32[]{:S(2)}) collective-permute-start(bf16[32,4224]{1,0:T(8,128)(2,1)S(1)} %shard_map.155.refs_0_), channel_id=1, source_target_pairs={{0,8},{4,0},{8,16},{12,4},{16,24},{20,12},{24,28},{28,20},{1,9},{5... | collective-permute-start | bytes 811016 | tf_op jit(solution)/shard_map/ppermute | solution.py:265
  79.6 11.8 %collective-permute-start.20 = (bf16[32,4224]{1,0:T(8,128)(2,1)S(1)}, bf16[32,4224]{1,0:T(8,128)(2,1)S(1)}, u32[]{:S(2)}, u32[]{:S(2)}) collective-permute-start(bf16[32,4224]{1,0:T(8,128)(2,1)S(1)} %shard_map.155.refs_0_), channel_id=1, source_target_pairs={{0,4},{4,12},{8,0},{12,20},{16,8},{20,28},{24,16},{28,24},{1,5},{5... | collective-permute-start | bytes 811016 | tf_op jit(solution)/shard_map/ppermute | solution.py:265
  84.5 12.7 %collective-permute-start.10 = (bf16[32,4224]{1,0:T(8,128)(2,1)S(1)}, bf16[32,4224]{1,0:T(8,128)(2,1)S(1)}, u32[]{:S(2)}, u32[]{:S(2)}) collective-permute-start(bf16[32,4224]{1,0:T(8,128)(2,1)S(1)} %collective-permute-done.8.refs_0_), channel_id=1, source_target_pairs={{0,8},{4,0},{8,16},{12,4},{16,24},{20,12},{24,28},{28,20},{1,9},{5... | collective-permute-start | bytes 811016 | tf_op jit(solution)/shard_map/ppermute | solution.py:265
  84.5 12.7 %collective-permute-start.11 = (bf16[32,4224]{1,0:T(8,128)(2,1)S(1)}, bf16[32,4224]{1,0:T(8,128)(2,1)S(1)}, u32[]{:S(2)}, u32[]{:S(2)}) collective-permute-start(bf16[32,4224]{1,0:T(8,128)(2,1)S(1)} %collective-permute-done.9.refs_1_), channel_id=1, source_target_pairs={{0,4},{4,12},{8,0},{12,20},{16,8},{20,28},{24,16},{28,24},{1,5},{5... | collective-permute-start | bytes 811016 | tf_op jit(solution)/shard_map/ppermute | solution.py:265
  91.4 11.6 %collective-permute-start.16 = (bf16[32,4224]{1,0:T(8,128)(2,1)S(1)}, bf16[32,4224]{1,0:T(8,128)(2,1)S(1)}, u32[]{:S(2)}, u32[]{:S(2)}) collective-permute-start(bf16[32,4224]{1,0:T(8,128)(2,1)S(1)} %collective-permute-done.15.refs_1_), channel_id=1, source_target_pairs={{0,8},{4,0},{8,16},{12,4},{16,24},{20,12},{24,28},{28,20},{1,9},{5... | collective-permute-start | bytes 811016 | tf_op jit(solution)/shard_map/ppermute | solution.py:265
  91.4 11.6 %collective-permute-start.21 = (bf16[32,4224]{1,0:T(8,128)(2,1)S(1)}, bf16[32,4224]{1,0:T(8,128)(2,1)S(1)}, u32[]{:S(2)}, u32[]{:S(2)}) collective-permute-start(bf16[32,4224]{1,0:T(8,128)(2,1)S(1)} %collective-permute-done.20.refs_2_), channel_id=1, source_target_pairs={{0,4},{4,12},{8,0},{12,20},{16,8},{20,28},{24,16},{28,24},{1,5},{5... | collective-permute-start | bytes 811016 | tf_op jit(solution)/shard_map/ppermute | solution.py:265
  97.2 11.6 %collective-permute-start.12 = (bf16[32,4224]{1,0:T(8,128)(2,1)S(1)}, bf16[32,4224]{1,0:T(8,128)(2,1)S(1)}, u32[]{:S(2)}, u32[]{:S(2)}) collective-permute-start(bf16[32,4224]{1,0:T(8,128)(2,1)S(1)} %collective-permute-done.10.refs_2_), channel_id=1, source_target_pairs={{0,8},{4,0},{8,16},{12,4},{16,24},{20,12},{24,28},{28,20},{1,9},{5... | collective-permute-start | bytes 811016 | tf_op jit(solution)/shard_map/ppermute | solution.py:265
  97.2 11.6 %collective-permute-start.13 = (bf16[32,4224]{1,0:T(8,128)(2,1)S(1)}, bf16[32,4224]{1,0:T(8,128)(2,1)S(1)}, u32[]{:S(2)}, u32[]{:S(2)}) collective-permute-start(bf16[32,4224]{1,0:T(8,128)(2,1)S(1)} %collective-permute-done.11.refs_3_), channel_id=1, source_target_pairs={{0,4},{4,12},{8,0},{12,20},{16,8},{20,28},{24,16},{28,24},{1,5},{5... | collective-permute-start | bytes 811016 | tf_op jit(solution)/shard_map/ppermute | solution.py:265
  103.0 10.3 %collective-permute-start.17 = (bf16[32,4224]{1,0:T(8,128)(2,1)S(1)}, bf16[32,4224]{1,0:T(8,128)(2,1)S(1)}, u32[]{:S(2)}, u32[]{:S(2)}) collective-permute-start(bf16[32,4224]{1,0:T(8,128)(2,1)S(1)} %collective-permute-done.16.refs_3_), channel_id=1, source_target_pairs={{0,8},{4,0},{8,16},{12,4},{16,24},{20,12},{24,28},{28,20},{1,9},{5... | collective-permute-start | bytes 811016 | tf_op jit(solution)/shard_map/ppermute | solution.py:265
  103.0 11.2 %collective-permute-start.22 = (bf16[32,4224]{1,0:T(8,128)(2,1)S(1)}, bf16[32,4224]{1,0:T(8,128)(2,1)S(1)}, u32[]{:S(2)}, u32[]{:S(2)}) collective-permute-start(bf16[32,4224]{1,0:T(8,128)(2,1)S(1)} %collective-permute-done.21.refs_4_), channel_id=1, source_target_pairs={{0,4},{4,12},{8,0},{12,20},{16,8},{20,28},{24,16},{28,24},{1,5},{5... | collective-permute-start | bytes 811016 | tf_op jit(solution)/shard_map/ppermute | solution.py:265
  108.8 19.8 %collective-permute-start.19 = (bf16[32,4224]{1,0:T(8,128)(2,1)S(1)}, bf16[32,4224]{1,0:T(8,128)(2,1)S(1)}, u32[]{:S(2)}, u32[]{:S(2)}) collective-permute-start(bf16[32,4224]{1,0:T(8,128)(2,1)S(1)} %collective-permute-done.13.refs_5_), channel_id=1, source_target_pairs={{0,4},{4,12},{8,0},{12,20},{16,8},{20,28},{24,16},{28,24},{1,5},{5... | collective-permute-start | bytes 811016 | tf_op jit(solution)/shard_map/ppermute | solution.py:265
  113.4 15.2 %collective-permute-start.18 = (bf16[32,4224]{1,0:T(8,128)(2,1)S(1)}, bf16[32,4224]{1,0:T(8,128)(2,1)S(1)}, u32[]{:S(2)}, u32[]{:S(2)}) collective-permute-start(bf16[32,4224]{1,0:T(8,128)(2,1)S(1)} %collective-permute-done.17.refs_5_), channel_id=1, source_target_pairs={{0,8},{4,0},{8,16},{12,4},{16,24},{20,12},{24,28},{28,20},{1,9},{5... | collective-permute-start | bytes 811016 | tf_op jit(solution)/shard_map/ppermute | solution.py:265

commit v3 on v2

--- a/solution.py
+++ b/solution.py
@@ -13,6 +13,7 @@
 META = 16
 STATE = 8
 FACTS = 5
+PARTS = 2
 MIB = 1 << 20
 
 
@@ -39,24 +40,28 @@
     state[head, size : size + STATE, :] = jnp.where(rows == 0, top, total)
 
 
-def attend_slab(core, want, kv, query, state, size, scale):
+def attend_slab(core, want, part, kv, query, state, size, scale):
     half = (kv.shape[0] - META) // 2
     heads = query.shape[1] // size
     meta = kv[2 * half : 2 * half + META, :].astype(jnp.float32)
     offset = jnp.max(meta[0:1, :]).astype(jnp.int32)
     length = jnp.max(meta[1:2, :] * 256.0 + meta[2:3, :]).astype(jnp.int32)
-    blocks = jnp.clip((length - core * BLOCK + 2 * BLOCK - 1) // (2 * BLOCK), 0, half // BLOCK)
-    blocks = jnp.where(offset == want, blocks, 0)
+    begin = part * half
+    blocks = (length - core * BLOCK + 2 * BLOCK - 1) // (2 * BLOCK)
+    blocks = jnp.clip(blocks - begin // BLOCK, 0, half // BLOCK)
+    blocks = jnp.where(offset == want, (blocks + 1) // 2, 0)
+    wide = 2 * BLOCK
 
     def step(j, carry):
-        start = pl.multiple_of(j * BLOCK, BLOCK)
-        keys = kv[pl.ds(start, BLOCK), :]
-        values = kv[pl.ds(half + start, BLOCK), :]
-        place = lax.broadcasted_iota(jnp.int32, (BLOCK, 1), 0) + (2 * j + core) * BLOCK
-        valid = place < length
+        start = pl.multiple_of(j * wide, wide)
+        keys = kv[pl.ds(start, wide), :]
+        values = kv[pl.ds(half + start, wide), :]
+        local = lax.broadcasted_iota(jnp.int32, (wide, 1), 0) + (start + begin)
+        place = (local // BLOCK) * (2 * BLOCK) + core * BLOCK + local % BLOCK
+        bias = jnp.where(place < length, 0.0, NEGATIVE)
+        products = [nt(keys, query[:, h * size : (h + 1) * size]) for h in range(heads)]
         for h in range(heads):
-            scores = nt(keys, query[:, h * size : (h + 1) * size]) * scale
-            scores = jnp.where(valid, scores, NEGATIVE)
+            scores = products[h] * scale + bias
             before = state[h, size : size + 1, :]
             top = jnp.maximum(before, jnp.max(scores, axis=0, keepdims=True))
             old = jnp.exp2(before - top)
@@ -69,19 +74,22 @@
     lax.fori_loop(0, blocks, step, 0)
 
 
-def first_kernel(sc, times, query, keys, values, kv, state, *, size, scale):
+def first_kernel(sc, times, query, keys, values, *refs, size, scale):
+    kvs, state = refs[:-1], refs[-1]
     core = sc[0]
     here = keys.shape[0]
     place = lax.broadcasted_iota(jnp.int32, (here, 1), 0) + core * here
     valid = place <= times[...]
-    for h in range(query.shape[1] // size):
-        scores = nt(keys[...], query[:, h * size : (h + 1) * size]) * scale
-        scores = jnp.where(valid, scores, NEGATIVE)
+    heads = query.shape[1] // size
+    products = [nt(keys[...], query[:, h * size : (h + 1) * size]) for h in range(heads)]
+    for h in range(heads):
+        scores = jnp.where(valid, products[h] * scale, NEGATIVE)
         top = jnp.max(scores, axis=0, keepdims=True)
         weights = jnp.exp2(scores - top)
         state[h, :size, :] = tn(values[...], weights.astype(jnp.bfloat16))
         put_state(state, h, size, top, jnp.sum(weights, axis=0, keepdims=True))
-    attend_slab(core, 0, kv, query, state, size, scale)
+    for part, kv in enumerate(kvs):
+        attend_slab(core, 0, part, kv, query, state, size, scale)
 
 
 def more_kernel(sc, query, *refs, size, scale, wants, split):
@@ -93,7 +101,8 @@
         state = outs[0]
     state[...] = given[...]
     for i, kv in enumerate(kvs):
-        attend_slab(sc[0], sc[1] if wants[i] is None else wants[i], kv, query, state, size, scale)
+        want = sc[1] if wants[i] is None else wants[i]
+        attend_slab(sc[0], want, i % PARTS, kv, query, state, size, scale)
     if split:
         middle = state.shape[2] // 2
         outs[0][...] = state[:, :, :middle]
@@ -138,7 +147,7 @@
     out[:, width:] = code.astype(jnp.float32).astype(jnp.bfloat16)
 
 
-def head_kernel(sc, *refs, block, homes, given):
+def head_kernel(sc, *refs, block, homes, given, finish):
     parts, weight = refs[: len(homes)], refs[len(homes)]
     table, rows, codes, slots, sems = refs[-5:]
     width = weight.shape[1]
@@ -185,28 +194,39 @@
     line = lax.broadcasted_iota(jnp.int32, (STATE, count), 0)
     value = jnp.where(line == 0, top, jnp.where(line == 1, total, weighted))
     value = jnp.where(line == 3, picked, value)
-    if given:
-        table[...] = refs[len(homes) + 1][...]
-    else:
-        table[...] = jnp.zeros_like(table)
+    held = jnp.zeros(table.shape, jnp.float32) if not given else refs[len(homes) + 1][...]
+    table[...] = held
     for i, (name, side) in enumerate(homes):
         piece = value[:, i * deep : (i + 1) * deep]
         table[sc[FACTS + name], :, side * deep : (side + 1) * deep] = piece
-
-
-def final_kernel(sc, pooled, out):
-    tops = pooled[:, 0:1, :]
-    highest = jnp.max(tops, axis=0)
-    scales = jnp.exp(tops - highest[None])
-    total = jnp.sum(pooled[:, 1:2, :] * scales, axis=0)
-    weighted = jnp.sum(pooled[:, 2:3, :] * scales, axis=0)
-    picked = jnp.sum(pooled[:, 3:4, :], axis=0)
-    log_total = highest + jnp.log(total)
-    place = lax.broadcasted_iota(jnp.int32, (1, pooled.shape[2]), 1) + sc[3]
+    if finish:
+        low, high = refs[-7:-5]
+        low[...] = table[: low.shape[0]]
+        high[...] = table[low.shape[0] :]
+
+
+def joined(mine, other):
+    highest = jnp.maximum(mine[:, 0:1, :], other[:, 0:1, :])
+    left, right = jnp.exp(mine[:, 0:1, :] - highest), jnp.exp(other[:, 0:1, :] - highest)
+    line = lax.broadcasted_iota(jnp.int32, mine.shape, 1)
+    scaled = mine * left + other * right
+    return jnp.where(line == 0, highest, jnp.where(line == 3, mine + other, scaled))
+
+
+def join_kernel(mine, other, low, high):
+    both = joined(mine[...], other[...])
+    low[...] = both[: low.shape[0]]
+    high[...] = both[low.shape[0] :]
+
+
+def final_kernel(sc, mine, other, logprob, entropy):
+    both = joined(mine[...], other[...])[0]
+    log_total = both[0:1] + jnp.log(both[1:2])
+    place = lax.broadcasted_iota(jnp.int32, (1, both.shape[1]), 1) + sc[3]
     valid = place < sc[4]
-    line = lax.broadcasted_iota(jnp.int32, (STATE, pooled.shape[2]), 0)
-    value = jnp.where(line == 0, picked - log_total, log_total - weighted / total)
-    out[...] = jnp.where(valid, value, 0.0)
+    count = logprob.shape[1]
+    logprob[...] = jnp.where(valid, both[3:4] - log_total, 0.0)[:, :count]
+    entropy[...] = jnp.where(valid, log_total - both[2:3] / both[1:2], 0.0)[:, :count]
 
 
 def smem():
@@ -276,11 +296,20 @@
     numbers = jnp.where(
         line == 0, piece_offset[0], jnp.where(line == 1, piece_len[0] // 256, piece_len[0] % 256)
     )
-    kv = jnp.concatenate(
-        [half_of(cached_key_slabs), half_of(cached_value_slabs), numbers.astype(jnp.bfloat16)]
-    )
-    two = over(kv, "req", lambda i: (i - 2) % groups)
-    one = over(kv, "req", lambda i: i - 1 if i % 2 else None)
+    all_keys, all_values = half_of(cached_key_slabs), half_of(cached_value_slabs)
+    deep = half // PARTS
+    kv = [
+        jnp.concatenate(
+            [
+                all_keys[p * deep : (p + 1) * deep],
+                all_values[p * deep : (p + 1) * deep],
+                numbers.astype(jnp.bfloat16),
+            ]
+        )
+        for p in range(PARTS)
+    ]
+    two = [over(part, "req", lambda i: (i - 2) % groups) for part in kv]
+    one = [over(part, "req", lambda i: i - 1 if i % 2 else None) for part in kv]
     mate_queries = over(queries, "mp", lambda i: i ^ 1)
     mate_weight = over(out_weight, "mp", lambda i: i ^ 1)
 
@@ -289,7 +318,7 @@
     at = jnp.sum(jnp.where(tour == request, jnp.arange(groups, dtype=jnp.int32), 0))
     spots = (at + jnp.arange(groups, dtype=jnp.int32)) % groups
     match = spots[:, None] == jnp.arange(groups, dtype=jnp.int32)[None]
-    homes = jnp.sum(jnp.where(match, tour[None], 0), axis=1)
+    homes = jnp.sum(jnp.where(match, tour[None], 0), axis=1) ^ request
     facts = [core, 3 - 2 * (request % 2), request * vocabulary_here, member * rows_here, rollout_len[0]]
     plan = jnp.concatenate([jnp.stack(facts).astype(jnp.int32), homes])
 
@@ -315,8 +344,8 @@
     state = call(
         functools.partial(first_kernel, size=size, scale=scale),
         full,
-        [smem()] + [vmem()] * 5,
-        16,
+        [smem()] + [vmem()] * (4 + PARTS),
+        32,
         work,
         2 * half * size * 4,
     )(
@@ -325,37 +354,37 @@
         query,
         own_half(rotated_rollout_keys),
         own_half(rollout_value_matrix),
-        kv,
-    )
-    two, state = lax.optimization_barrier((two, state))
-    swap = over(two, "req", lambda i: i ^ 1)
+        *kv,
+    )
+    first_two, state = lax.optimization_barrier((two[0], state))
+    second_two, one = lax.optimization_barrier((two[1:], one))
+    swap = [over(part, "req", lambda i: i ^ 1) for part in (first_two, *second_two)]
+    three = [over(part, "req", lambda i: (i - 2) % groups if i % 2 else None) for part in swap]
     state = call(
-        functools.partial(more_kernel, size=size, scale=scale, wants=(1, 2), split=False),
+        functools.partial(more_kernel, size=size, scale=scale, wants=(1,) * PARTS + (2,) * PARTS, split=False),
         full,
-        [smem()] + [vmem()] * 4,
-        16,
+        [smem()] + [vmem()] * (2 + 2 * PARTS),
+        32,
         2 * work,
         4 * half * size * 4,
-    )(plan, query, one, two, state)
-    swap, state = lax.optimization_barrier((swap, state))
-    three = over(swap, "req", lambda i: (i - 2) % groups if i % 2 else None)
+    )(plan, query, *one, *two, state)
     state = call(
-        functools.partial(more_kernel, size=size, scale=scale, wants=(None,), split=False),
+        functools.partial(more_kernel, size=size, scale=scale, wants=(None,) * PARTS, split=False),
         full,
-        [smem()] + [vmem()] * 3,
-        16,
+        [smem()] + [vmem()] * (2 + PARTS),
+        32,
         work,
         2 * half * size * 4,
-    )(plan, query, swap, state)
+    )(plan, query, *swap, state)
     kept, sent = call(
-        functools.partial(more_kernel, size=size, scale=scale, wants=(3,), split=True),
+        functools.partial(more_kernel, size=size, scale=scale, wants=(3,) * PARTS, split=True),
         (part, part),
-        [smem()] + [vmem()] * 3,
-        16,
+        [smem()] + [vmem()] * (2 + PARTS),
+        32,
         work,
         2 * half * size * 4,
         scratch_shapes=[pltpu.VMEM(full.shape, jnp.float32)],
-    )(plan, query, three, state)
+    )(plan, query, *three, state)
     came = over(sent, "mp", lambda i: i ^ 1)
 
     tile = 1024
@@ -435,18 +464,21 @@
     batch = max(1, 256 // deep)
     depth = 4
     table = None
+    whole, halves = shape((groups, STATE, 128)), shape((groups // 2, STATE, 128))
     for at in range(0, len(arrived), batch):
         now = arrived[at : at + batch]
         count = deep * len(now)
         given = [] if table is None else [table]
+        done = at + batch >= len(arrived)
         table = call(
             functools.partial(
                 head_kernel,
                 block=block,
                 homes=[(name, side) for name, side, _ in now],
                 given=len(given),
+                finish=done,
             ),
-            shape((groups, STATE, 128)),
+            (halves, halves) if done else whole,
             [smem()]
             + [vmem()] * len(now)
             + [pl.BlockSpec(memory_space=pl.ANY)]
@@ -454,16 +486,27 @@
             44,
             2 * count * width * vocabulary_here,
             2 * width * vocabulary_here,
-            scratch_shapes=[
+            scratch_shapes=[pltpu.VMEM(whole.shape, jnp.float32)] * done
+            + [
                 pltpu.VMEM((count, width), jnp.bfloat16),
                 pltpu.VMEM((count, size), jnp.float32),
                 pltpu.VMEM((depth, block, width), jnp.bfloat16),
                 pltpu.SemaphoreType.DMA((depth,)),
             ],
         )(plan, *[rows for _, _, rows in now], weight, *given)
-    pooled = lax.all_to_all(table, "req", 0, 0)
-    out = call(final_kernel, shape((STATE, 128)), [smem(), vmem()], 4)(plan, pooled)
-    return (out[0, :rows_here], out[1, :rows_here])
+    mine, away = table
+    bit = groups // 2
+    while bit > 1:
+        other = over(away, "req", lambda i, bit=bit: i ^ bit)
+        bit //= 2
+        part = shape((bit, STATE, 128))
+        mine, away = call(join_kernel, (part, part), [vmem()] * 2, 4)(mine, other)
+    other = over(away, "req", lambda i: i ^ 1)
+    rows_out = shape((1, rows_here))
+    logprob, entropy = call(final_kernel, (rows_out, rows_out), [smem()] + [vmem()] * 2, 4)(
+        plan, mine, other
+    )
+    return (logprob.reshape(rows_here), entropy.reshape(rows_here))
 
 
 def solution(mesh):

time: 157 us -> 147 us (0.936)
  blocking collectives: 11.6 us -> 0 us
  waiting for transfers between devices: 44.4 us -> 51.5 us
  starting transfers between devices: 51.1 us -> 44.1 us
  Pallas kernels: 40.3 us -> 42.8 us
    all_to_all x1 -> x0, blocking collectives: 11.6 us -> none  [body(): pooled = lax.all_to_all(table, 'req', 0, 0)]
    ppermute x23 -> x30, waiting for transfers between devices: 44.4 us -> 51.5 us  [over(): return lax.ppermute(block, axis, pairs)]
    ppermute x23 -> x30, starting transfers between devices: 51.1 us -> 44.1 us  [over(): return lax.ppermute(block, axis, pairs)]
    dynamic_slice x1 -> x0, local copies, waits for them, and re-layouts: 2.38 us -> none  [half_of(): lax.dynamic_index_in_dim(cut, value_head, 2, keepdims=False)]
    slice x0 -> x1, local copies, waits for them, and re-layouts: none -> 2.37 us  [body(): all_values[p * deep:(p + 1) * deep]]
    pallas_call x1, Pallas kernels: 1.37 us -> 3.23 us  [body(): call(functools.partial(first_kernel, size=size, scale=scale), full, [smem...]
    pallas_call x3 -> x5, Pallas kernels: 4.68 us -> 5.12 us  [the longest x1 3.12 us: body(): call(functools.partial(more_kernel, size=size, scale=scale, wants=(1,) *...]
  transfers between devices with their start and end apart: 23 -> 30, of which waited for: 11 -> 15; matrix products, arithmetic and copies ran while one was open for 3% -> 3% of each run, Pallas kernels for 13% -> 16%
where the time goes in v3:
time: 147 us; the launch traced here: 146 us
  waiting for transfers between devices  51.5 us (35%)
  starting transfers between devices  44.1 us (30%)
  Pallas kernels  42.8 us (29%)
  between operations  3.11 us (2%)
  local copies, waits for them, and re-layouts  2.87 us (2%)
  other arithmetic  1.73 us (1%)
    ppermute x30, waiting for transfers between devices, over(): return lax.ppermute(block, axis, pairs)  51.5 us
    ppermute x30, starting transfers between devices, over(): return lax.ppermute(block, axis, pairs)  44.1 us
    pallas_call x2, Pallas kernels, body(): call(functools.partial(head_kernel, block=block, homes=[(name, side) for...  28.7 us
    pallas_call x1, Pallas kernels, body(): pl.pallas_call(functools.partial(merge_kernel, size=size, rows=rows_here)...  4.45 us
    pallas_call x1, Pallas kernels, body(): call(functools.partial(first_kernel, size=size, scale=scale), full, [smem...  3.23 us
    pallas_call x1, Pallas kernels, body(): call(functools.partial(more_kernel, size=size, scale=scale, wants=(1,) *...  3.12 us
  transfers between devices with their start and end apart: 30, of which 15 were waited for; matrix products, arithmetic and copies ran while one was open for 3% of the time, Pallas kernels for 16%

profile of v3, /device:TPU:0, one launch (start us, length us, event | category | flops | bytes accessed | tf_op | source)
XLA Modules:
  0.0 146.1 jit_solution(17151705410968052196)
XLA Ops:
  1.9 2.4 %constant_dynamic-slice_fusion.4 = (bf16[2,1,256,1,128]{4,3,2,1,0:T(2,128)(2,1)S(1)}, bf16[2,1,256,1,128]{4,3,2,1,0:T(2,128)(2,1)S(1)}, bf16[2,1,256,1,128]{4,3,...) fusion(bf16[4,2,256,2,128]{4,3,2,1,0:T(2,128)(2,1)} %bitcast.40, s32[]{:T(128)S(6)} %add.129, s32[]{:T(128)S(6)} %select_n.98, ...), kind=kLoop, calls=%fused_computation.12 | loop fusion | bytes 1048588 | tf_op jit(solution)/shard_map/slice | solution.py:305
  5.2 4.8 %collective-permute-start.4 = (bf16[1040,128]{1,0:T(8,128)(2,1)S(1)}, bf16[1040,128]{1,0:T(8,128)(2,1)S(1)}, u32[]{:S(2)}, u32[]{:S(2)}) collective-permute-start(bf16[1040,128]{1,0:T(8,128)(2,1)S(1)} %get-tuple-element.52.refs_1_), channel_id=1, source_target_pairs={{0,24},{4,28},{8,0},{12,4},{16,8},{20,12},{24,16},{28,20},{1,25},{... | collective-permute-start | bytes 798728 | tf_op jit(solution)/shard_map/ppermute | solution.py:285
  10.0 1.3 collective-permute-start.6
  11.3 1.3 collective-permute-start.5
  15.9 3.2 %shard_map.149.refs_4_ = f32[8,136,256]{2,1,0:T(8,128)S(1)} custom-call(s32[13]{0:T(128)S(1)} %concatenate.21.sc, s32[1,256]{1,0:T(1,128)S(1)} %bitcast.33, bf16[256,1024]{1,0:T(8,128)(2,1)S(1)} %maximum_maximum_fusion.query, bf16[128,128]{1,0:T(8,128)(2,1)S(1)} %bitcast.32, bf16[128,128]{1,0:T(8,128)(2,1)S(1)} %bitcast.31, ...), custom_call_target="tpu_custom_call" | custom-call | flops 1073741824 | bytes 1048576 | tf_op jit(solution)/shard_map/pallas_call | solution.py:344
  19.2 6.8 %collective-permute-done.5.refs_0_ = bf16[1040,128]{1,0:T(8,128)(2,1)S(1)} collective-permute-done((bf16[1040,128]{1,0:T(8,128)(2,1)S(1)}, bf16[1040,128]{1,0:T(8,128)(2,1)S(1)}, u32[]{:S(2)}, u32[]{:S(2)}) %collective-permute-start.5) | collective-permute-done | bytes 266272 | tf_op jit(solution)/shard_map/ppermute | solution.py:285
  28.0 7.3 %collective-permute-done.7.refs_1_ = bf16[1040,128]{1,0:T(8,128)(2,1)S(1)} collective-permute-done((bf16[1040,128]{1,0:T(8,128)(2,1)S(1)}, bf16[1040,128]{1,0:T(8,128)(2,1)S(1)}, u32[]{:S(2)}, u32[]{:S(2)}) %collective-permute-start.7) | collective-permute-done | bytes 266272 | tf_op jit(solution)/shard_map/ppermute | solution.py:285
  36.0 3.2 %collective-permute-done.2.refs_0_ = bf16[1040,128]{1,0:T(8,128)(2,1)S(1)} collective-permute-done((bf16[1040,128]{1,0:T(8,128)(2,1)S(1)}, bf16[1040,128]{1,0:T(8,128)(2,1)S(1)}, u32[]{:S(2)}, u32[]{:S(2)}) %collective-permute-start.2) | collective-permute-done | bytes 266272 | tf_op jit(solution)/shard_map/ppermute | solution.py:285
  39.9 3.1 %shard_map.150.refs_2_ = f32[8,136,256]{2,1,0:T(8,128)S(1)} custom-call(s32[13]{0:T(128)S(1)} %concatenate.21.sc, bf16[256,1024]{1,0:T(8,128)(2,1)S(1)} %maximum_maximum_fusion.query, bf16[1040,128]{1,0:T(8,128)(2,1)S(1)} %collective-permute-done.5.refs_0_, bf16[1040,128]{1,0:T(8,128)(2,1)S(1)} %collective-permute-done.6.refs_1_, ...), custom_call_target="tpu_custom_call" | custom-call | flops 2147483648 | bytes 2097152 | tf_op jit(solution)/shard_map/pallas_call | solution.py:363
  44.8 1.9 %collective-permute-done.9.came = f32[8,136,128]{2,1,0:T(8,128)S(1)} collective-permute-done((f32[8,136,128]{2,1,0:T(8,128)S(1)}, f32[8,136,128]{2,1,0:T(8,128)S(1)}, u32[]{:S(2)}, u32[]{:S(2)}) %collective-permute-start.9) | collective-permute-done | bytes 557088 | tf_op jit(solution)/shard_map/ppermute | solution.py:285
  46.8 4.5 %shard_map.153 = (f32[64,4096]{1,0:T(8,128)S(1)}, bf16[32,4096]{1,0:T(8,128)(2,1)S(1)}, bf16[32,4096]{1,0:T(8,128)(2,1)S(1)}) custom-call(f32[8,136,128]{2,1,0:T(8,128)S(1)} %get-tuple-element.26.kept, f32[8,136,128]{2,1,0:T(8,128)S(1)} %collective-permute-done.9.came, bf16[512,4096]{1,0:T(8,128)(2,1)S(1)} %copy-done, ...), custom_call_target="tpu_custom_call" | custom-call | flops 1073741824 | bytes 8388608 | tf_op jit(solution)/shard_map/pallas_call | solution.py:394
  51.3 1.6 %collective-permute-start.11 = (bf16[32,4096]{1,0:T(8,128)(2,1)S(1)}, bf16[32,4096]{1,0:T(8,128)(2,1)S(1)}, u32[]{:S(2)}, u32[]{:S(2)}) collective-permute-start(bf16[32,4096]{1,0:T(8,128)(2,1)S(1)} %get-tuple-element.29), channel_id=1, source_target_pairs={{0,2},{1,3},{2,0},{3,1},{4,6},{5,7},{6,4},{7,5},{8,10},{9,11},{10,... | collective-permute-start | bytes 786440 | tf_op jit(solution)/shard_map/ppermute | solution.py:285
  53.5 7.0 %collective-permute-done.11.refs_0_ = bf16[32,4096]{1,0:T(8,128)(2,1)S(1)} collective-permute-done((bf16[32,4096]{1,0:T(8,128)(2,1)S(1)}, bf16[32,4096]{1,0:T(8,128)(2,1)S(1)}, u32[]{:S(2)}, u32[]{:S(2)}) %collective-permute-start.11) | collective-permute-done | bytes 262176 | tf_op jit(solution)/shard_map/ppermute | solution.py:285
  60.8 6.3 %collective-permute-start.13 = (bf16[32,4224]{1,0:T(8,128)(2,1)S(1)}, bf16[32,4224]{1,0:T(8,128)(2,1)S(1)}, u32[]{:S(2)}, u32[]{:S(2)}) collective-permute-start(bf16[32,4224]{1,0:T(8,128)(2,1)S(1)} %shard_map.154.refs_7_), channel_id=1, source_target_pairs={{0,4},{4,12},{8,0},{12,20},{16,8},{20,28},{24,16},{28,24},{1,5},{5... | collective-permute-start | bytes 811016 | tf_op jit(solution)/shard_map/ppermute | solution.py:285
  67.3 4.7 %collective-permute-start.24 = (bf16[32,4224]{1,0:T(8,128)(2,1)S(1)}, bf16[32,4224]{1,0:T(8,128)(2,1)S(1)}, u32[]{:S(2)}, u32[]{:S(2)}) collective-permute-start(bf16[32,4224]{1,0:T(8,128)(2,1)S(1)} %shard_map.155.refs_0_), channel_id=1, source_target_pairs={{0,4},{4,12},{8,0},{12,20},{16,8},{20,28},{24,16},{28,24},{1,5},{5... | collective-permute-start | bytes 811016 | tf_op jit(solution)/shard_map/ppermute | solution.py:285
  72.3 2.0 %collective-permute-start.15 = (bf16[32,4224]{1,0:T(8,128)(2,1)S(1)}, bf16[32,4224]{1,0:T(8,128)(2,1)S(1)}, u32[]{:S(2)}, u32[]{:S(2)}) collective-permute-start(bf16[32,4224]{1,0:T(8,128)(2,1)S(1)} %collective-permute-done.13.refs_1_), channel_id=1, source_target_pairs={{0,4},{4,12},{8,0},{12,20},{16,8},{20,28},{24,16},{28,24},{1,5},{5... | collective-permute-start | bytes 811016 | tf_op jit(solution)/shard_map/ppermute | solution.py:285
  74.3 4.9 %collective-permute-done.19.refs_1_ = bf16[32,4224]{1,0:T(8,128)(2,1)S(1)} collective-permute-done((bf16[32,4224]{1,0:T(8,128)(2,1)S(1)}, bf16[32,4224]{1,0:T(8,128)(2,1)S(1)}, u32[]{:S(2)}, u32[]{:S(2)}) %collective-permute-start.19) | collective-permute-done | bytes 270368 | tf_op jit(solution)/shard_map/ppermute | solution.py:285
  79.2 2.3 %collective-permute-start.25 = (bf16[32,4224]{1,0:T(8,128)(2,1)S(1)}, bf16[32,4224]{1,0:T(8,128)(2,1)S(1)}, u32[]{:S(2)}, u32[]{:S(2)}) collective-permute-start(bf16[32,4224]{1,0:T(8,128)(2,1)S(1)} %collective-permute-done.24.refs_2_), channel_id=1, source_target_pairs={{0,4},{4,12},{8,0},{12,20},{16,8},{20,28},{24,16},{28,24},{1,5},{5... | collective-permute-start | bytes 811016 | tf_op jit(solution)/shard_map/ppermute | solution.py:285
  81.5 3.5 %collective-permute-done.14.refs_2_ = bf16[32,4224]{1,0:T(8,128)(2,1)S(1)} collective-permute-done((bf16[32,4224]{1,0:T(8,128)(2,1)S(1)}, bf16[32,4224]{1,0:T(8,128)(2,1)S(1)}, u32[]{:S(2)}, u32[]{:S(2)}) %collective-permute-start.14) | collective-permute-done | bytes 270368 | tf_op jit(solution)/shard_map/ppermute | solution.py:285
  85.0 2.3 %collective-permute-start.17 = (bf16[32,4224]{1,0:T(8,128)(2,1)S(1)}, bf16[32,4224]{1,0:T(8,128)(2,1)S(1)}, u32[]{:S(2)}, u32[]{:S(2)}) collective-permute-start(bf16[32,4224]{1,0:T(8,128)(2,1)S(1)} %collective-permute-done.15.refs_3_), channel_id=1, source_target_pairs={{0,4},{4,12},{8,0},{12,20},{16,8},{20,28},{24,16},{28,24},{1,5},{5... | collective-permute-start | bytes 811016 | tf_op jit(solution)/shard_map/ppermute | solution.py:285
  87.3 3.5 %collective-permute-done.20.refs_3_ = bf16[32,4224]{1,0:T(8,128)(2,1)S(1)} collective-permute-done((bf16[32,4224]{1,0:T(8,128)(2,1)S(1)}, bf16[32,4224]{1,0:T(8,128)(2,1)S(1)}, u32[]{:S(2)}, u32[]{:S(2)}) %collective-permute-start.20) | collective-permute-done | bytes 270368 | tf_op jit(solution)/shard_map/ppermute | solution.py:285
  90.8 2.3 %collective-permute-start.26 = (bf16[32,4224]{1,0:T(8,128)(2,1)S(1)}, bf16[32,4224]{1,0:T(8,128)(2,1)S(1)}, u32[]{:S(2)}, u32[]{:S(2)}) collective-permute-start(bf16[32,4224]{1,0:T(8,128)(2,1)S(1)} %collective-permute-done.25.refs_4_), channel_id=1, source_target_pairs={{0,4},{4,12},{8,0},{12,20},{16,8},{20,28},{24,16},{28,24},{1,5},{5... | collective-permute-start | bytes 811016 | tf_op jit(solution)/shard_map/ppermute | solution.py:285
  93.1 3.5 %collective-permute-done.16.refs_4_ = bf16[32,4224]{1,0:T(8,128)(2,1)S(1)} collective-permute-done((bf16[32,4224]{1,0:T(8,128)(2,1)S(1)}, bf16[32,4224]{1,0:T(8,128)(2,1)S(1)}, u32[]{:S(2)}, u32[]{:S(2)}) %collective-permute-start.16) | collective-permute-done | bytes 270368 | tf_op jit(solution)/shard_map/ppermute | solution.py:285
  96.6 2.3 %collective-permute-start.23 = (bf16[32,4224]{1,0:T(8,128)(2,1)S(1)}, bf16[32,4224]{1,0:T(8,128)(2,1)S(1)}, u32[]{:S(2)}, u32[]{:S(2)}) collective-permute-start(bf16[32,4224]{1,0:T(8,128)(2,1)S(1)} %collective-permute-done.17.refs_5_), channel_id=1, source_target_pairs={{0,4},{4,12},{8,0},{12,20},{16,8},{20,28},{24,16},{28,24},{1,5},{5... | collective-permute-start | bytes 811016 | tf_op jit(solution)/shard_map/ppermute | solution.py:285
  98.9 2.2 %collective-permute-done.21.refs_5_ = bf16[32,4224]{1,0:T(8,128)(2,1)S(1)} collective-permute-done((bf16[32,4224]{1,0:T(8,128)(2,1)S(1)}, bf16[32,4224]{1,0:T(8,128)(2,1)S(1)}, u32[]{:S(2)}, u32[]{:S(2)}) %collective-permute-start.21) | collective-permute-done | bytes 270368 | tf_op jit(solution)/shard_map/ppermute | solution.py:285
  102.2 14.4 %shard_map.156.refs_9_ = f32[8,8,128]{2,1,0:T(8,128)S(1)} custom-call(s32[13]{0:T(128)S(1)} %concatenate.21.sc, bf16[32,4224]{1,0:T(8,128)(2,1)S(1)} %shard_map.155.refs_0_, bf16[32,4224]{1,0:T(8,128)(2,1)S(1)} %collective-permute-done.19.refs_1_, bf16[32,4224]{1,0:T(8,128)(2,1)S(1)} %collective-permute-done.24.refs_2_, ...), custom_call_target="tpu_custom_call" | custom-call | flops 8388608000 | bytes 32768000 | tf_op jit(solution)/shard_map/pallas_call | solution.py:473
  116.6 14.4 %shard_map.157 = (f32[4,8,128]{2,1,0:T(8,128)S(1)}, f32[4,8,128]{2,1,0:T(8,128)S(1)}) custom-call(s32[13]{0:T(128)S(1)} %concatenate.21.sc, bf16[32,4224]{1,0:T(8,128)(2,1)S(1)} %collective-permute-done.12.refs_0_, bf16[32,4224]{1,0:T(8,128)(2,1)S(1)} %collective-permute-done.13.refs_1_, bf16[32,4224]{1,0:T(8,128)(2,1)S(1)} %collective-permute-done.14.refs_2_, ...), custom_call_target="tpu_custom_call" | custom-call | flops 8388608000 | bytes 32768000 | tf_op jit(solution)/shard_map/pallas_call | solution.py:473
  131.0 4.9 %collective-permute-start.27 = (f32[4,8,128]{2,1,0:T(8,128)S(1)}, f32[4,8,128]{2,1,0:T(8,128)S(1)}, u32[]{:S(2)}, u32[]{:S(2)}) collective-permute-start(f32[4,8,128]{2,1,0:T(8,128)S(1)} %get-tuple-element.33), channel_id=1, source_target_pairs={{0,16},{4,20},{8,24},{12,28},{16,0},{20,4},{24,8},{28,12},{1,17},{... | collective-permute-start | bytes 49160 | tf_op jit(solution)/shard_map/ppermute | solution.py:285
  135.8 1.7 %collective-permute-done.27.other = f32[4,8,128]{2,1,0:T(8,128)S(1)} collective-permute-done((f32[4,8,128]{2,1,0:T(8,128)S(1)}, f32[4,8,128]{2,1,0:T(8,128)S(1)}, u32[]{:S(2)}, u32[]{:S(2)}) %collective-permute-start.27) | collective-permute-done | bytes 16416 | tf_op jit(solution)/shard_map/ppermute | solution.py:285
  137.6 2.1 %collective-permute-start.28 = (f32[2,8,128]{2,1,0:T(8,128)S(1)}, f32[2,8,128]{2,1,0:T(8,128)S(1)}, u32[]{:S(2)}, u32[]{:S(2)}) collective-permute-start(f32[2,8,128]{2,1,0:T(8,128)S(1)} %get-tuple-element.35), channel_id=1, source_target_pairs={{0,8},{4,12},{8,0},{12,4},{16,24},{20,28},{24,16},{28,20},{1,9},{5... | collective-permute-start | bytes 24584 | tf_op jit(solution)/shard_map/ppermute | solution.py:285
  139.7 1.6 %collective-permute-done.28.other = f32[2,8,128]{2,1,0:T(8,128)S(1)} collective-permute-done((f32[2,8,128]{2,1,0:T(8,128)S(1)}, f32[2,8,128]{2,1,0:T(8,128)S(1)}, u32[]{:S(2)}, u32[]{:S(2)}) %collective-permute-start.28) | collective-permute-done | bytes 8224 | tf_op jit(solution)/shard_map/ppermute | solution.py:285
  142.0 3.0 %collective-permute-done.29.other = f32[1,8,128]{2,1,0:T(8,128)S(1)} collective-permute-done((f32[1,8,128]{2,1,0:T(8,128)S(1)}, f32[1,8,128]{2,1,0:T(8,128)S(1)}, u32[]{:S(2)}, u32[]{:S(2)}) %collective-permute-start.29) | collective-permute-done | bytes 4128 | tf_op jit(solution)/shard_map/ppermute | solution.py:285
  (80 shorter events, 12.7 us)
Async XLA Ops:
  0.7 46.1 %collective-permute-start.10 = (bf16[512,4096]{1,0:T(8,128)(2,1)}, bf16[512,4096]{1,0:T(8,128)(2,1)}, u32[]{:S(2)}, u32[]{:S(2)}) collective-permute-start(bf16[512,4096]{1,0:T(8,128)(2,1)} %mine.1), channel_id=1, source_target_pairs={{0,1},{1,0},{2,3},{3,2},{4,5},{5,4},{6,7},{7,6},{8,9},{9,8},{10,11... | collective-permute-start | bytes 12582920 | tf_op jit(solution)/shard_map/ppermute | solution.py:285
  5.2 14.0 %collective-permute-start.4 = (bf16[1040,128]{1,0:T(8,128)(2,1)S(1)}, bf16[1040,128]{1,0:T(8,128)(2,1)S(1)}, u32[]{:S(2)}, u32[]{:S(2)}) collective-permute-start(bf16[1040,128]{1,0:T(8,128)(2,1)S(1)} %get-tuple-element.52.refs_1_), channel_id=1, source_target_pairs={{0,24},{4,28},{8,0},{12,4},{16,8},{20,12},{24,16},{28,20},{1,25},{... | collective-permute-start | bytes 798728 | tf_op jit(solution)/shard_map/ppermute | solution.py:285
  10.0 16.0 %collective-permute-start.6 = (bf16[1040,128]{1,0:T(8,128)(2,1)S(1)}, bf16[1040,128]{1,0:T(8,128)(2,1)S(1)}, u32[]{:S(2)}, u32[]{:S(2)}) collective-permute-start(bf16[1040,128]{1,0:T(8,128)(2,1)S(1)} %get-tuple-element.52.refs_1_), channel_id=1, source_target_pairs={{4,0},{12,8},{20,16},{28,24},{5,1},{13,9},{21,17},{29,25},{6,2},{1... | collective-permute-start | bytes 798728 | tf_op jit(solution)/shard_map/ppermute | solution.py:285
  11.3 14.7 %collective-permute-start.5 = (bf16[1040,128]{1,0:T(8,128)(2,1)S(1)}, bf16[1040,128]{1,0:T(8,128)(2,1)S(1)}, u32[]{:S(2)}, u32[]{:S(2)}) collective-permute-start(bf16[1040,128]{1,0:T(8,128)(2,1)S(1)} %get-tuple-element.53.refs_0_), channel_id=1, source_target_pairs={{4,0},{12,8},{20,16},{28,24},{5,1},{13,9},{21,17},{29,25},{6,2},{1... | collective-permute-start | bytes 798728 | tf_op jit(solution)/shard_map/ppermute | solution.py:285
  12.6 2.7 %collective-permute-start = (bf16[256,512]{1,0:T(8,128)(2,1)S(1)}, bf16[256,512]{1,0:T(8,128)(2,1)S(1)}, u32[]{:S(2)}, u32[]{:S(2)}) collective-permute-start(bf16[256,512]{1,0:T(8,128)(2,1)S(1)} %copy-done.3), channel_id=1, source_target_pairs={{0,1},{1,0},{2,3},{3,2},{4,5},{5,4},{6,7},{7,6},{8,9},{9,8},{10,11... | collective-permute-start | bytes 786440 | tf_op jit(solution)/shard_map/ppermute | solution.py:285
  15.3 10.6 %collective-permute-start.1 = (bf16[1040,128]{1,0:T(8,128)(2,1)S(1)}, bf16[1040,128]{1,0:T(8,128)(2,1)S(1)}, u32[]{:S(2)}, u32[]{:S(2)}) collective-permute-start(bf16[1040,128]{1,0:T(8,128)(2,1)S(1)} %get-tuple-element.53.refs_0_), channel_id=1, source_target_pairs={{0,24},{4,28},{8,0},{12,4},{16,8},{20,12},{24,16},{28,20},{1,25},{... | collective-permute-start | bytes 798728 | tf_op jit(solution)/shard_map/ppermute | solution.py:285
  26.0 9.3 %collective-permute-start.7 = (bf16[1040,128]{1,0:T(8,128)(2,1)S(1)}, bf16[1040,128]{1,0:T(8,128)(2,1)S(1)}, u32[]{:S(2)}, u32[]{:S(2)}) collective-permute-start(bf16[1040,128]{1,0:T(8,128)(2,1)S(1)} %collective-permute-done.4.refs_3_), channel_id=1, source_target_pairs={{0,4},{4,0},{8,12},{12,8},{16,20},{20,16},{24,28},{28,24},{1,5},{5... | collective-permute-start | bytes 798728 | tf_op jit(solution)/shard_map/ppermute | solution.py:285
  26.8 12.4 %collective-permute-start.2 = (bf16[1040,128]{1,0:T(8,128)(2,1)S(1)}, bf16[1040,128]{1,0:T(8,128)(2,1)S(1)}, u32[]{:S(2)}, u32[]{:S(2)}) collective-permute-start(bf16[1040,128]{1,0:T(8,128)(2,1)S(1)} %collective-permute-done.1.refs_2_), channel_id=1, source_target_pairs={{0,4},{4,0},{8,12},{12,8},{16,20},{20,16},{24,28},{28,24},{1,5},{5... | collective-permute-start | bytes 798728 | tf_op jit(solution)/shard_map/ppermute | solution.py:285
  35.3 8.5 %collective-permute-start.8 = (bf16[1040,128]{1,0:T(8,128)(2,1)S(1)}, bf16[1040,128]{1,0:T(8,128)(2,1)S(1)}, u32[]{:S(2)}, u32[]{:S(2)}) collective-permute-start(bf16[1040,128]{1,0:T(8,128)(2,1)S(1)} %collective-permute-done.7.refs_1_), channel_id=1, source_target_pairs={{4,28},{12,4},{20,12},{28,20},{5,29},{13,5},{21,13},{29,21},{6,30}... | collective-permute-start | bytes 798728 | tf_op jit(solution)/shard_map/ppermute | solution.py:285
  39.2 4.7 %collective-permute-start.3 = (bf16[1040,128]{1,0:T(8,128)(2,1)S(1)}, bf16[1040,128]{1,0:T(8,128)(2,1)S(1)}, u32[]{:S(2)}, u32[]{:S(2)}) collective-permute-start(bf16[1040,128]{1,0:T(8,128)(2,1)S(1)} %collective-permute-done.2.refs_0_), channel_id=1, source_target_pairs={{4,28},{12,4},{20,12},{28,20},{5,29},{13,5},{21,13},{29,21},{6,30}... | collective-permute-start | bytes 798728 | tf_op jit(solution)/shard_map/ppermute | solution.py:285
  44.7 2.0 %collective-permute-start.9 = (f32[8,136,128]{2,1,0:T(8,128)S(1)}, f32[8,136,128]{2,1,0:T(8,128)S(1)}, u32[]{:S(2)}, u32[]{:S(2)}) collective-permute-start(f32[8,136,128]{2,1,0:T(8,128)S(1)} %get-tuple-element.27), channel_id=1, source_target_pairs={{0,1},{1,0},{2,3},{3,2},{4,5},{5,4},{6,7},{7,6},{8,9},{9,8},{10,11... | collective-permute-start | bytes 1671176 | tf_op jit(solution)/shard_map/ppermute | solution.py:285
  46.8 13.7 %copy-start.1 = (bf16[64,4096]{1,0:T(8,128)(2,1)S(1)}, bf16[64,4096]{1,0:T(8,128)(2,1)}, u32[]{:S(2)}) copy-start(bf16[64,4096]{1,0:T(8,128)(2,1)} %hidden.3) | copy-start | bytes 1572868
  46.8 13.7 %copy-start.2 = (f32[4096]{0:T(1024)S(1)}, f32[4096]{0:T(1024)}, u32[]{:S(2)}) copy-start(f32[4096]{0:T(1024)} %param.21) | copy-start | bytes 49156
  51.3 9.2 %collective-permute-start.11 = (bf16[32,4096]{1,0:T(8,128)(2,1)S(1)}, bf16[32,4096]{1,0:T(8,128)(2,1)S(1)}, u32[]{:S(2)}, u32[]{:S(2)}) collective-permute-start(bf16[32,4096]{1,0:T(8,128)(2,1)S(1)} %get-tuple-element.29), channel_id=1, source_target_pairs={{0,2},{1,3},{2,0},{3,1},{4,6},{5,7},{6,4},{7,5},{8,10},{9,11},{10,... | collective-permute-start | bytes 786440 | tf_op jit(solution)/shard_map/ppermute | solution.py:285
  52.9 14.2 %collective-permute-start.18 = (bf16[32,4096]{1,0:T(8,128)(2,1)S(1)}, bf16[32,4096]{1,0:T(8,128)(2,1)S(1)}, u32[]{:S(2)}, u32[]{:S(2)}) collective-permute-start(bf16[32,4096]{1,0:T(8,128)(2,1)S(1)} %get-tuple-element.30), channel_id=1, source_target_pairs={{0,2},{1,3},{2,0},{3,1},{4,6},{5,7},{6,4},{7,5},{8,10},{9,11},{10,... | collective-permute-start | bytes 786440 | tf_op jit(solution)/shard_map/ppermute | solution.py:285
  60.7 11.5 %collective-permute-start.12 = (bf16[32,4224]{1,0:T(8,128)(2,1)S(1)}, bf16[32,4224]{1,0:T(8,128)(2,1)S(1)}, u32[]{:S(2)}, u32[]{:S(2)}) collective-permute-start(bf16[32,4224]{1,0:T(8,128)(2,1)S(1)} %shard_map.154.refs_7_), channel_id=1, source_target_pairs={{0,8},{4,0},{8,16},{12,4},{16,24},{20,12},{24,28},{28,20},{1,9},{5... | collective-permute-start | bytes 811016 | tf_op jit(solution)/shard_map/ppermute | solution.py:285
  60.8 11.5 %collective-permute-start.13 = (bf16[32,4224]{1,0:T(8,128)(2,1)S(1)}, bf16[32,4224]{1,0:T(8,128)(2,1)S(1)}, u32[]{:S(2)}, u32[]{:S(2)}) collective-permute-start(bf16[32,4224]{1,0:T(8,128)(2,1)S(1)} %shard_map.154.refs_7_), channel_id=1, source_target_pairs={{0,4},{4,12},{8,0},{12,20},{16,8},{20,28},{24,16},{28,24},{1,5},{5... | collective-permute-start | bytes 811016 | tf_op jit(solution)/shard_map/ppermute | solution.py:285
  67.3 11.9 %collective-permute-start.19 = (bf16[32,4224]{1,0:T(8,128)(2,1)S(1)}, bf16[32,4224]{1,0:T(8,128)(2,1)S(1)}, u32[]{:S(2)}, u32[]{:S(2)}) collective-permute-start(bf16[32,4224]{1,0:T(8,128)(2,1)S(1)} %shard_map.155.refs_0_), channel_id=1, source_target_pairs={{0,8},{4,0},{8,16},{12,4},{16,24},{20,12},{24,28},{28,20},{1,9},{5... | collective-permute-start | bytes 811016 | tf_op jit(solution)/shard_map/ppermute | solution.py:285
  67.3 11.8 %collective-permute-start.24 = (bf16[32,4224]{1,0:T(8,128)(2,1)S(1)}, bf16[32,4224]{1,0:T(8,128)(2,1)S(1)}, u32[]{:S(2)}, u32[]{:S(2)}) collective-permute-start(bf16[32,4224]{1,0:T(8,128)(2,1)S(1)} %shard_map.155.refs_0_), channel_id=1, source_target_pairs={{0,4},{4,12},{8,0},{12,20},{16,8},{20,28},{24,16},{28,24},{1,5},{5... | collective-permute-start | bytes 811016 | tf_op jit(solution)/shard_map/ppermute | solution.py:285
  72.3 12.7 %collective-permute-start.14 = (bf16[32,4224]{1,0:T(8,128)(2,1)S(1)}, bf16[32,4224]{1,0:T(8,128)(2,1)S(1)}, u32[]{:S(2)}, u32[]{:S(2)}) collective-permute-start(bf16[32,4224]{1,0:T(8,128)(2,1)S(1)} %collective-permute-done.12.refs_0_), channel_id=1, source_target_pairs={{0,8},{4,0},{8,16},{12,4},{16,24},{20,12},{24,28},{28,20},{1,9},{5... | collective-permute-start | bytes 811016 | tf_op jit(solution)/shard_map/ppermute | solution.py:285
  72.3 12.7 %collective-permute-start.15 = (bf16[32,4224]{1,0:T(8,128)(2,1)S(1)}, bf16[32,4224]{1,0:T(8,128)(2,1)S(1)}, u32[]{:S(2)}, u32[]{:S(2)}) collective-permute-start(bf16[32,4224]{1,0:T(8,128)(2,1)S(1)} %collective-permute-done.13.refs_1_), channel_id=1, source_target_pairs={{0,4},{4,12},{8,0},{12,20},{16,8},{20,28},{24,16},{28,24},{1,5},{5... | collective-permute-start | bytes 811016 | tf_op jit(solution)/shard_map/ppermute | solution.py:285
  79.2 11.6 %collective-permute-start.20 = (bf16[32,4224]{1,0:T(8,128)(2,1)S(1)}, bf16[32,4224]{1,0:T(8,128)(2,1)S(1)}, u32[]{:S(2)}, u32[]{:S(2)}) collective-permute-start(bf16[32,4224]{1,0:T(8,128)(2,1)S(1)} %collective-permute-done.19.refs_1_), channel_id=1, source_target_pairs={{0,8},{4,0},{8,16},{12,4},{16,24},{20,12},{24,28},{28,20},{1,9},{5... | collective-permute-start | bytes 811016 | tf_op jit(solution)/shard_map/ppermute | solution.py:285
  79.2 11.6 %collective-permute-start.25 = (bf16[32,4224]{1,0:T(8,128)(2,1)S(1)}, bf16[32,4224]{1,0:T(8,128)(2,1)S(1)}, u32[]{:S(2)}, u32[]{:S(2)}) collective-permute-start(bf16[32,4224]{1,0:T(8,128)(2,1)S(1)} %collective-permute-done.24.refs_2_), channel_id=1, source_target_pairs={{0,4},{4,12},{8,0},{12,20},{16,8},{20,28},{24,16},{28,24},{1,5},{5... | collective-permute-start | bytes 811016 | tf_op jit(solution)/shard_map/ppermute | solution.py:285
  85.0 11.6 %collective-permute-start.16 = (bf16[32,4224]{1,0:T(8,128)(2,1)S(1)}, bf16[32,4224]{1,0:T(8,128)(2,1)S(1)}, u32[]{:S(2)}, u32[]{:S(2)}) collective-permute-start(bf16[32,4224]{1,0:T(8,128)(2,1)S(1)} %collective-permute-done.14.refs_2_), channel_id=1, source_target_pairs={{0,8},{4,0},{8,16},{12,4},{16,24},{20,12},{24,28},{28,20},{1,9},{5... | collective-permute-start | bytes 811016 | tf_op jit(solution)/shard_map/ppermute | solution.py:285
  85.0 11.6 %collective-permute-start.17 = (bf16[32,4224]{1,0:T(8,128)(2,1)S(1)}, bf16[32,4224]{1,0:T(8,128)(2,1)S(1)}, u32[]{:S(2)}, u32[]{:S(2)}) collective-permute-start(bf16[32,4224]{1,0:T(8,128)(2,1)S(1)} %collective-permute-done.15.refs_3_), channel_id=1, source_target_pairs={{0,4},{4,12},{8,0},{12,20},{16,8},{20,28},{24,16},{28,24},{1,5},{5... | collective-permute-start | bytes 811016 | tf_op jit(solution)/shard_map/ppermute | solution.py:285
  90.8 10.3 %collective-permute-start.21 = (bf16[32,4224]{1,0:T(8,128)(2,1)S(1)}, bf16[32,4224]{1,0:T(8,128)(2,1)S(1)}, u32[]{:S(2)}, u32[]{:S(2)}) collective-permute-start(bf16[32,4224]{1,0:T(8,128)(2,1)S(1)} %collective-permute-done.20.refs_3_), channel_id=1, source_target_pairs={{0,8},{4,0},{8,16},{12,4},{16,24},{20,12},{24,28},{28,20},{1,9},{5... | collective-permute-start | bytes 811016 | tf_op jit(solution)/shard_map/ppermute | solution.py:285
  90.8 11.4 %collective-permute-start.26 = (bf16[32,4224]{1,0:T(8,128)(2,1)S(1)}, bf16[32,4224]{1,0:T(8,128)(2,1)S(1)}, u32[]{:S(2)}, u32[]{:S(2)}) collective-permute-start(bf16[32,4224]{1,0:T(8,128)(2,1)S(1)} %collective-permute-done.25.refs_4_), channel_id=1, source_target_pairs={{0,4},{4,12},{8,0},{12,20},{16,8},{20,28},{24,16},{28,24},{1,5},{5... | collective-permute-start | bytes 811016 | tf_op jit(solution)/shard_map/ppermute | solution.py:285
  96.6 20.0 %collective-permute-start.23 = (bf16[32,4224]{1,0:T(8,128)(2,1)S(1)}, bf16[32,4224]{1,0:T(8,128)(2,1)S(1)}, u32[]{:S(2)}, u32[]{:S(2)}) collective-permute-start(bf16[32,4224]{1,0:T(8,128)(2,1)S(1)} %collective-permute-done.17.refs_5_), channel_id=1, source_target_pairs={{0,4},{4,12},{8,0},{12,20},{16,8},{20,28},{24,16},{28,24},{1,5},{5... | collective-permute-start | bytes 811016 | tf_op jit(solution)/shard_map/ppermute | solution.py:285
  101.1 15.5 %collective-permute-start.22 = (bf16[32,4224]{1,0:T(8,128)(2,1)S(1)}, bf16[32,4224]{1,0:T(8,128)(2,1)S(1)}, u32[]{:S(2)}, u32[]{:S(2)}) collective-permute-start(bf16[32,4224]{1,0:T(8,128)(2,1)S(1)} %collective-permute-done.21.refs_5_), channel_id=1, source_target_pairs={{0,8},{4,0},{8,16},{12,4},{16,24},{20,12},{24,28},{28,20},{1,9},{5... | collective-permute-start | bytes 811016 | tf_op jit(solution)/shard_map/ppermute | solution.py:285
  131.0 6.6 %collective-permute-start.27 = (f32[4,8,128]{2,1,0:T(8,128)S(1)}, f32[4,8,128]{2,1,0:T(8,128)S(1)}, u32[]{:S(2)}, u32[]{:S(2)}) collective-permute-start(f32[4,8,128]{2,1,0:T(8,128)S(1)} %get-tuple-element.33), channel_id=1, source_target_pairs={{0,16},{4,20},{8,24},{12,28},{16,0},{20,4},{24,8},{28,12},{1,17},{... | collective-permute-start | bytes 49160 | tf_op jit(solution)/shard_map/ppermute | solution.py:285
  137.6 3.7 %collective-permute-start.28 = (f32[2,8,128]{2,1,0:T(8,128)S(1)}, f32[2,8,128]{2,1,0:T(8,128)S(1)}, u32[]{:S(2)}, u32[]{:S(2)}) collective-permute-start(f32[2,8,128]{2,1,0:T(8,128)S(1)} %get-tuple-element.35), channel_id=1, source_target_pairs={{0,8},{4,12},{8,0},{12,4},{16,24},{20,28},{24,16},{28,20},{1,9},{5... | collective-permute-start | bytes 24584 | tf_op jit(solution)/shard_map/ppermute | solution.py:285
  141.3 3.7 %collective-permute-start.29 = (f32[1,8,128]{2,1,0:T(8,128)S(1)}, f32[1,8,128]{2,1,0:T(8,128)S(1)}, u32[]{:S(2)}, u32[]{:S(2)}) collective-permute-start(f32[1,8,128]{2,1,0:T(8,128)S(1)} %get-tuple-element.37), channel_id=1, source_target_pairs={{0,4},{4,0},{8,12},{12,8},{16,20},{20,16},{24,28},{28,24},{1,5},{5... | collective-permute-start | bytes 12296 | tf_op jit(solution)/shard_map/ppermute | solution.py:285
  (6 other events, 61.5 us)

commit v4 on v3

--- a/solution.py
+++ b/solution.py
@@ -387,7 +387,7 @@
     )(plan, query, *three, state)
     came = over(sent, "mp", lambda i: i ^ 1)
 
-    tile = 1024
+    tile = 2048
     rows_core = rollout // 2
     deep = rows_here // 2
     pieces = [(k, side) for k in range(1, members // 2) for side in (0, 1)]
@@ -406,7 +406,7 @@
             *[pl.BlockSpec((deep, tile), lambda i: (0, i))] * len(pieces),
         ),
         scratch_shapes=[pltpu.VMEM((rows_core, heads * size), jnp.bfloat16)],
-        compiler_params=pltpu.CompilerParams(vmem_limit_bytes=16 * MIB),
+        compiler_params=pltpu.CompilerParams(vmem_limit_bytes=24 * MIB),
         cost_estimate=pl.CostEstimate(
             flops=2 * rows_core * heads * size * width,
             bytes_accessed=4 * out_weight.shape[0] * width,

time: 147 us -> 146 us (level)
  no operation moved by 1% of the time
where the time goes in v4:
time: 146 us; the launch traced here: 145 us
  waiting for transfers between devices  50.7 us (35%)
  starting transfers between devices  45.1 us (31%)
  Pallas kernels  41.8 us (29%)
  between operations  3.11 us (2%)
  local copies, waits for them, and re-layouts  2.87 us (2%)
  other arithmetic  1.73 us (1%)
    ppermute x30, waiting for transfers between devices, over(): return lax.ppermute(block, axis, pairs)  50.7 us
    ppermute x30, starting transfers between devices, over(): return lax.ppermute(block, axis, pairs)  45.1 us
    pallas_call x2, Pallas kernels, body(): call(functools.partial(head_kernel, block=block, homes=[(name, side) for...  28.7 us
    pallas_call x1, Pallas kernels, body(): pl.pallas_call(functools.partial(merge_kernel, size=size, rows=rows_here)...  3.51 us
    pallas_call x1, Pallas kernels, body(): call(functools.partial(first_kernel, size=size, scale=scale), full, [smem...  3.23 us
    pallas_call x1, Pallas kernels, body(): call(functools.partial(more_kernel, size=size, scale=scale, wants=(1,) *...  3.12 us
  transfers between devices with their start and end apart: 30, of which 15 were waited for; matrix products, arithmetic and copies ran while one was open for 3% of the time, Pallas kernels for 16%

profile of v4, /device:TPU:0, one launch (start us, length us, event | category | flops | bytes accessed | tf_op | source)
XLA Modules:
  0.0 145.3 jit_solution(10039055165823636203)
XLA Ops:
  1.9 2.4 %constant_dynamic-slice_fusion.4 = (bf16[2,1,256,1,128]{4,3,2,1,0:T(2,128)(2,1)S(1)}, bf16[2,1,256,1,128]{4,3,2,1,0:T(2,128)(2,1)S(1)}, bf16[2,1,256,1,128]{4,3,...) fusion(bf16[4,2,256,2,128]{4,3,2,1,0:T(2,128)(2,1)} %bitcast.40, s32[]{:T(128)S(6)} %add.129, s32[]{:T(128)S(6)} %select_n.98, ...), kind=kLoop, calls=%fused_computation.12 | loop fusion | bytes 1048588 | tf_op jit(solution)/shard_map/slice | solution.py:305
  5.2 4.8 %collective-permute-start.4 = (bf16[1040,128]{1,0:T(8,128)(2,1)S(1)}, bf16[1040,128]{1,0:T(8,128)(2,1)S(1)}, u32[]{:S(2)}, u32[]{:S(2)}) collective-permute-start(bf16[1040,128]{1,0:T(8,128)(2,1)S(1)} %get-tuple-element.52.refs_1_), channel_id=1, source_target_pairs={{0,24},{4,28},{8,0},{12,4},{16,8},{20,12},{24,16},{28,20},{1,25},{... | collective-permute-start | bytes 798728 | tf_op jit(solution)/shard_map/ppermute | solution.py:285
  11.3 1.3 collective-permute-start.5
  15.9 3.2 %shard_map.149.refs_4_ = f32[8,136,256]{2,1,0:T(8,128)S(1)} custom-call(s32[13]{0:T(128)S(1)} %concatenate.21.sc, s32[1,256]{1,0:T(1,128)S(1)} %bitcast.33, bf16[256,1024]{1,0:T(8,128)(2,1)S(1)} %maximum_maximum_fusion.query, bf16[128,128]{1,0:T(8,128)(2,1)S(1)} %bitcast.32, bf16[128,128]{1,0:T(8,128)(2,1)S(1)} %bitcast.31, ...), custom_call_target="tpu_custom_call" | custom-call | flops 1073741824 | bytes 1048576 | tf_op jit(solution)/shard_map/pallas_call | solution.py:344
  19.2 6.8 %collective-permute-done.5.refs_0_ = bf16[1040,128]{1,0:T(8,128)(2,1)S(1)} collective-permute-done((bf16[1040,128]{1,0:T(8,128)(2,1)S(1)}, bf16[1040,128]{1,0:T(8,128)(2,1)S(1)}, u32[]{:S(2)}, u32[]{:S(2)}) %collective-permute-start.5) | collective-permute-done | bytes 266272 | tf_op jit(solution)/shard_map/ppermute | solution.py:285
  28.0 7.3 %collective-permute-done.7.refs_1_ = bf16[1040,128]{1,0:T(8,128)(2,1)S(1)} collective-permute-done((bf16[1040,128]{1,0:T(8,128)(2,1)S(1)}, bf16[1040,128]{1,0:T(8,128)(2,1)S(1)}, u32[]{:S(2)}, u32[]{:S(2)}) %collective-permute-start.7) | collective-permute-done | bytes 266272 | tf_op jit(solution)/shard_map/ppermute | solution.py:285
  36.0 3.2 %collective-permute-done.2.refs_0_ = bf16[1040,128]{1,0:T(8,128)(2,1)S(1)} collective-permute-done((bf16[1040,128]{1,0:T(8,128)(2,1)S(1)}, bf16[1040,128]{1,0:T(8,128)(2,1)S(1)}, u32[]{:S(2)}, u32[]{:S(2)}) %collective-permute-start.2) | collective-permute-done | bytes 266272 | tf_op jit(solution)/shard_map/ppermute | solution.py:285
  39.9 3.1 %shard_map.150.refs_2_ = f32[8,136,256]{2,1,0:T(8,128)S(1)} custom-call(s32[13]{0:T(128)S(1)} %concatenate.21.sc, bf16[256,1024]{1,0:T(8,128)(2,1)S(1)} %maximum_maximum_fusion.query, bf16[1040,128]{1,0:T(8,128)(2,1)S(1)} %collective-permute-done.5.refs_0_, bf16[1040,128]{1,0:T(8,128)(2,1)S(1)} %collective-permute-done.6.refs_1_, ...), custom_call_target="tpu_custom_call" | custom-call | flops 2147483648 | bytes 2097152 | tf_op jit(solution)/shard_map/pallas_call | solution.py:363
  44.8 1.9 %collective-permute-done.9.came = f32[8,136,128]{2,1,0:T(8,128)S(1)} collective-permute-done((f32[8,136,128]{2,1,0:T(8,128)S(1)}, f32[8,136,128]{2,1,0:T(8,128)S(1)}, u32[]{:S(2)}, u32[]{:S(2)}) %collective-permute-start.9) | collective-permute-done | bytes 557088 | tf_op jit(solution)/shard_map/ppermute | solution.py:285
  46.8 3.5 %shard_map.153 = (f32[64,4096]{1,0:T(8,128)S(1)}, bf16[32,4096]{1,0:T(8,128)(2,1)S(1)}, bf16[32,4096]{1,0:T(8,128)(2,1)S(1)}) custom-call(f32[8,136,128]{2,1,0:T(8,128)S(1)} %get-tuple-element.26.kept, f32[8,136,128]{2,1,0:T(8,128)S(1)} %collective-permute-done.9.came, bf16[512,4096]{1,0:T(8,128)(2,1)S(1)} %copy-done, ...), custom_call_target="tpu_custom_call" | custom-call | flops 1073741824 | bytes 8388608 | tf_op jit(solution)/shard_map/pallas_call | solution.py:394
  50.3 1.6 %collective-permute-start.11 = (bf16[32,4096]{1,0:T(8,128)(2,1)S(1)}, bf16[32,4096]{1,0:T(8,128)(2,1)S(1)}, u32[]{:S(2)}, u32[]{:S(2)}) collective-permute-start(bf16[32,4096]{1,0:T(8,128)(2,1)S(1)} %get-tuple-element.29), channel_id=1, source_target_pairs={{0,2},{1,3},{2,0},{3,1},{4,6},{5,7},{6,4},{7,5},{8,10},{9,11},{10,... | collective-permute-start | bytes 786440 | tf_op jit(solution)/shard_map/ppermute | solution.py:285
  52.5 7.0 %collective-permute-done.11.refs_0_ = bf16[32,4096]{1,0:T(8,128)(2,1)S(1)} collective-permute-done((bf16[32,4096]{1,0:T(8,128)(2,1)S(1)}, bf16[32,4096]{1,0:T(8,128)(2,1)S(1)}, u32[]{:S(2)}, u32[]{:S(2)}) %collective-permute-start.11) | collective-permute-done | bytes 262176 | tf_op jit(solution)/shard_map/ppermute | solution.py:285
  59.8 8.3 %collective-permute-start.13 = (bf16[32,4224]{1,0:T(8,128)(2,1)S(1)}, bf16[32,4224]{1,0:T(8,128)(2,1)S(1)}, u32[]{:S(2)}, u32[]{:S(2)}) collective-permute-start(bf16[32,4224]{1,0:T(8,128)(2,1)S(1)} %shard_map.154.refs_7_), channel_id=1, source_target_pairs={{0,4},{4,12},{8,0},{12,20},{16,8},{20,28},{24,16},{28,24},{1,5},{5... | collective-permute-start | bytes 811016 | tf_op jit(solution)/shard_map/ppermute | solution.py:285
  68.5 4.3 %collective-permute-start.24 = (bf16[32,4224]{1,0:T(8,128)(2,1)S(1)}, bf16[32,4224]{1,0:T(8,128)(2,1)S(1)}, u32[]{:S(2)}, u32[]{:S(2)}) collective-permute-start(bf16[32,4224]{1,0:T(8,128)(2,1)S(1)} %shard_map.155.refs_0_), channel_id=1, source_target_pairs={{0,4},{4,12},{8,0},{12,20},{16,8},{20,28},{24,16},{28,24},{1,5},{5... | collective-permute-start | bytes 811016 | tf_op jit(solution)/shard_map/ppermute | solution.py:285
  73.2 2.2 %collective-permute-start.15 = (bf16[32,4224]{1,0:T(8,128)(2,1)S(1)}, bf16[32,4224]{1,0:T(8,128)(2,1)S(1)}, u32[]{:S(2)}, u32[]{:S(2)}) collective-permute-start(bf16[32,4224]{1,0:T(8,128)(2,1)S(1)} %collective-permute-done.13.refs_1_), channel_id=1, source_target_pairs={{0,4},{4,12},{8,0},{12,20},{16,8},{20,28},{24,16},{28,24},{1,5},{5... | collective-permute-start | bytes 811016 | tf_op jit(solution)/shard_map/ppermute | solution.py:285
  75.4 4.7 %collective-permute-done.19.refs_1_ = bf16[32,4224]{1,0:T(8,128)(2,1)S(1)} collective-permute-done((bf16[32,4224]{1,0:T(8,128)(2,1)S(1)}, bf16[32,4224]{1,0:T(8,128)(2,1)S(1)}, u32[]{:S(2)}, u32[]{:S(2)}) %collective-permute-start.19) | collective-permute-done | bytes 270368 | tf_op jit(solution)/shard_map/ppermute | solution.py:285
  80.1 2.1 %collective-permute-start.25 = (bf16[32,4224]{1,0:T(8,128)(2,1)S(1)}, bf16[32,4224]{1,0:T(8,128)(2,1)S(1)}, u32[]{:S(2)}, u32[]{:S(2)}) collective-permute-start(bf16[32,4224]{1,0:T(8,128)(2,1)S(1)} %collective-permute-done.24.refs_2_), channel_id=1, source_target_pairs={{0,4},{4,12},{8,0},{12,20},{16,8},{20,28},{24,16},{28,24},{1,5},{5... | collective-permute-start | bytes 811016 | tf_op jit(solution)/shard_map/ppermute | solution.py:285
  82.2 3.7 %collective-permute-done.14.refs_2_ = bf16[32,4224]{1,0:T(8,128)(2,1)S(1)} collective-permute-done((bf16[32,4224]{1,0:T(8,128)(2,1)S(1)}, bf16[32,4224]{1,0:T(8,128)(2,1)S(1)}, u32[]{:S(2)}, u32[]{:S(2)}) %collective-permute-start.14) | collective-permute-done | bytes 270368 | tf_op jit(solution)/shard_map/ppermute | solution.py:285
  85.9 2.1 %collective-permute-start.17 = (bf16[32,4224]{1,0:T(8,128)(2,1)S(1)}, bf16[32,4224]{1,0:T(8,128)(2,1)S(1)}, u32[]{:S(2)}, u32[]{:S(2)}) collective-permute-start(bf16[32,4224]{1,0:T(8,128)(2,1)S(1)} %collective-permute-done.15.refs_3_), channel_id=1, source_target_pairs={{0,4},{4,12},{8,0},{12,20},{16,8},{20,28},{24,16},{28,24},{1,5},{5... | collective-permute-start | bytes 811016 | tf_op jit(solution)/shard_map/ppermute | solution.py:285
  88.0 3.7 %collective-permute-done.20.refs_3_ = bf16[32,4224]{1,0:T(8,128)(2,1)S(1)} collective-permute-done((bf16[32,4224]{1,0:T(8,128)(2,1)S(1)}, bf16[32,4224]{1,0:T(8,128)(2,1)S(1)}, u32[]{:S(2)}, u32[]{:S(2)}) %collective-permute-start.20) | collective-permute-done | bytes 270368 | tf_op jit(solution)/shard_map/ppermute | solution.py:285
  91.7 2.1 %collective-permute-start.26 = (bf16[32,4224]{1,0:T(8,128)(2,1)S(1)}, bf16[32,4224]{1,0:T(8,128)(2,1)S(1)}, u32[]{:S(2)}, u32[]{:S(2)}) collective-permute-start(bf16[32,4224]{1,0:T(8,128)(2,1)S(1)} %collective-permute-done.25.refs_4_), channel_id=1, source_target_pairs={{0,4},{4,12},{8,0},{12,20},{16,8},{20,28},{24,16},{28,24},{1,5},{5... | collective-permute-start | bytes 811016 | tf_op jit(solution)/shard_map/ppermute | solution.py:285
  93.8 3.7 %collective-permute-done.16.refs_4_ = bf16[32,4224]{1,0:T(8,128)(2,1)S(1)} collective-permute-done((bf16[32,4224]{1,0:T(8,128)(2,1)S(1)}, bf16[32,4224]{1,0:T(8,128)(2,1)S(1)}, u32[]{:S(2)}, u32[]{:S(2)}) %collective-permute-start.16) | collective-permute-done | bytes 270368 | tf_op jit(solution)/shard_map/ppermute | solution.py:285
  97.5 2.1 %collective-permute-start.23 = (bf16[32,4224]{1,0:T(8,128)(2,1)S(1)}, bf16[32,4224]{1,0:T(8,128)(2,1)S(1)}, u32[]{:S(2)}, u32[]{:S(2)}) collective-permute-start(bf16[32,4224]{1,0:T(8,128)(2,1)S(1)} %collective-permute-done.17.refs_5_), channel_id=1, source_target_pairs={{0,4},{4,12},{8,0},{12,20},{16,8},{20,28},{24,16},{28,24},{1,5},{5... | collective-permute-start | bytes 811016 | tf_op jit(solution)/shard_map/ppermute | solution.py:285
  99.6 2.5 %collective-permute-done.21.refs_5_ = bf16[32,4224]{1,0:T(8,128)(2,1)S(1)} collective-permute-done((bf16[32,4224]{1,0:T(8,128)(2,1)S(1)}, bf16[32,4224]{1,0:T(8,128)(2,1)S(1)}, u32[]{:S(2)}, u32[]{:S(2)}) %collective-permute-start.21) | collective-permute-done | bytes 270368 | tf_op jit(solution)/shard_map/ppermute | solution.py:285
  102.9 14.4 %shard_map.156.refs_9_ = f32[8,8,128]{2,1,0:T(8,128)S(1)} custom-call(s32[13]{0:T(128)S(1)} %concatenate.21.sc, bf16[32,4224]{1,0:T(8,128)(2,1)S(1)} %shard_map.155.refs_0_, bf16[32,4224]{1,0:T(8,128)(2,1)S(1)} %collective-permute-done.19.refs_1_, bf16[32,4224]{1,0:T(8,128)(2,1)S(1)} %collective-permute-done.24.refs_2_, ...), custom_call_target="tpu_custom_call" | custom-call | flops 8388608000 | bytes 32768000 | tf_op jit(solution)/shard_map/pallas_call | solution.py:473
  117.3 14.4 %shard_map.157 = (f32[4,8,128]{2,1,0:T(8,128)S(1)}, f32[4,8,128]{2,1,0:T(8,128)S(1)}) custom-call(s32[13]{0:T(128)S(1)} %concatenate.21.sc, bf16[32,4224]{1,0:T(8,128)(2,1)S(1)} %collective-permute-done.12.refs_0_, bf16[32,4224]{1,0:T(8,128)(2,1)S(1)} %collective-permute-done.13.refs_1_, bf16[32,4224]{1,0:T(8,128)(2,1)S(1)} %collective-permute-done.14.refs_2_, ...), custom_call_target="tpu_custom_call" | custom-call | flops 8388608000 | bytes 32768000 | tf_op jit(solution)/shard_map/pallas_call | solution.py:473
  131.7 3.2 %collective-permute-start.27 = (f32[4,8,128]{2,1,0:T(8,128)S(1)}, f32[4,8,128]{2,1,0:T(8,128)S(1)}, u32[]{:S(2)}, u32[]{:S(2)}) collective-permute-start(f32[4,8,128]{2,1,0:T(8,128)S(1)} %get-tuple-element.33), channel_id=1, source_target_pairs={{0,16},{4,20},{8,24},{12,28},{16,0},{20,4},{24,8},{28,12},{1,17},{... | collective-permute-start | bytes 49160 | tf_op jit(solution)/shard_map/ppermute | solution.py:285
  134.9 1.7 %collective-permute-done.27.other = f32[4,8,128]{2,1,0:T(8,128)S(1)} collective-permute-done((f32[4,8,128]{2,1,0:T(8,128)S(1)}, f32[4,8,128]{2,1,0:T(8,128)S(1)}, u32[]{:S(2)}, u32[]{:S(2)}) %collective-permute-start.27) | collective-permute-done | bytes 16416 | tf_op jit(solution)/shard_map/ppermute | solution.py:285
  136.6 2.1 %collective-permute-start.28 = (f32[2,8,128]{2,1,0:T(8,128)S(1)}, f32[2,8,128]{2,1,0:T(8,128)S(1)}, u32[]{:S(2)}, u32[]{:S(2)}) collective-permute-start(f32[2,8,128]{2,1,0:T(8,128)S(1)} %get-tuple-element.35), channel_id=1, source_target_pairs={{0,8},{4,12},{8,0},{12,4},{16,24},{20,28},{24,16},{28,20},{1,9},{5... | collective-permute-start | bytes 24584 | tf_op jit(solution)/shard_map/ppermute | solution.py:285
  138.7 1.6 %collective-permute-done.28.other = f32[2,8,128]{2,1,0:T(8,128)S(1)} collective-permute-done((f32[2,8,128]{2,1,0:T(8,128)S(1)}, f32[2,8,128]{2,1,0:T(8,128)S(1)}, u32[]{:S(2)}, u32[]{:S(2)}) %collective-permute-start.28) | collective-permute-done | bytes 8224 | tf_op jit(solution)/shard_map/ppermute | solution.py:285
  140.4 2.3 %collective-permute-start.29 = (f32[1,8,128]{2,1,0:T(8,128)S(1)}, f32[1,8,128]{2,1,0:T(8,128)S(1)}, u32[]{:S(2)}, u32[]{:S(2)}) collective-permute-start(f32[1,8,128]{2,1,0:T(8,128)S(1)} %get-tuple-element.37), channel_id=1, source_target_pairs={{0,4},{4,0},{8,12},{12,8},{16,20},{20,16},{24,28},{28,24},{1,5},{5... | collective-permute-start | bytes 12296 | tf_op jit(solution)/shard_map/ppermute | solution.py:285
  142.7 1.6 %collective-permute-done.29.other = f32[1,8,128]{2,1,0:T(8,128)S(1)} collective-permute-done((f32[1,8,128]{2,1,0:T(8,128)S(1)}, f32[1,8,128]{2,1,0:T(8,128)S(1)}, u32[]{:S(2)}, u32[]{:S(2)}) %collective-permute-start.29) | collective-permute-done | bytes 4128 | tf_op jit(solution)/shard_map/ppermute | solution.py:285
  (80 shorter events, 13.3 us)
Async XLA Ops:
  0.7 13.6 %copy-start.5 = (bf16[256,2,128]{2,1,0:T(2,128)(2,1)S(1)}, bf16[256,2,128]{2,1,0:T(2,128)(2,1)}, u32[]{:S(2)}) copy-start(bf16[256,2,128]{2,1,0:T(2,128)(2,1)} %param.16) | copy-start | bytes 393220
  0.7 13.6 %copy-start.4 = (bf16[256,2,128]{2,1,0:T(2,128)(2,1)S(1)}, bf16[256,2,128]{2,1,0:T(2,128)(2,1)}, u32[]{:S(2)}) copy-start(bf16[256,2,128]{2,1,0:T(2,128)(2,1)} %param.17) | copy-start | bytes 393220
  0.7 46.1 %collective-permute-start.10 = (bf16[512,4096]{1,0:T(8,128)(2,1)}, bf16[512,4096]{1,0:T(8,128)(2,1)}, u32[]{:S(2)}, u32[]{:S(2)}) collective-permute-start(bf16[512,4096]{1,0:T(8,128)(2,1)} %mine.1), channel_id=1, source_target_pairs={{0,1},{1,0},{2,3},{3,2},{4,5},{5,4},{6,7},{7,6},{8,9},{9,8},{10,11... | collective-permute-start | bytes 12582920 | tf_op jit(solution)/shard_map/ppermute | solution.py:285
  5.2 14.0 %collective-permute-start.4 = (bf16[1040,128]{1,0:T(8,128)(2,1)S(1)}, bf16[1040,128]{1,0:T(8,128)(2,1)S(1)}, u32[]{:S(2)}, u32[]{:S(2)}) collective-permute-start(bf16[1040,128]{1,0:T(8,128)(2,1)S(1)} %get-tuple-element.52.refs_1_), channel_id=1, source_target_pairs={{0,24},{4,28},{8,0},{12,4},{16,8},{20,12},{24,16},{28,20},{1,25},{... | collective-permute-start | bytes 798728 | tf_op jit(solution)/shard_map/ppermute | solution.py:285
  10.0 16.0 %collective-permute-start.6 = (bf16[1040,128]{1,0:T(8,128)(2,1)S(1)}, bf16[1040,128]{1,0:T(8,128)(2,1)S(1)}, u32[]{:S(2)}, u32[]{:S(2)}) collective-permute-start(bf16[1040,128]{1,0:T(8,128)(2,1)S(1)} %get-tuple-element.52.refs_1_), channel_id=1, source_target_pairs={{4,0},{12,8},{20,16},{28,24},{5,1},{13,9},{21,17},{29,25},{6,2},{1... | collective-permute-start | bytes 798728 | tf_op jit(solution)/shard_map/ppermute | solution.py:285
  11.3 14.7 %collective-permute-start.5 = (bf16[1040,128]{1,0:T(8,128)(2,1)S(1)}, bf16[1040,128]{1,0:T(8,128)(2,1)S(1)}, u32[]{:S(2)}, u32[]{:S(2)}) collective-permute-start(bf16[1040,128]{1,0:T(8,128)(2,1)S(1)} %get-tuple-element.53.refs_0_), channel_id=1, source_target_pairs={{4,0},{12,8},{20,16},{28,24},{5,1},{13,9},{21,17},{29,25},{6,2},{1... | collective-permute-start | bytes 798728 | tf_op jit(solution)/shard_map/ppermute | solution.py:285
  12.6 2.7 %collective-permute-start = (bf16[256,512]{1,0:T(8,128)(2,1)S(1)}, bf16[256,512]{1,0:T(8,128)(2,1)S(1)}, u32[]{:S(2)}, u32[]{:S(2)}) collective-permute-start(bf16[256,512]{1,0:T(8,128)(2,1)S(1)} %copy-done.3), channel_id=1, source_target_pairs={{0,1},{1,0},{2,3},{3,2},{4,5},{5,4},{6,7},{7,6},{8,9},{9,8},{10,11... | collective-permute-start | bytes 786440 | tf_op jit(solution)/shard_map/ppermute | solution.py:285
  15.3 10.6 %collective-permute-start.1 = (bf16[1040,128]{1,0:T(8,128)(2,1)S(1)}, bf16[1040,128]{1,0:T(8,128)(2,1)S(1)}, u32[]{:S(2)}, u32[]{:S(2)}) collective-permute-start(bf16[1040,128]{1,0:T(8,128)(2,1)S(1)} %get-tuple-element.53.refs_0_), channel_id=1, source_target_pairs={{0,24},{4,28},{8,0},{12,4},{16,8},{20,12},{24,16},{28,20},{1,25},{... | collective-permute-start | bytes 798728 | tf_op jit(solution)/shard_map/ppermute | solution.py:285
  26.0 9.3 %collective-permute-start.7 = (bf16[1040,128]{1,0:T(8,128)(2,1)S(1)}, bf16[1040,128]{1,0:T(8,128)(2,1)S(1)}, u32[]{:S(2)}, u32[]{:S(2)}) collective-permute-start(bf16[1040,128]{1,0:T(8,128)(2,1)S(1)} %collective-permute-done.4.refs_3_), channel_id=1, source_target_pairs={{0,4},{4,0},{8,12},{12,8},{16,20},{20,16},{24,28},{28,24},{1,5},{5... | collective-permute-start | bytes 798728 | tf_op jit(solution)/shard_map/ppermute | solution.py:285
  26.8 12.4 %collective-permute-start.2 = (bf16[1040,128]{1,0:T(8,128)(2,1)S(1)}, bf16[1040,128]{1,0:T(8,128)(2,1)S(1)}, u32[]{:S(2)}, u32[]{:S(2)}) collective-permute-start(bf16[1040,128]{1,0:T(8,128)(2,1)S(1)} %collective-permute-done.1.refs_2_), channel_id=1, source_target_pairs={{0,4},{4,0},{8,12},{12,8},{16,20},{20,16},{24,28},{28,24},{1,5},{5... | collective-permute-start | bytes 798728 | tf_op jit(solution)/shard_map/ppermute | solution.py:285
  35.3 8.5 %collective-permute-start.8 = (bf16[1040,128]{1,0:T(8,128)(2,1)S(1)}, bf16[1040,128]{1,0:T(8,128)(2,1)S(1)}, u32[]{:S(2)}, u32[]{:S(2)}) collective-permute-start(bf16[1040,128]{1,0:T(8,128)(2,1)S(1)} %collective-permute-done.7.refs_1_), channel_id=1, source_target_pairs={{4,28},{12,4},{20,12},{28,20},{5,29},{13,5},{21,13},{29,21},{6,30}... | collective-permute-start | bytes 798728 | tf_op jit(solution)/shard_map/ppermute | solution.py:285
  39.2 4.7 %collective-permute-start.3 = (bf16[1040,128]{1,0:T(8,128)(2,1)S(1)}, bf16[1040,128]{1,0:T(8,128)(2,1)S(1)}, u32[]{:S(2)}, u32[]{:S(2)}) collective-permute-start(bf16[1040,128]{1,0:T(8,128)(2,1)S(1)} %collective-permute-done.2.refs_0_), channel_id=1, source_target_pairs={{4,28},{12,4},{20,12},{28,20},{5,29},{13,5},{21,13},{29,21},{6,30}... | collective-permute-start | bytes 798728 | tf_op jit(solution)/shard_map/ppermute | solution.py:285
  44.8 2.0 %collective-permute-start.9 = (f32[8,136,128]{2,1,0:T(8,128)S(1)}, f32[8,136,128]{2,1,0:T(8,128)S(1)}, u32[]{:S(2)}, u32[]{:S(2)}) collective-permute-start(f32[8,136,128]{2,1,0:T(8,128)S(1)} %get-tuple-element.27), channel_id=1, source_target_pairs={{0,1},{1,0},{2,3},{3,2},{4,5},{5,4},{6,7},{7,6},{8,9},{9,8},{10,11... | collective-permute-start | bytes 1671176 | tf_op jit(solution)/shard_map/ppermute | solution.py:285
  50.3 9.2 %collective-permute-start.11 = (bf16[32,4096]{1,0:T(8,128)(2,1)S(1)}, bf16[32,4096]{1,0:T(8,128)(2,1)S(1)}, u32[]{:S(2)}, u32[]{:S(2)}) collective-permute-start(bf16[32,4096]{1,0:T(8,128)(2,1)S(1)} %get-tuple-element.29), channel_id=1, source_target_pairs={{0,2},{1,3},{2,0},{3,1},{4,6},{5,7},{6,4},{7,5},{8,10},{9,11},{10,... | collective-permute-start | bytes 786440 | tf_op jit(solution)/shard_map/ppermute | solution.py:285
  51.9 16.2 %collective-permute-start.18 = (bf16[32,4096]{1,0:T(8,128)(2,1)S(1)}, bf16[32,4096]{1,0:T(8,128)(2,1)S(1)}, u32[]{:S(2)}, u32[]{:S(2)}) collective-permute-start(bf16[32,4096]{1,0:T(8,128)(2,1)S(1)} %get-tuple-element.30), channel_id=1, source_target_pairs={{0,2},{1,3},{2,0},{3,1},{4,6},{5,7},{6,4},{7,5},{8,10},{9,11},{10,... | collective-permute-start | bytes 786440 | tf_op jit(solution)/shard_map/ppermute | solution.py:285
  59.8 13.4 %collective-permute-start.12 = (bf16[32,4224]{1,0:T(8,128)(2,1)S(1)}, bf16[32,4224]{1,0:T(8,128)(2,1)S(1)}, u32[]{:S(2)}, u32[]{:S(2)}) collective-permute-start(bf16[32,4224]{1,0:T(8,128)(2,1)S(1)} %shard_map.154.refs_7_), channel_id=1, source_target_pairs={{0,8},{4,0},{8,16},{12,4},{16,24},{20,12},{24,28},{28,20},{1,9},{5... | collective-permute-start | bytes 811016 | tf_op jit(solution)/shard_map/ppermute | solution.py:285
  59.8 13.3 %collective-permute-start.13 = (bf16[32,4224]{1,0:T(8,128)(2,1)S(1)}, bf16[32,4224]{1,0:T(8,128)(2,1)S(1)}, u32[]{:S(2)}, u32[]{:S(2)}) collective-permute-start(bf16[32,4224]{1,0:T(8,128)(2,1)S(1)} %shard_map.154.refs_7_), channel_id=1, source_target_pairs={{0,4},{4,12},{8,0},{12,20},{16,8},{20,28},{24,16},{28,24},{1,5},{5... | collective-permute-start | bytes 811016 | tf_op jit(solution)/shard_map/ppermute | solution.py:285
  68.4 11.7 %collective-permute-start.19 = (bf16[32,4224]{1,0:T(8,128)(2,1)S(1)}, bf16[32,4224]{1,0:T(8,128)(2,1)S(1)}, u32[]{:S(2)}, u32[]{:S(2)}) collective-permute-start(bf16[32,4224]{1,0:T(8,128)(2,1)S(1)} %shard_map.155.refs_0_), channel_id=1, source_target_pairs={{0,8},{4,0},{8,16},{12,4},{16,24},{20,12},{24,28},{28,20},{1,9},{5... | collective-permute-start | bytes 811016 | tf_op jit(solution)/shard_map/ppermute | solution.py:285
  68.5 11.6 %collective-permute-start.24 = (bf16[32,4224]{1,0:T(8,128)(2,1)S(1)}, bf16[32,4224]{1,0:T(8,128)(2,1)S(1)}, u32[]{:S(2)}, u32[]{:S(2)}) collective-permute-start(bf16[32,4224]{1,0:T(8,128)(2,1)S(1)} %shard_map.155.refs_0_), channel_id=1, source_target_pairs={{0,4},{4,12},{8,0},{12,20},{16,8},{20,28},{24,16},{28,24},{1,5},{5... | collective-permute-start | bytes 811016 | tf_op jit(solution)/shard_map/ppermute | solution.py:285
  73.2 12.7 %collective-permute-start.14 = (bf16[32,4224]{1,0:T(8,128)(2,1)S(1)}, bf16[32,4224]{1,0:T(8,128)(2,1)S(1)}, u32[]{:S(2)}, u32[]{:S(2)}) collective-permute-start(bf16[32,4224]{1,0:T(8,128)(2,1)S(1)} %collective-permute-done.12.refs_0_), channel_id=1, source_target_pairs={{0,8},{4,0},{8,16},{12,4},{16,24},{20,12},{24,28},{28,20},{1,9},{5... | collective-permute-start | bytes 811016 | tf_op jit(solution)/shard_map/ppermute | solution.py:285
  73.2 12.7 %collective-permute-start.15 = (bf16[32,4224]{1,0:T(8,128)(2,1)S(1)}, bf16[32,4224]{1,0:T(8,128)(2,1)S(1)}, u32[]{:S(2)}, u32[]{:S(2)}) collective-permute-start(bf16[32,4224]{1,0:T(8,128)(2,1)S(1)} %collective-permute-done.13.refs_1_), channel_id=1, source_target_pairs={{0,4},{4,12},{8,0},{12,20},{16,8},{20,28},{24,16},{28,24},{1,5},{5... | collective-permute-start | bytes 811016 | tf_op jit(solution)/shard_map/ppermute | solution.py:285
  80.1 11.6 %collective-permute-start.20 = (bf16[32,4224]{1,0:T(8,128)(2,1)S(1)}, bf16[32,4224]{1,0:T(8,128)(2,1)S(1)}, u32[]{:S(2)}, u32[]{:S(2)}) collective-permute-start(bf16[32,4224]{1,0:T(8,128)(2,1)S(1)} %collective-permute-done.19.refs_1_), channel_id=1, source_target_pairs={{0,8},{4,0},{8,16},{12,4},{16,24},{20,12},{24,28},{28,20},{1,9},{5... | collective-permute-start | bytes 811016 | tf_op jit(solution)/shard_map/ppermute | solution.py:285
  80.1 11.6 %collective-permute-start.25 = (bf16[32,4224]{1,0:T(8,128)(2,1)S(1)}, bf16[32,4224]{1,0:T(8,128)(2,1)S(1)}, u32[]{:S(2)}, u32[]{:S(2)}) collective-permute-start(bf16[32,4224]{1,0:T(8,128)(2,1)S(1)} %collective-permute-done.24.refs_2_), channel_id=1, source_target_pairs={{0,4},{4,12},{8,0},{12,20},{16,8},{20,28},{24,16},{28,24},{1,5},{5... | collective-permute-start | bytes 811016 | tf_op jit(solution)/shard_map/ppermute | solution.py:285
  85.9 11.6 %collective-permute-start.16 = (bf16[32,4224]{1,0:T(8,128)(2,1)S(1)}, bf16[32,4224]{1,0:T(8,128)(2,1)S(1)}, u32[]{:S(2)}, u32[]{:S(2)}) collective-permute-start(bf16[32,4224]{1,0:T(8,128)(2,1)S(1)} %collective-permute-done.14.refs_2_), channel_id=1, source_target_pairs={{0,8},{4,0},{8,16},{12,4},{16,24},{20,12},{24,28},{28,20},{1,9},{5... | collective-permute-start | bytes 811016 | tf_op jit(solution)/shard_map/ppermute | solution.py:285
  85.9 11.6 %collective-permute-start.17 = (bf16[32,4224]{1,0:T(8,128)(2,1)S(1)}, bf16[32,4224]{1,0:T(8,128)(2,1)S(1)}, u32[]{:S(2)}, u32[]{:S(2)}) collective-permute-start(bf16[32,4224]{1,0:T(8,128)(2,1)S(1)} %collective-permute-done.15.refs_3_), channel_id=1, source_target_pairs={{0,4},{4,12},{8,0},{12,20},{16,8},{20,28},{24,16},{28,24},{1,5},{5... | collective-permute-start | bytes 811016 | tf_op jit(solution)/shard_map/ppermute | solution.py:285
  91.7 10.4 %collective-permute-start.21 = (bf16[32,4224]{1,0:T(8,128)(2,1)S(1)}, bf16[32,4224]{1,0:T(8,128)(2,1)S(1)}, u32[]{:S(2)}, u32[]{:S(2)}) collective-permute-start(bf16[32,4224]{1,0:T(8,128)(2,1)S(1)} %collective-permute-done.20.refs_3_), channel_id=1, source_target_pairs={{0,8},{4,0},{8,16},{12,4},{16,24},{20,12},{24,28},{28,20},{1,9},{5... | collective-permute-start | bytes 811016 | tf_op jit(solution)/shard_map/ppermute | solution.py:285
  91.7 11.2 %collective-permute-start.26 = (bf16[32,4224]{1,0:T(8,128)(2,1)S(1)}, bf16[32,4224]{1,0:T(8,128)(2,1)S(1)}, u32[]{:S(2)}, u32[]{:S(2)}) collective-permute-start(bf16[32,4224]{1,0:T(8,128)(2,1)S(1)} %collective-permute-done.25.refs_4_), channel_id=1, source_target_pairs={{0,4},{4,12},{8,0},{12,20},{16,8},{20,28},{24,16},{28,24},{1,5},{5... | collective-permute-start | bytes 811016 | tf_op jit(solution)/shard_map/ppermute | solution.py:285
  97.5 19.8 %collective-permute-start.23 = (bf16[32,4224]{1,0:T(8,128)(2,1)S(1)}, bf16[32,4224]{1,0:T(8,128)(2,1)S(1)}, u32[]{:S(2)}, u32[]{:S(2)}) collective-permute-start(bf16[32,4224]{1,0:T(8,128)(2,1)S(1)} %collective-permute-done.17.refs_5_), channel_id=1, source_target_pairs={{0,4},{4,12},{8,0},{12,20},{16,8},{20,28},{24,16},{28,24},{1,5},{5... | collective-permute-start | bytes 811016 | tf_op jit(solution)/shard_map/ppermute | solution.py:285
  102.0 15.2 %collective-permute-start.22 = (bf16[32,4224]{1,0:T(8,128)(2,1)S(1)}, bf16[32,4224]{1,0:T(8,128)(2,1)S(1)}, u32[]{:S(2)}, u32[]{:S(2)}) collective-permute-start(bf16[32,4224]{1,0:T(8,128)(2,1)S(1)} %collective-permute-done.21.refs_5_), channel_id=1, source_target_pairs={{0,8},{4,0},{8,16},{12,4},{16,24},{20,12},{24,28},{28,20},{1,9},{5... | collective-permute-start | bytes 811016 | tf_op jit(solution)/shard_map/ppermute | solution.py:285
  131.7 5.0 %collective-permute-start.27 = (f32[4,8,128]{2,1,0:T(8,128)S(1)}, f32[4,8,128]{2,1,0:T(8,128)S(1)}, u32[]{:S(2)}, u32[]{:S(2)}) collective-permute-start(f32[4,8,128]{2,1,0:T(8,128)S(1)} %get-tuple-element.33), channel_id=1, source_target_pairs={{0,16},{4,20},{8,24},{12,28},{16,0},{20,4},{24,8},{28,12},{1,17},{... | collective-permute-start | bytes 49160 | tf_op jit(solution)/shard_map/ppermute | solution.py:285
  136.6 3.7 %collective-permute-start.28 = (f32[2,8,128]{2,1,0:T(8,128)S(1)}, f32[2,8,128]{2,1,0:T(8,128)S(1)}, u32[]{:S(2)}, u32[]{:S(2)}) collective-permute-start(f32[2,8,128]{2,1,0:T(8,128)S(1)} %get-tuple-element.35), channel_id=1, source_target_pairs={{0,8},{4,12},{8,0},{12,4},{16,24},{20,28},{24,16},{28,20},{1,9},{5... | collective-permute-start | bytes 24584 | tf_op jit(solution)/shard_map/ppermute | solution.py:285
  140.4 3.9 %collective-permute-start.29 = (f32[1,8,128]{2,1,0:T(8,128)S(1)}, f32[1,8,128]{2,1,0:T(8,128)S(1)}, u32[]{:S(2)}, u32[]{:S(2)}) collective-permute-start(f32[1,8,128]{2,1,0:T(8,128)S(1)} %get-tuple-element.37), channel_id=1, source_target_pairs={{0,4},{4,0},{8,12},{12,8},{16,20},{20,16},{24,28},{28,24},{1,5},{5... | collective-permute-start | bytes 12296 | tf_op jit(solution)/shard_map/ppermute | solution.py:285
  (6 other events, 59.0 us)
